TPU v7x, 256 devices: a whole 4x4x8 slice. The times are simulated.
256 devices in a mesh: orb: 32 (over y, z), row: 8 (over x, core).
Axes of the slice: x: 4, y: 4, z: 8, core: 2. Of those that a mesh axis runs over, the one named last changes fastest.
Arguments:
- orbital_fragments: bfloat16 [1572864, 128], P(('orb', 'row')), may hold values from -6 to 6
- receiving_devices: int32 [1572864, 1], P(('orb', 'row')), may hold values from 0 to 255; in each aligned block of 6144 rows (0 to 6143, 6144 to 12287, ...) at most 48 rows name the same one
- fragment_grid_tile: int32 [1572864], P(('orb', 'row')), may hold values from 0 to 767
- outside_field_grid: float32 [196608, 128], P(('orb', 'row')), may hold values from -6 to 6
- density_matrix_tiles: bfloat16 [512, 12, 128, 128], P(('orb', 'row')), may hold values from -2 to 2
- energy_operator_tiles: bfloat16 [512, 12, 128, 128], P(('orb', 'row')), may hold values from -0.796875 to 0.796875
- tile_column_numbers: int32 [512, 12], P('orb'), may hold values from 0 to 511, as said below
Outputs:
- applied: bfloat16 [1572864, 128], P(('orb', 'row'))
- charge_distribution: float32 [196608, 128], P(('orb', 'row'))
- product: bfloat16 [512, 12, 128, 128], P(('orb', 'row'))
Inputs may be any that keep to these rules, and one draw needn't show every extreme that they name: `receiving_devices`: among the 6144 segments of one device at most 48 have the same target, and some target has exactly 48. `tile_column_numbers`: block row i names 12 distinct block columns j with j // 16 == i // 16; its first is i itself.
All inputs are finite; a program needn't handle non-finite values.
Results may differ from a plain program's by a relative error of at most 0.0044.
Values may be sent and summed in bfloat16 or wider, within the bound.
No kernel may reach another device: no remote copies, remote signals or barrier semaphores. Data moves between devices by JAX's collectives and lax.ppermute only.
A program may use at most 64 MiB of HBM per device.

v0:
```python
import math

import jax
import jax.numpy as jnp
from jax import lax
from jax.sharding import PartitionSpec as P

BLK = 128
SEGF = 24


def slot_ranks(dest, devices):
    seg_dev = dest.shape[0]
    block_len = math.gcd(seg_dev, 128)
    block_count = seg_dev // block_len
    dest_blocks = dest.reshape(block_count, block_len)
    owners = jnp.arange(devices, dtype=jnp.int32)
    hits = dest_blocks[:, :, None] == owners[None, None, :]
    counts = jnp.sum(hits.astype(jnp.int32), axis=1)
    before = jnp.cumsum(counts, axis=0) - counts
    carried = jnp.sum(jnp.where(hits, before[:, None, :], 0), axis=2)
    positions = jnp.arange(block_len, dtype=jnp.int32)
    earlier_mask = positions[:, None] > positions[None, :]
    same_owner = dest_blocks[:, :, None] == dest_blocks[:, None, :]
    within = jnp.sum((same_owner & earlier_mask[None, :, :]).astype(jnp.int32), axis=2)
    return (carried + within).reshape(-1)


def body(
    orbital_fragments,
    receiving_devices,
    fragment_grid_tile,
    outside_field_grid,
    density_matrix_tiles,
    energy_operator_tiles,
    tile_column_numbers,
):
    seg_dev, seg_len = orbital_fragments.shape
    n_orb = lax.axis_size("orb")
    n_row = lax.axis_size("row")
    devices = n_orb * n_row
    capacity = 2 * seg_dev // devices
    tile_roster = outside_field_grid.shape[0]
    dest = receiving_devices[:, 0]
    rank = slot_ranks(dest, devices)
    slots = dest * capacity + rank
    outgoing = (
        jnp.zeros((devices * capacity, seg_len), jnp.bfloat16).at[slots].set(orbital_fragments)
    )
    labels = (
        jnp.full((devices * capacity,), tile_roster, jnp.int32).at[slots].set(fragment_grid_tile)
    )
    outgoing = outgoing.reshape(n_orb, n_row, capacity, seg_len)
    labels = labels.reshape(n_orb, n_row, capacity)
    arrived, where = (
        lax.all_to_all(
            lax.all_to_all(outgoing, "orb", split_axis=0, concat_axis=0, tiled=True),
            "row",
            split_axis=1,
            concat_axis=1,
            tiled=True,
        ),
        lax.all_to_all(
            lax.all_to_all(labels, "orb", split_axis=0, concat_axis=0, tiled=True),
            "row",
            split_axis=1,
            concat_axis=1,
            tiled=True,
        ),
    )
    flat_where = where.reshape(-1)
    values = arrived.reshape(-1, seg_len).astype(jnp.float32)
    charge_distribution = (
        jnp.zeros((tile_roster + 1, seg_len), jnp.float32)
        .at[flat_where]
        .add(values * values)[:tile_roster]
    )
    effective_field_values = outside_field_grid - 1.5 * jnp.cbrt(1.0 + charge_distribution)
    padded = jnp.concatenate([effective_field_values, jnp.zeros((1, seg_len), jnp.float32)], axis=0)
    results = (
        (padded[flat_where] * values).astype(jnp.bfloat16).reshape(n_orb, n_row, capacity, seg_len)
    )
    returned = lax.all_to_all(
        lax.all_to_all(results, "orb", split_axis=0, concat_axis=0, tiled=True),
        "row",
        split_axis=1,
        concat_axis=1,
        tiled=True,
    )
    applied = returned.reshape(-1, seg_len)[slots]
    weighted = (orbital_fragments.astype(jnp.float32) * applied.astype(jnp.float32)).reshape(
        -1, SEGF * seg_len
    )
    shift = (jnp.sum(weighted, axis=1) / (SEGF * seg_len)).astype(jnp.bfloat16)
    shift_rows = shift.reshape(-1, BLK)
    group_h, group_shift = (
        lax.all_gather(energy_operator_tiles, "row", axis=0, tiled=True),
        lax.all_gather(shift_rows, "row", axis=0, tiled=True),
    )
    own_rows = density_matrix_tiles.shape[0]
    group = own_rows * n_row
    own_pattern = lax.dynamic_slice_in_dim(
        tile_column_numbers, lax.axis_index("row") * own_rows, own_rows, 0
    )

    def one_row(inputs):
        kernel_row, columns = inputs
        local = columns % group
        rows_h = group_h[local]
        row_sparsity_pattern = tile_column_numbers[local]
        match = (row_sparsity_pattern[:, :, None] == columns[None, None, :]).astype(jnp.bfloat16)
        selected = jnp.einsum(
            "efg,efab->egab", match, rows_h, preferred_element_type=jnp.float32
        ).astype(jnp.bfloat16)
        main = jnp.einsum("eab,egbc->gac", kernel_row, selected, preferred_element_type=jnp.float32)
        diag = kernel_row.astype(jnp.float32) * group_shift[local].astype(jnp.float32)[:, None, :]
        return (main + diag).astype(jnp.bfloat16)

    product = lax.map(one_row, (density_matrix_tiles, own_pattern))
    return (applied, charge_distribution, product)


def solution(mesh):
    return jax.shard_map(
        body,
        mesh=mesh,
        in_specs=(
            P(("orb", "row"), None),
            P(("orb", "row"), None),
            P(("orb", "row")),
            P(("orb", "row"), None),
            P(("orb", "row"), None, None, None),
            P(("orb", "row"), None, None, None),
            P("orb", None),
        ),
        out_specs=(
            P(("orb", "row"), None),
            P(("orb", "row"), None),
            P(("orb", "row"), None, None, None),
        ),
        check_vma=False,
    )
```

profile of v0, /device:TPU:1, one launch (start us, length us, event | category | flops | bytes accessed | tf_op | source)
XLA Modules:
  0.0 549.6 jit_solution(7097711950273191063)
XLA Ops:
  7.2 2.3 convert_reduce_fusion
  9.6 3.0 select_reduce_fusion
  12.6 3.2 convert_reduce_fusion.1
  15.8 0.8 compare_select_fusion.4
  16.6 23.2 %scatter_custom_fusion = s32[12288]{0:T(1024)S(1)} fusion(s32[6144]{0:T(1024)S(1)} %bitcast.74, s32[6144]{0:T(1024)} %param.11, s32[]{:T(128)} %constant.67.clone.1), kind=kCustom, calls=%fused_computation.51 | custom fusion | bytes 49664 | tf_op jit(solution)/shard_map/scatter | solution.py:51
  40.1 20.6 %all_to_all.30 = s32[32,1,384]{2,1,0:T(1,128)S(1)} all-to-all(s32[32,1,384]{2,1,0:T(1,128)S(1)} %reshape.244), channel_id=1, replica_groups=mesh['orb'=32,'row'=8] {'orb'}, dimensions={0} | all-to-all | bytes 98304 | tf_op jit(solution)/shard_map/all_to_all | solution.py:64
  60.7 0.5 broadcast.138
  61.2 0.8 reduce.2
  62.1 0.8 reshape.246
  62.9 6.4 %all-to-all-start.1 = ((s32[8,1,1536]{2,1,0:T(1,128)}), s32[8,1,1536]{2,1,0:T(1,128)S(1)}, u32[]{:S(2)}, u32[]{:S(2)}) async-start(s32[8,1,1536]{2,1,0:T(1,128)} %reshape.246), calls=%async_computation.1 | async-start | bytes 98304 | tf_op jit(solution)/shard_map/all_to_all | solution.py:63
  69.3 18.4 %scatter_custom_fusion.1 = bf16[12288,128]{1,0:T(8,128)(2,1)} fusion(s32[6144]{0:T(1024)S(1)} %bitcast.75, bf16[6144,128]{1,0:T(8,128)(2,1)} %param.9, bf16[]{:T(256)} %constant.72.clone.1), kind=kCustom, calls=%fused_computation.42 | custom fusion | bytes 3146240 | tf_op jit(solution)/shard_map/scatter | solution.py:48
  87.7 4.1 all-to-all-start.2
  91.8 0.7 all-gather.3.cloned.1.call-update
  92.5 0.8 reduce.3
  93.6 70.6 %all-to-all-done.2 = bf16[32,8,48,128]{3,2,1,0:T(8,128)(2,1)S(1)} async-done(((bf16[32,8,48,128]{3,2,1,0:T(8,128)(2,1)}), bf16[32,8,48,128]{3,2,1,0:T(8,128)(2,1)S(1)}, u32[]{:S(2)}, u32[]{:S(2)}) %all-to-all-start.2) | async-done | bytes 3145760 | tf_op jit(solution)/shard_map/all_to_all | solution.py:57
  164.2 2.3 copy.44
  166.5 7.5 %all-to-all-start.3 = ((bf16[32,8,48,128]{3,2,0,1:T(8,128)(2,1)}), bf16[32,8,48,128]{3,2,0,1:T(8,128)(2,1)S(1)}, u32[]{:S(2)}, u32[]{:S(2)}) async-start(bf16[32,8,48,128]{3,2,0,1:T(8,128)(2,1)} %copy.44), calls=%async_computation.3 | async-start | bytes 6291456 | tf_op jit(solution)/shard_map/all_to_all | solution.py:56
  174.1 0.6 copy-done.1
  174.7 0.6 broadcast_clamp_fusion
  175.3 36.1 %all-to-all-done.3 = bf16[32,8,48,128]{3,2,0,1:T(8,128)(2,1)S(1)} async-done(((bf16[32,8,48,128]{3,2,0,1:T(8,128)(2,1)}), bf16[32,8,48,128]{3,2,0,1:T(8,128)(2,1)S(1)}, u32[]{:S(2)}, u32[]{:S(2)}) %all-to-all-start.3) | async-done | bytes 3145760 | tf_op jit(solution)/shard_map/all_to_all | solution.py:56
  211.5 0.6 convert_multiply_fusion.1
  212.0 3.5 copy.45
  215.5 73.7 %scatter_custom_fusion.2 = f32[769,128]{1,0:T(8,128)S(1)} fusion(s32[12288]{0:T(1024)} %bitcast.73, f32[12288,128]{1,0:T(8,128)} %bitcast.66, f32[]{:T(128)} %constant.66.clone.1), kind=kCustom, calls=%fused_computation.46 | custom fusion | flops 1572864 | bytes 394240 | tf_op jit(solution)/shard_map/scatter-add | solution.py:76
  289.3 2.0 multiply_subtract_fusion
  291.3 45.0 %gather_fusion.3 = f32[12288,128]{1,0:T(8,128)} fusion(f32[769,128]{1,0:T(8,128)S(1)} %concatenate.3, s32[12288]{0:T(1024)} %broadcast_clamp_fusion), kind=kCustom, calls=%fused_computation.3 | custom fusion | bytes 12632064 | tf_op jit(solution)/shard_map/gather | solution.py:81
  336.3 3.4 fusion.32
  339.7 0.9 copy.47
  340.6 74.2 %all_to_all.31 = bf16[32,8,48,128]{3,2,1,0:T(8,128)(2,1)S(1)} all-to-all(bf16[32,8,48,128]{3,2,1,0:T(8,128)(2,1)S(1)} %copy.47), channel_id=1, replica_groups=mesh['orb'=32,'row'=8] {'orb'}, dimensions={0} | all-to-all | bytes 6291456 | tf_op jit(solution)/shard_map/all_to_all | solution.py:84
  414.8 2.2 copy.48
  417.0 9.1 %all-to-all-start.5 = ((bf16[32,8,48,128]{3,2,0,1:T(8,128)(2,1)}), bf16[32,8,48,128]{3,2,0,1:T(8,128)(2,1)}, u32[]{:S(2)}, u32[]{:S(2)}) async-start(bf16[32,8,48,128]{3,2,0,1:T(8,128)(2,1)} %copy.48), calls=%async_computation.5 | async-start | bytes 6291456 | tf_op jit(solution)/shard_map/all_to_all | solution.py:83
  426.2 37.5 %all-to-all-done.5 = bf16[32,8,48,128]{3,2,0,1:T(8,128)(2,1)} async-done(((bf16[32,8,48,128]{3,2,0,1:T(8,128)(2,1)}), bf16[32,8,48,128]{3,2,0,1:T(8,128)(2,1)}, u32[]{:S(2)}, u32[]{:S(2)}) %all-to-all-start.5) | async-done | bytes 3145760 | tf_op jit(solution)/shard_map/all_to_all | solution.py:83
  463.7 2.8 copy.49
  466.5 22.3 %gather_fusion.4 = bf16[6144,128]{1,0:T(8,128)(2,1)} fusion(bf16[12288,128]{1,0:T(8,128)(2,1)S(1)} %bitcast.63, s32[6144]{0:T(1024)S(1)} %broadcast_clamp_fusion.1), kind=kCustom, calls=%fused_computation.4 | custom fusion | bytes 3170304 | tf_op jit(solution)/shard_map/gather | solution.py:90
  488.8 2.8 multiply_reduce_fusion
  491.8 9.7 %all-gather = bf16[8,2,128]{2,1,0:T(2,128)(2,1)S(1)} all-gather(bf16[1,2,128]{2,1,0:T(2,128)(2,1)S(1)} %fusion.39), channel_id=1, replica_groups=mesh['orb'=32,'row'=8] {'row'}, dimensions={0}, use_global_device_ids=true | all-gather | bytes 4608 | tf_op jit(solution)/shard_map/all_gather | solution.py:98
  501.5 41.3 %while.12 = (s32[]{:T(128)}, bf16[2,12,128,128]{3,2,1,0:T(8,128)(2,1)}, s32[2,12]{1,0:T(2,128)S(1)}, s32[16,12]{1,0:T(8,128)S(1)}, bf16[16,12,128,128]{3,2,1,0:T...) while((s32[]{:T(128)}, ...), condition=%wide.region_10.11_spmd, body=%wide.region_9.10_spmd.sunk | while | flops 663753088 | bytes 35813664 | solution.py:119
  501.6 6.2 %gather_fusion = bf16[12,12,128,128]{3,2,1,0:T(8,128)(2,1)} fusion(bf16[16,12,128,128]{3,2,1,0:T(8,128)(2,1)} %get-tuple-element.173, s32[1024]{0:T(1024)S(1)} %pad_clamp_fusion.2), kind=kCustom, calls=%fused_computation.1.clone.1 | custom fusion | bytes 9437232 | tf_op jit(solution)/shard_map/while/body/eval_jaxpr/gather | solution.py:109
  507.8 0.6 gather_fusion.1
  508.4 8.5 %fusion.54 = bf16[12,12,128,128]{3,1,2,0:T(8,128)(2,1)} fusion(bf16[12,12,128,128]{3,2,1,0:T(8,128)(2,1)} %gather_fusion, s32[12,12]{1,0:T(8,128)S(1)} %gather_fusion.1, s32[12]{0:T(128)S(1)} %fusion.53), kind=kOutput, calls=%fused_computation.12.clone.1 | convolution fusion | flops 58984128 | bytes 9437808 | tf_op jit(solution)/shard_map/while/body/eval_jaxpr/efg,efab->egab/dot_general | solution.py:112
  516.8 0.6 gather_fusion.2
  517.4 3.8 fusion.55
  521.3 0.9 copy-done.6
  522.2 6.2 %gather_fusion = bf16[12,12,128,128]{3,2,1,0:T(8,128)(2,1)} fusion(bf16[16,12,128,128]{3,2,1,0:T(8,128)(2,1)} %get-tuple-element.173, s32[1024]{0:T(1024)S(1)} %pad_clamp_fusion.2), kind=kCustom, calls=%fused_computation.1.clone.1 | custom fusion | bytes 9437232 | tf_op jit(solution)/shard_map/while/body/eval_jaxpr/gather | solution.py:109
  528.4 0.6 gather_fusion.1
  529.0 8.5 %fusion.54 = bf16[12,12,128,128]{3,1,2,0:T(8,128)(2,1)} fusion(bf16[12,12,128,128]{3,2,1,0:T(8,128)(2,1)} %gather_fusion, s32[12,12]{1,0:T(8,128)S(1)} %gather_fusion.1, s32[12]{0:T(128)S(1)} %fusion.53), kind=kOutput, calls=%fused_computation.12.clone.1 | convolution fusion | flops 58984128 | bytes 9437808 | tf_op jit(solution)/shard_map/while/body/eval_jaxpr/efg,efab->egab/dot_general | solution.py:112
  537.5 0.6 gather_fusion.2
  538.0 3.8 fusion.55
  541.9 0.9 copy-done.6
  (47 shorter events, 1.3 us)
Async XLA Ops:
  16.6 71.1 %copy-start.2 = (s32[6144,1]{0,1:T(1,128)}, s32[6144,1]{0,1:T(1,128)S(1)}, u32[]{:S(2)}) copy-start(s32[6144,1]{0,1:T(1,128)S(1)} %compare_select_fusion.4) | copy-start | bytes 73732
  62.9 24.8 %all-to-all-start.1 = ((s32[8,1,1536]{2,1,0:T(1,128)}), s32[8,1,1536]{2,1,0:T(1,128)S(1)}, u32[]{:S(2)}, u32[]{:S(2)}) async-start(s32[8,1,1536]{2,1,0:T(1,128)} %reshape.246), calls=%async_computation.1 | async-start | bytes 98304 | tf_op jit(solution)/shard_map/all_to_all | solution.py:63
  87.7 76.5 %all-to-all-start.2 = ((bf16[32,8,48,128]{3,2,1,0:T(8,128)(2,1)}), bf16[32,8,48,128]{3,2,1,0:T(8,128)(2,1)S(1)}, u32[]{:S(2)}, u32[]{:S(2)}) async-start(bf16[32,8,48,128]{3,2,1,0:T(8,128)(2,1)} %bitcast.14), calls=%async_computation.2 | async-start | bytes 6291456 | tf_op jit(solution)/shard_map/all_to_all | solution.py:57
  91.8 409.8 %all-gather.3.cloned.1.call-start = ((), (), s32[]{:S(2)}) async-start(), calls=%async_computation.6 | async-start | bytes 7077888 | tf_op jit(solution)/shard_map/all_gather | solution.py:97
  166.5 45.0 %all-to-all-start.3 = ((bf16[32,8,48,128]{3,2,0,1:T(8,128)(2,1)}), bf16[32,8,48,128]{3,2,0,1:T(8,128)(2,1)S(1)}, u32[]{:S(2)}, u32[]{:S(2)}) async-start(bf16[32,8,48,128]{3,2,0,1:T(8,128)(2,1)} %copy.44), calls=%async_computation.3 | async-start | bytes 6291456 | tf_op jit(solution)/shard_map/all_to_all | solution.py:56
  174.1 0.6 copy-start.1
  417.0 9.2 %copy-start = (s32[16,12]{1,0:T(8,128)S(1)}, s32[16,12]{1,0:T(8,128)}, u32[]{:S(2)}) copy-start(s32[16,12]{1,0:T(8,128)} %param.15) | copy-start | bytes 2308
  417.0 9.2 %copy-start.3 = (s32[6144,1]{0,1:T(1,128)S(1)}, s32[6144,1]{0,1:T(1,128)}, u32[]{:S(2)}) copy-start(s32[6144,1]{0,1:T(1,128)} %copy-done.2) | copy-start | bytes 73732
  417.0 46.7 %all-to-all-start.5 = ((bf16[32,8,48,128]{3,2,0,1:T(8,128)(2,1)}), bf16[32,8,48,128]{3,2,0,1:T(8,128)(2,1)}, u32[]{:S(2)}, u32[]{:S(2)}) async-start(bf16[32,8,48,128]{3,2,0,1:T(8,128)(2,1)} %copy.48), calls=%async_computation.5 | async-start | bytes 6291456 | tf_op jit(solution)/shard_map/all_to_all | solution.py:83
  508.3 9.1 %copy-start.4 = (bf16[2,12,128,128]{3,2,1,0:T(8,128)(2,1)S(1)}, bf16[2,12,128,128]{3,2,1,0:T(8,128)(2,1)}, u32[]{:S(2)}) copy-start(bf16[2,12,128,128]{3,2,1,0:T(8,128)(2,1)} %get-tuple-element.174) | copy-start | bytes 2359300 | tf_op jit(solution)/shard_map/while
  508.3 9.1 %copy-start.5 = (bf16[2,12,128,128]{3,2,1,0:T(8,128)(2,1)S(1)}, bf16[2,12,128,128]{3,2,1,0:T(8,128)(2,1)}, u32[]{:S(2)}) copy-start(bf16[2,12,128,128]{3,2,1,0:T(8,128)(2,1)} %get-tuple-element.162) | copy-start | bytes 2359300 | tf_op jit(solution)/shard_map/while
  521.3 0.9 copy-start.6
  529.0 9.1 %copy-start.4 = (bf16[2,12,128,128]{3,2,1,0:T(8,128)(2,1)S(1)}, bf16[2,12,128,128]{3,2,1,0:T(8,128)(2,1)}, u32[]{:S(2)}) copy-start(bf16[2,12,128,128]{3,2,1,0:T(8,128)(2,1)} %get-tuple-element.174) | copy-start | bytes 2359300 | tf_op jit(solution)/shard_map/while
  529.0 9.1 %copy-start.5 = (bf16[2,12,128,128]{3,2,1,0:T(8,128)(2,1)S(1)}, bf16[2,12,128,128]{3,2,1,0:T(8,128)(2,1)}, u32[]{:S(2)}) copy-start(bf16[2,12,128,128]{3,2,1,0:T(8,128)(2,1)} %get-tuple-element.162) | copy-start | bytes 2359300 | tf_op jit(solution)/shard_map/while
  541.9 0.9 copy-start.6
Sparse Core Ops, SparseCore 0:
  94.4 44.8 all-gather.2
where the time goes:
time: 552 us; the launch traced here: 550 us
  waiting for transfers between devices  145 us (26%)
  local copies, waits for them, and re-layouts  140 us (25%)
  blocking collectives  105 us (19%)
  other arithmetic  94.3 us (17%)
  starting transfers between devices  27.2 us (5%)
  matrix products  24.6 us (4%)
  between operations  14.3 us (3%)
    all_to_all x1, blocking collectives, body(): lax.all_to_all(results, 'orb', split_axis=0, concat_axis=0, tiled=True)  74.2 us
    scatter-add x1, other arithmetic, body(): charge_distribution = jnp.zeros((tile_roster + 1, seg_len), jnp.float32)....  73.7 us
    all_to_all x1, waiting for transfers between devices, body(): lax.all_to_all(outgoing, 'orb', split_axis=0, concat_axis=0, tiled=True)  70.6 us
    gather x1, local copies, waits for them, and re-layouts, body(): padded[flat_where] * values  45 us
    all_to_all x1, waiting for transfers between devices, body(): lax.all_to_all(lax.all_to_all(results, 'orb', split_axis=0, concat_axis=0...  37.5 us
    all_to_all x1, waiting for transfers between devices, body(): lax.all_to_all(lax.all_to_all(outgoing, 'orb', split_axis=0, concat_axis=...  36.1 us
    scatter x1, local copies, waits for them, and re-layouts, body(): jnp.full((devices * capacity,), tile_roster, jnp.int32).at[slots]  23.2 us
    gather x1, local copies, waits for them, and re-layouts, body(): applied = returned.reshape(-1, seg_len)[slots]  22.3 us
  transfers between devices with their start and end apart: 5, of which 3 were waited for; matrix products, arithmetic and copies ran while one was open for 33% of the time, Pallas kernels for 0%

commit v1 on v0

v1 whole, which is shorter than its diff:
```python
import functools

import jax
import jax.numpy as jnp
from jax import lax
from jax.experimental import pallas as pl
from jax.experimental.pallas import tpu as pltpu
from jax.sharding import PartitionSpec as P

BLK = 128
SEGF = 24
CAP = 48
LANES = 128
F32 = jnp.float32
BF16 = jnp.bfloat16
VMEM = pl.BlockSpec(memory_space=pltpu.VMEM)
SMEM = pl.BlockSpec(memory_space=pltpu.SMEM)


def params(mib):
    return pltpu.CompilerParams(vmem_limit_bytes=mib << 20)


def cost(us, nbytes):
    return pl.CostEstimate(
        flops=int(us * 1e9), bytes_accessed=int(nbytes), transcendentals=0
    )


def iota(shape, axis):
    return lax.broadcasted_iota(jnp.int32, shape, axis)


def rank_kernel(devices, dest_ref, tile_ref, slot_ref, label_ref, run, acc):
    blocks = dest_ref.shape[0]
    owner = iota((devices, LANES), 0)
    src, dst = iota((LANES, 2 * LANES), 0), iota((LANES, 2 * LANES), 1)
    tri = ((dst >= LANES) | (src < dst)).astype(F32).astype(BF16)
    place = iota((LANES, LANES), 0)
    run[...] = jnp.zeros_like(run)
    acc[...] = jnp.zeros_like(acc)

    def step(b, carry):
        d = dest_ref[pl.ds(b, 1), :]
        hit = owner == d
        hot = hit.astype(F32).astype(BF16)
        counts = jnp.dot(hot, tri, preferred_element_type=F32)
        before = counts[:, :LANES] + run[...]
        rank = jnp.sum(jnp.where(hit, before, 0.0), axis=0, keepdims=True)
        run[...] += counts[:, LANES:]
        rank = rank.astype(jnp.int32)
        slot_ref[pl.ds(b, 1), :] = d * CAP + rank
        label = tile_ref[pl.ds(b, 1), :] + 1
        high = (label >> 2).astype(F32)
        low = (label & 3).astype(F32)
        spread = jnp.where(place == rank, high, 0.0)
        spread = spread + jnp.where(place == rank + 64, low, 0.0)
        acc[...] += lax.dot_general(
            hot,
            spread.astype(BF16),
            (((1,), (1,)), ((), ())),
            preferred_element_type=F32,
        )
        return carry

    lax.fori_loop(0, blocks, step, 0, unroll=4)
    both = acc[...]
    label_ref[...] = (both * 4.0 + pltpu.roll(both, 64, 1)).astype(jnp.int32) - 1


def rank_and_labels(dest, tile, devices):
    blocks = dest.shape[0]
    return pl.pallas_call(
        functools.partial(rank_kernel, devices),
        out_shape=(
            jax.ShapeDtypeStruct((blocks, LANES), jnp.int32),
            jax.ShapeDtypeStruct((devices, LANES), jnp.int32),
        ),
        in_specs=[VMEM, VMEM],
        out_specs=(VMEM, VMEM),
        scratch_shapes=[
            pltpu.VMEM((devices, LANES), F32),
            pltpu.VMEM((devices, LANES), F32),
        ],
        compiler_params=params(4),
        cost_estimate=cost(5, 1 << 18),
        name="rank",
    )(dest, tile)


def pack_kernel(slot_ref, x_ref, out_ref, xf, of):
    rows = x_ref.shape[0]
    slots = out_ref.shape[0]

    def widen(i, c):
        at = pl.ds(pl.multiple_of(i * 256, 256), 256)
        xf[at, :] = x_ref[at, :].astype(F32)
        return c

    lax.fori_loop(0, rows // 256, widen, 0)

    def clear(i, c):
        of[pl.ds(pl.multiple_of(i * 512, 512), 512), :] = jnp.zeros((512, LANES), F32)
        return c

    lax.fori_loop(0, slots // 512, clear, 0)

    def move(i, c):
        b = i // 4
        first = (i % 4) * 32
        for j in range(32):
            s = slot_ref[b, first + j]
            of[pl.ds(s, 1), :] = xf[pl.ds(i * 32 + j, 1), :]
        return c

    lax.fori_loop(0, rows // 32, move, 0)

    def narrow(i, c):
        at = pl.ds(pl.multiple_of(i * 256, 256), 256)
        out_ref[at, :] = of[at, :].astype(BF16)
        return c

    lax.fori_loop(0, slots // 256, narrow, 0)


def pack(slot, x, slots):
    rows = x.shape[0]
    return pl.pallas_call(
        pack_kernel,
        out_shape=jax.ShapeDtypeStruct((slots, LANES), BF16),
        in_specs=[SMEM, VMEM],
        out_specs=VMEM,
        scratch_shapes=[pltpu.VMEM((rows, LANES), F32), pltpu.VMEM((slots, LANES), F32)],
        compiler_params=params(17),
        cost_estimate=cost(12, 5 << 20),
        name="pack",
    )(slot, x)


def owner_kernel(label_ref, v_ref, field_ref, out_ref, charge_ref, acc, pot):
    slots = v_ref.shape[0]
    tiles = field_ref.shape[0]
    acc[...] = jnp.zeros_like(acc)
    depth = 512
    cell = iota((tiles, LANES), 0)

    def add(k, c):
        hot = []
        for j in range(depth // LANES):
            lab = label_ref[pl.ds(k * (depth // LANES) + j, 1), :]
            hot.append((cell == lab).astype(F32).astype(BF16))
        v = v_ref[pl.ds(pl.multiple_of(k * depth, depth), depth), :].astype(F32)
        square = v * v
        high = square.astype(BF16)
        low = (square - high.astype(F32)).astype(BF16)
        acc[...] += jnp.dot(
            jnp.concatenate(hot, axis=1),
            jnp.concatenate([high, low], axis=1),
            preferred_element_type=F32,
        )
        return c

    lax.fori_loop(0, slots // depth, add, 0)
    charge = acc[:, :LANES] + acc[:, LANES:]
    charge_ref[...] = charge
    field = field_ref[...] - 1.5 * jnp.exp(jnp.log(1.0 + charge) * (1.0 / 3.0))
    high = field.astype(BF16)
    pot[:, :LANES] = high
    pot[:, LANES:] = (field - high.astype(F32)).astype(BF16)
    chunk = 512
    lane = iota((LANES, tiles), 1)

    def apply(k, c):
        hot = []
        for j in range(chunk // LANES):
            lab = label_ref[pl.ds(k * (chunk // LANES) + j, 1), :]
            col = jnp.transpose(jnp.broadcast_to(lab, (LANES, LANES)))
            wide = jnp.concatenate([col] * (tiles // LANES), axis=1)
            hot.append((lane == wide).astype(F32).astype(BF16))
        got = jnp.dot(jnp.concatenate(hot, axis=0), pot[...], preferred_element_type=F32)
        at = pl.ds(pl.multiple_of(k * chunk, chunk), chunk)
        here = got[:, :LANES] + got[:, LANES:]
        out_ref[at, :] = (here * v_ref[at, :].astype(F32)).astype(BF16)
        return c

    lax.fori_loop(0, slots // chunk, apply, 0)


def owner_step(label, values, field):
    slots = values.shape[0]
    tiles = field.shape[0]
    return pl.pallas_call(
        owner_kernel,
        out_shape=(
            jax.ShapeDtypeStruct((slots, LANES), BF16),
            jax.ShapeDtypeStruct((tiles, LANES), F32),
        ),
        in_specs=[VMEM, VMEM, VMEM],
        out_specs=(VMEM, VMEM),
        scratch_shapes=[
            pltpu.VMEM((tiles, 2 * LANES), F32),
            pltpu.VMEM((tiles, 2 * LANES), BF16),
        ],
        compiler_params=params(18),
        cost_estimate=cost(20, 7 << 20),
        name="owner",
    )(label, values, field)


def unpack_kernel(n_row, slot_ref, ret_ref, x_ref, out_ref, shift_ref, rf, of, part):
    rows = x_ref.shape[0]
    slots = ret_ref.shape[0]

    def widen(i, c):
        at = pl.ds(pl.multiple_of(i * 256, 256), 256)
        rf[at, :] = ret_ref[at, :].astype(F32)
        return c

    lax.fori_loop(0, slots // 256, widen, 0)

    def move(i, c):
        b = i // 4
        first = (i % 4) * 32
        for j in range(32):
            s = slot_ref[b, first + j]
            of[pl.ds(i * 32 + j, 1), :] = rf[pl.ds(s, 1), :]
        return c

    lax.fori_loop(0, rows // 32, move, 0)
    count = 8

    def finish(i, c):
        at = pl.ds(pl.multiple_of(i * count * SEGF, count * SEGF), count * SEGF)
        got = of[at, :]
        out_ref[at, :] = got.astype(BF16)
        work = (got * x_ref[at, :].astype(F32)).reshape(count, SEGF, LANES)
        part[pl.ds(pl.multiple_of(i * count, count), count), :] = jnp.sum(work, axis=1)
        return c

    lax.fori_loop(0, rows // (count * SEGF), finish, 0)
    functions = rows // SEGF
    total = lax.dot_general(
        jnp.ones((8, LANES), F32),
        part[...],
        (((1,), (1,)), ((), ())),
        precision=lax.Precision.HIGHEST,
        preferred_element_type=F32,
    )
    total = total * (1.0 / (SEGF * LANES))
    one = jnp.concatenate(
        [total[0:1, i * BLK : (i + 1) * BLK] for i in range(functions // BLK)]
        + [jnp.zeros((8 - functions // BLK, BLK), F32)],
        axis=0,
    )
    one = one.astype(BF16).astype(F32)
    for r in range(n_row):
        shift_ref[r] = one


def unpack(slot, ret, x, n_row):
    rows = x.shape[0]
    slots = ret.shape[0]
    return pl.pallas_call(
        functools.partial(unpack_kernel, n_row),
        out_shape=(
            jax.ShapeDtypeStruct((rows, LANES), BF16),
            jax.ShapeDtypeStruct((n_row, 8, LANES), F32),
        ),
        in_specs=[SMEM, VMEM, VMEM],
        out_specs=(VMEM, VMEM),
        scratch_shapes=[
            pltpu.VMEM((slots, LANES), F32),
            pltpu.VMEM((rows, LANES), F32),
            pltpu.VMEM((rows // SEGF, LANES), F32),
        ],
        compiler_params=params(19),
        cost_estimate=cost(12, 7 << 20),
        name="unpack",
    )(slot, ret, x)


def main_kernel(row_at, col_at, d_ref, *refs):
    bufs, (out_ref, sel, dcat) = refs[:-3], refs[-3:]
    rows, nnz = d_ref.shape[:2]
    width = nnz * BLK

    def one(i, carry):
        def clear(e, c):
            sel[pl.ds(pl.multiple_of(e * BLK, BLK), BLK), :] = jnp.zeros(
                (BLK, sel.shape[1]), BF16
            )
            return c

        lax.fori_loop(0, nnz, clear, 0)
        for e in range(nnz):
            dcat[:, e * BLK : (e + 1) * BLK] = d_ref[i, e]
        for b, buf in enumerate(bufs):
            for j in range(rows):
                e = row_at[i, b * rows + j]

                @pl.when(e < nnz)
                def _():
                    top = pl.multiple_of(e * BLK, BLK)

                    def put(f, c):
                        g = col_at[i, (b * rows + j) * nnz + f]
                        left = pl.multiple_of(g * BLK, BLK)
                        sel[pl.ds(top, BLK), pl.ds(left, BLK)] = buf[j, f]
                        return c

                    lax.fori_loop(0, nnz, put, 0)

        def mult(n, c):
            at = pl.ds(pl.multiple_of(n * 256, 256), 256)
            out_ref[i, :, at] = jnp.dot(dcat[...], sel[:, at], preferred_element_type=F32)
            return c

        lax.fori_loop(0, width // 256, mult, 0)
        return carry

    lax.fori_loop(0, rows, one, 0)


def main_product(row_at, col_at, d, bufs):
    rows, nnz = d.shape[:2]
    return pl.pallas_call(
        main_kernel,
        out_shape=jax.ShapeDtypeStruct((rows, BLK, nnz * BLK), F32),
        in_specs=[SMEM, SMEM, VMEM] + [VMEM] * len(bufs),
        out_specs=VMEM,
        scratch_shapes=[
            pltpu.VMEM((nnz * BLK, (nnz + 1) * BLK), BF16),
            pltpu.VMEM((BLK, nnz * BLK), BF16),
        ],
        compiler_params=params(18),
        cost_estimate=cost(10, 10 << 20),
        name="hamiltonian",
    )(row_at, col_at, d, *bufs)


def final_kernel(at_ref, main_ref, d_ref, shift_ref, out_ref):
    rows, nnz = d_ref.shape[:2]
    for i in range(rows):
        for g in range(nnz):
            s = shift_ref[pl.ds(at_ref[i, g], 1), :]
            out_ref[i, g] = (
                main_ref[i, :, g * BLK : (g + 1) * BLK] + d_ref[i, g].astype(F32) * s
            ).astype(BF16)


def final(at, main, d, shift):
    return pl.pallas_call(
        final_kernel,
        out_shape=jax.ShapeDtypeStruct(d.shape, BF16),
        in_specs=[SMEM, VMEM, VMEM, VMEM],
        out_specs=VMEM,
        compiler_params=params(6),
        cost_estimate=cost(2, 4 << 20),
        name="final",
    )(at, main, d, shift)


def gather_hamiltonian(tiles, n_row):
    chips = n_row // 2
    same = [tiles]
    for d in range(1, chips):
        perm = [(r, ((r // 2 + d) % chips) * 2 + r % 2) for r in range(n_row)]
        same.append(lax.ppermute(tiles, "row", perm))
    swap = [(r, r ^ 1) for r in range(n_row)]
    other = [lax.ppermute(t, "row", swap) for t in same]
    return same + other


def positions(pattern, own_rows, n_row):
    me = lax.axis_index("row")
    chips = n_row // 2
    chip, core = me // 2, me % 2
    back = jnp.arange(chips, dtype=jnp.int32)
    owner = (chip - back + chips) % chips * 2
    owner = jnp.concatenate([owner + core, owner + 1 - core])
    k = (owner[:, None] * own_rows + jnp.arange(own_rows, dtype=jnp.int32)).reshape(-1)
    own = lax.dynamic_slice_in_dim(pattern, me * own_rows, own_rows, 0)
    nnz = pattern.shape[1]
    local = own % (own_rows * n_row)
    index = jnp.arange(nnz, dtype=jnp.int32)
    row_at = jnp.min(
        jnp.where(local[:, None, :] == k[None, :, None], index, nnz), axis=2
    )
    rows = pattern[k]
    col_at = jnp.min(
        jnp.where(own[:, None, None, :] == rows[None, :, :, None], index, nnz), axis=3
    )
    shift_at = local // own_rows * 8 + local % own_rows
    return row_at, col_at.reshape(own_rows, -1), shift_at


def body(
    orbital_fragments,
    receiving_devices,
    fragment_grid_tile,
    outside_field_grid,
    density_matrix_tiles,
    energy_operator_tiles,
    tile_column_numbers,
):
    seg_dev = orbital_fragments.shape[0]
    n_orb = lax.axis_size("orb")
    n_row = lax.axis_size("row")
    devices = n_orb * n_row
    slots = devices * CAP
    axes = ("orb", "row")

    def exchange(x):
        return lax.all_to_all(x, axes, split_axis=0, concat_axis=0, tiled=True)

    dest = receiving_devices.reshape(seg_dev // LANES, LANES)
    tile = fragment_grid_tile.reshape(seg_dev // LANES, LANES)
    slot, labels = rank_and_labels(dest, tile, devices)
    labels = exchange(labels.reshape(devices, 1, LANES)).reshape(devices, LANES)
    where = labels[:, :CAP].reshape(slots // LANES, LANES)
    outgoing = pack(slot, orbital_fragments, slots)
    arrived = exchange(outgoing.reshape(devices, CAP, LANES)).reshape(slots, LANES)

    own_rows = density_matrix_tiles.shape[0]
    row_at, col_at, shift_at = positions(tile_column_numbers, own_rows, n_row)
    bufs = gather_hamiltonian(energy_operator_tiles, n_row)
    main = main_product(row_at, col_at, density_matrix_tiles, bufs)

    arrived, main = lax.optimization_barrier((arrived, main))
    results, charge = owner_step(where, arrived, outside_field_grid)
    returned = exchange(results.reshape(devices, CAP, LANES)).reshape(slots, LANES)
    applied, shift = unpack(slot, returned, orbital_fragments, n_row)
    shift = lax.all_to_all(shift, "row", split_axis=0, concat_axis=0, tiled=True)
    product = final(shift_at, main, density_matrix_tiles, shift.reshape(n_row * 8, LANES))
    return (applied, charge, product)


def solution(mesh):
    return jax.shard_map(
        body,
        mesh=mesh,
        in_specs=(
            P(("orb", "row"), None),
            P(("orb", "row"), None),
            P(("orb", "row")),
            P(("orb", "row"), None),
            P(("orb", "row"), None, None, None),
            P(("orb", "row"), None, None, None),
            P("orb", None),
        ),
        out_specs=(
            P(("orb", "row"), None),
            P(("orb", "row"), None),
            P(("orb", "row"), None, None, None),
        ),
        check_vma=False,
    )
```

time: 552 us -> 290 us (0.53)
  local copies, waits for them, and re-layouts: 140 us -> 10.2 us
  other arithmetic: 94.3 us -> 0.48 us
  waiting for transfers between devices: 145 us -> 59.1 us
  Pallas kernels: 0 us -> 78.3 us
  matrix products: 24.6 us -> 0 us
  between operations: 14.3 us -> 0.78 us
  starting transfers between devices: 27.2 us -> 38.9 us
    all_to_all x4 -> x2, waiting for transfers between devices: 144 us -> 0.01 us  [exchange(): return lax.all_to_all(x, axes, split_axis=0, concat_axis=0, tiled=True)]
    gather x8 -> x2, local copies, waits for them, and re-layouts: 81.9 us -> 0.65 us  [positions(): rows = pattern[k]]
    pallas_call x0 -> x6, Pallas kernels: none -> 78.3 us  [the longest x1 20.7 us: owner_step(): pl.pallas_call(owner_kernel, out_shape=(jax.ShapeDtypeStruct((slots, LANE...]
    scatter-add x1 -> x0, other arithmetic: 73.7 us -> none  [body(): charge_distribution = jnp.zeros((tile_roster + 1, seg_len), jnp.float32)....]
    ppermute x0 -> x7, waiting for transfers between devices: none -> 59.1 us  [the longest x3 58.6 us: gather_hamiltonian(): same.append(lax.ppermute(tiles, 'row', perm))]
    scatter x2 -> x0, local copies, waits for them, and re-layouts: 41.6 us -> none  [the longest x1 23.2 us: body(): jnp.full((devices * capacity,), tile_roster, jnp.int32).at[slots]]
    dot_general x4 -> x0, matrix products: 24.6 us -> none  [the longest x2 16.9 us: one_row(): jnp.einsum('efg,efab->egab', match, rows_h, preferred_element_type=jnp.fl...]
    reduce_sum x5 -> x0, other arithmetic: 11.4 us -> none  [the longest x1 3.18 us: slot_ranks(): jnp.sum((same_owner & earlier_mask[None, :, :]).astype(jnp.int32), axis=2)]
  transfers between devices with their start and end apart: 5 -> 9, of which waited for: 3 -> 4; matrix products, arithmetic and copies ran while one was open for 33% -> 1% of each run, Pallas kernels for 0% -> 10%
where the time goes in v1:
time: 290 us; the launch traced here: 289 us
  blocking collectives  101 us (35%)
  Pallas kernels  78.3 us (27%)
  waiting for transfers between devices  59.1 us (20%)
  starting transfers between devices  38.9 us (13%)
  local copies, waits for them, and re-layouts  10.2 us (4%)
    all_to_all x1, blocking collectives, exchange(): return lax.all_to_all(x, axes, split_axis=0, concat_axis=0, tiled=True)  92 us
    ppermute x3, waiting for transfers between devices, gather_hamiltonian(): same.append(lax.ppermute(tiles, 'row', perm))  58.6 us
    all_to_all x2, starting transfers between devices, exchange(): return lax.all_to_all(x, axes, split_axis=0, concat_axis=0, tiled=True)  29.4 us
    pallas_call x1, Pallas kernels, owner_step(): pl.pallas_call(owner_kernel, out_shape=(jax.ShapeDtypeStruct((slots, LANE...  20.7 us
    pallas_call x1, Pallas kernels, unpack(): pl.pallas_call(functools.partial(unpack_kernel, n_row), out_shape=(jax.Sh...  18.5 us
    pallas_call x1, Pallas kernels, pack(): pl.pallas_call(pack_kernel, out_shape=jax.ShapeDtypeStruct((slots, LANES)...  17 us
    pallas_call x1, Pallas kernels, main_product(): pl.pallas_call(main_kernel, out_shape=jax.ShapeDtypeStruct((rows, BLK, nn...  10.9 us
    pallas_call x1, Pallas kernels, rank_and_labels(): pl.pallas_call(functools.partial(rank_kernel, devices), out_shape=(jax.Sh...  9.66 us
  transfers between devices with their start and end apart: 9, of which 4 were waited for; matrix products, arithmetic and copies ran while one was open for 1% of the time, Pallas kernels for 10%

profile of v1, /device:TPU:1, one launch (start us, length us, event | category | flops | bytes accessed | tf_op | source)
XLA Modules:
  0.0 289.3 jit_solution(12434314579444027044)
XLA Ops:
  0.6 0.7 copy-done.7
  1.4 0.7 copy-done.8
  2.1 9.7 %rank.1 = (s32[48,128]{1,0:T(8,128)S(1)}, s32[256,128]{1,0:T(8,128)}) custom-call(s32[48,128]{1,0:T(8,128)S(1)} %bitcast.19, s32[48,128]{1,0:T(8,128)S(1)} %bitcast.20), custom_call_target="tpu_custom_call" | custom-call | flops 5000000000 | bytes 262144 | tf_op jit(solution)/shard_map/rank/pallas_call | solution.py:73
  11.8 15.6 %all-to-all-start = ((s32[256,1,128]{2,1,0:T(1,128)}), s32[256,1,128]{2,1,0:T(1,128)S(1)}, u32[]{:S(2)}, u32[]{:S(2)}) async-start(s32[256,1,128]{2,1,0:T(1,128)} %bitcast.3), calls=%async_computation | async-start | bytes 262144 | tf_op jit(solution)/shard_map/all_to_all | solution.py:414
  27.4 0.0 copy-start.1
  27.4 1.4 copy-done.1
  28.8 17.0 %pack.1 = bf16[12288,128]{1,0:T(8,128)(2,1)S(1)} custom-call(s32[48,128]{1,0:T(8,128)S(1)} %get-tuple-element.11.slot_ref, bf16[6144,128]{1,0:T(8,128)(2,1)S(1)} %copy-done.1), custom_call_target="tpu_custom_call" | custom-call | flops 12000000000 | bytes 5242880 | tf_op jit(solution)/shard_map/pack/pallas_call | solution.py:128
  45.9 1.6 copy-done
  47.5 0.0 all-to-all-done
  47.5 13.7 %all-to-all-start.1 = ((bf16[256,48,128]{2,1,0:T(8,128)(2,1)}), bf16[256,48,128]{2,1,0:T(8,128)(2,1)S(1)}, u32[]{:S(2)}, u32[]{:S(2)}) async-start(bf16[256,48,128]{2,1,0:T(8,128)(2,1)} %bitcast.15), calls=%async_computation.1 | async-start | bytes 6291456 | tf_op jit(solution)/shard_map/all_to_all | solution.py:414
  61.2 2.6 collective-permute-start.2
  63.9 0.6 collective-permute-start.1
  64.4 0.6 collective-permute-start
  65.0 1.2 collective-permute-start.3
  66.3 0.1 add_multiply_fusion
  66.4 30.6 %collective-permute-done.2.refs_3_ = bf16[2,12,128,128]{3,2,1,0:T(8,128)(2,1)} collective-permute-done((bf16[2,12,128,128]{3,2,1,0:T(8,128)(2,1)}, bf16[2,12,128,128]{3,2,1,0:T(8,128)(2,1)}, u32[]{:S(2)}, u32[]{:S(2)}) %collective-permute-start.2) | collective-permute-done | bytes 786464 | tf_op jit(solution)/shard_map/ppermute | solution.py:368
  97.0 1.7 collective-permute-start.6
  98.7 0.5 collective-permute-done.1.refs_2_
  99.2 2.0 collective-permute-start.5
  101.2 27.5 %collective-permute-done.refs_1_ = bf16[2,12,128,128]{3,2,1,0:T(8,128)(2,1)} collective-permute-done((bf16[2,12,128,128]{3,2,1,0:T(8,128)(2,1)}, bf16[2,12,128,128]{3,2,1,0:T(8,128)(2,1)}, u32[]{:S(2)}, u32[]{:S(2)}) %collective-permute-start) | collective-permute-done | bytes 786464 | tf_op jit(solution)/shard_map/ppermute | solution.py:368
  128.7 0.8 collective-permute-start.4
  129.5 0.1 iota_add_fusion
  129.6 0.1 add.105
  129.7 0.1 add.104
  129.8 0.6 gather_fusion
  130.3 0.1 copy.14
  130.4 0.1 copy.12
  130.5 0.1 copy.13
  130.6 0.2 fusion
  130.8 0.1 copy.15
  130.9 0.1 reshape.107.col_at
  131.0 0.1 fusion.1.row_at
  131.1 0.1 reshape.104.label_ref
  131.2 0.0 collective-permute-done.3.refs_4_
  131.2 0.0 collective-permute-done.6.refs_7_
  131.2 0.0 collective-permute-done.5.refs_6_
  131.2 0.5 collective-permute-done.4.refs_5_
  131.8 1.1 copy-done.3
  132.9 1.1 copy-done.4
  134.0 10.9 %hamiltonian.1.main_ref = f32[2,128,1536]{2,1,0:T(8,128)S(1)} custom-call(s32[2,16]{1,0:T(2,128)S(1)} %fusion.1.row_at, s32[2,192]{1,0:T(2,128)S(1)} %reshape.107.col_at, bf16[2,12,128,128]{3,2,1,0:T(8,128)(2,1)S(1)} %copy-done.4, bf16[2,12,128,128]{3,2,1,0:T(8,128)(2,1)S(1)} %copy-done.3, bf16[2,12,128,128]{3,2,1,0:T(8,128)(2,1)} %collective-permute-done.refs_1_, ...), custom_call_target="tpu_custom_call" | custom-call | flops 10000000000 | bytes 10485760 | tf_op jit(solution)/shard_map/hamiltonian/pallas_call | solution.py:326
  144.9 1.2 copy-done.9
  146.1 0.0 all-to-all-done.1
  146.1 1.0 copy-done.6
  147.1 20.7 %owner.1 = (bf16[12288,128]{1,0:T(8,128)(2,1)S(1)}, f32[768,128]{1,0:T(8,128)}) custom-call(s32[96,128]{1,0:T(8,128)S(1)} %reshape.104.label_ref, bf16[12288,128]{1,0:T(8,128)(2,1)S(1)} %bitcast.14, f32[768,128]{1,0:T(8,128)S(1)} %copy-done.6), custom_call_target="tpu_custom_call" | custom-call | flops 20000000000 | bytes 7340032 | tf_op jit(solution)/shard_map/owner/pallas_call | solution.py:192
  167.7 92.0 %all_to_all.20 = bf16[256,48,128]{2,1,0:T(8,128)(2,1)S(1)} all-to-all(bf16[256,48,128]{2,1,0:T(8,128)(2,1)S(1)} %bitcast.16), channel_id=1, replica_groups=mesh['orb'=32,'row'=8] {'orb','row'}, dimensions={0} | all-to-all | bytes 6291456 | tf_op jit(solution)/shard_map/all_to_all | solution.py:414
  259.7 18.5 %unpack.1 = (bf16[6144,128]{1,0:T(8,128)(2,1)}, f32[8,8,128]{2,1,0:T(8,128)S(1)}) custom-call(s32[48,128]{1,0:T(8,128)S(1)} %get-tuple-element.11.slot_ref, bf16[12288,128]{1,0:T(8,128)(2,1)S(1)} %bitcast.17, bf16[6144,128]{1,0:T(8,128)(2,1)S(1)} %copy-done.2), custom_call_target="tpu_custom_call" | custom-call | flops 12000000000 | bytes 7340032 | tf_op jit(solution)/shard_map/unpack/pallas_call | solution.py:263
  278.2 9.5 %all_to_all.21 = f32[8,8,128]{2,1,0:T(8,128)S(1)} all-to-all(f32[8,8,128]{2,1,0:T(8,128)S(1)} %get-tuple-element.18), channel_id=1, replica_groups=mesh['orb'=32,'row'=8] {'row'}, dimensions={0} | all-to-all | bytes 65536 | tf_op jit(solution)/shard_map/all_to_all | solution.py:433
  287.7 1.6 final.1
  (19 shorter events, 0.1 us)
Async XLA Ops:
  0.6 0.7 copy-start.7
  1.4 0.7 copy-start.8
  11.8 35.7 %all-to-all-start = ((s32[256,1,128]{2,1,0:T(1,128)}), s32[256,1,128]{2,1,0:T(1,128)S(1)}, u32[]{:S(2)}, u32[]{:S(2)}) async-start(s32[256,1,128]{2,1,0:T(1,128)} %bitcast.3), calls=%async_computation | async-start | bytes 262144 | tf_op jit(solution)/shard_map/all_to_all | solution.py:414
  27.4 1.4 copy-start.1
  45.9 1.6 copy-start
  47.5 82.3 %copy-start.11 = (s32[16,12]{1,0:T(8,128)S(1)}, s32[16,12]{1,0:T(8,128)}, u32[]{:S(2)}) copy-start(s32[16,12]{1,0:T(8,128)} %param.13) | copy-start | bytes 2308
  47.5 98.5 %all-to-all-start.1 = ((bf16[256,48,128]{2,1,0:T(8,128)(2,1)}), bf16[256,48,128]{2,1,0:T(8,128)(2,1)S(1)}, u32[]{:S(2)}, u32[]{:S(2)}) async-start(bf16[256,48,128]{2,1,0:T(8,128)(2,1)} %bitcast.15), calls=%async_computation.1 | async-start | bytes 6291456 | tf_op jit(solution)/shard_map/all_to_all | solution.py:414
  61.2 35.7 %collective-permute-start.2 = (bf16[2,12,128,128]{3,2,1,0:T(8,128)(2,1)}, bf16[2,12,128,128]{3,2,1,0:T(8,128)(2,1)}, u32[]{:S(2)}, u32[]{:S(2)}) collective-permute-start(bf16[2,12,128,128]{3,2,1,0:T(8,128)(2,1)} %refs_0_.1), channel_id=1, source_target_pairs={{0,6},{1,7},{2,0},{3,1},{4,2},{5,3},{6,4},{7,5},{8,14},{9,15},{10,... | collective-permute-start | bytes 2359304 | tf_op jit(solution)/shard_map/ppermute | solution.py:368
  63.9 35.4 %collective-permute-start.1 = (bf16[2,12,128,128]{3,2,1,0:T(8,128)(2,1)}, bf16[2,12,128,128]{3,2,1,0:T(8,128)(2,1)}, u32[]{:S(2)}, u32[]{:S(2)}) collective-permute-start(bf16[2,12,128,128]{3,2,1,0:T(8,128)(2,1)} %refs_0_.1), channel_id=1, source_target_pairs={{0,4},{1,5},{2,6},{3,7},{4,0},{5,1},{6,2},{7,3},{8,12},{9,13},{10,... | collective-permute-start | bytes 2359304 | tf_op jit(solution)/shard_map/ppermute | solution.py:368
  64.4 64.3 %collective-permute-start = (bf16[2,12,128,128]{3,2,1,0:T(8,128)(2,1)}, bf16[2,12,128,128]{3,2,1,0:T(8,128)(2,1)}, u32[]{:S(2)}, u32[]{:S(2)}) collective-permute-start(bf16[2,12,128,128]{3,2,1,0:T(8,128)(2,1)} %refs_0_.1), channel_id=1, source_target_pairs={{0,2},{1,3},{2,4},{3,5},{4,6},{5,7},{6,0},{7,1},{8,10},{9,11},{10,... | collective-permute-start | bytes 2359304 | tf_op jit(solution)/shard_map/ppermute | solution.py:368
  65.0 66.2 %collective-permute-start.3 = (bf16[2,12,128,128]{3,2,1,0:T(8,128)(2,1)}, bf16[2,12,128,128]{3,2,1,0:T(8,128)(2,1)}, u32[]{:S(2)}, u32[]{:S(2)}) collective-permute-start(bf16[2,12,128,128]{3,2,1,0:T(8,128)(2,1)} %refs_0_.1), channel_id=1, source_target_pairs={{0,1},{1,0},{2,3},{3,2},{4,5},{5,4},{6,7},{7,6},{8,9},{9,8},{10,11... | collective-permute-start | bytes 2359304 | tf_op jit(solution)/shard_map/ppermute | solution.py:370
  97.0 34.3 %collective-permute-start.6 = (bf16[2,12,128,128]{3,2,1,0:T(8,128)(2,1)}, bf16[2,12,128,128]{3,2,1,0:T(8,128)(2,1)}, u32[]{:S(2)}, u32[]{:S(2)}) collective-permute-start(bf16[2,12,128,128]{3,2,1,0:T(8,128)(2,1)} %collective-permute-done.2.refs_3_), channel_id=1, source_target_pairs={{0,1},{1,0},{2,3},{3,2},{4,5},{5,4},{6,7},{7,6},{8,9},{9,8},{10,11... | collective-permute-start | bytes 2359304 | tf_op jit(solution)/shard_map/ppermute | solution.py:370
  99.2 32.0 %collective-permute-start.5 = (bf16[2,12,128,128]{3,2,1,0:T(8,128)(2,1)}, bf16[2,12,128,128]{3,2,1,0:T(8,128)(2,1)}, u32[]{:S(2)}, u32[]{:S(2)}) collective-permute-start(bf16[2,12,128,128]{3,2,1,0:T(8,128)(2,1)} %collective-permute-done.1.refs_2_), channel_id=1, source_target_pairs={{0,1},{1,0},{2,3},{3,2},{4,5},{5,4},{6,7},{7,6},{8,9},{9,8},{10,11... | collective-permute-start | bytes 2359304 | tf_op jit(solution)/shard_map/ppermute | solution.py:370
  128.7 3.0 %collective-permute-start.4 = (bf16[2,12,128,128]{3,2,1,0:T(8,128)(2,1)}, bf16[2,12,128,128]{3,2,1,0:T(8,128)(2,1)}, u32[]{:S(2)}, u32[]{:S(2)}) collective-permute-start(bf16[2,12,128,128]{3,2,1,0:T(8,128)(2,1)} %collective-permute-done.refs_1_), channel_id=1, source_target_pairs={{0,1},{1,0},{2,3},{3,2},{4,5},{5,4},{6,7},{7,6},{8,9},{9,8},{10,11... | collective-permute-start | bytes 2359304 | tf_op jit(solution)/shard_map/ppermute | solution.py:370
  131.8 1.1 copy-start.3
  132.9 1.1 copy-start.4
  144.9 1.2 copy-start.9
  146.1 1.0 copy-start.6
  167.7 92.0 %copy-start.2 = (bf16[6144,128]{1,0:T(8,128)(2,1)S(1)}, bf16[6144,128]{1,0:T(8,128)(2,1)}, u32[]{:S(2)}) copy-start(bf16[6144,128]{1,0:T(8,128)(2,1)} %x_ref.3) | copy-start | bytes 4718596
  259.7 28.0 %copy-start.5 = (bf16[2,12,128,128]{3,2,1,0:T(8,128)(2,1)S(1)}, bf16[2,12,128,128]{3,2,1,0:T(8,128)(2,1)}, u32[]{:S(2)}) copy-start(bf16[2,12,128,128]{3,2,1,0:T(8,128)(2,1)} %d_ref.3) | copy-start | bytes 2359300
  259.7 28.0 %copy-start.10 = (f32[2,128,1536]{2,1,0:T(8,128)S(1)}, f32[2,128,1536]{2,1,0:T(8,128)}, u32[]{:S(2)}) copy-start(f32[2,128,1536]{2,1,0:T(8,128)} %copy-done.9) | copy-start | bytes 4718596

commit v2 on v1

v2 whole, which is shorter than its diff:
```python
import functools

import jax
import jax.numpy as jnp
from jax import lax
from jax.experimental import pallas as pl
from jax.experimental.pallas import tpu as pltpu
from jax.sharding import PartitionSpec as P

BLK = 128
SEGF = 24
CAP = 48
PAIR = 50
LANES = 128
F32 = jnp.float32
BF16 = jnp.bfloat16
VMEM = pl.BlockSpec(memory_space=pltpu.VMEM)
SMEM = pl.BlockSpec(memory_space=pltpu.SMEM)


def params(mib):
    return pltpu.CompilerParams(vmem_limit_bytes=mib << 20)


def cost(us, nbytes):
    return pl.CostEstimate(
        flops=int(us * 1e9), bytes_accessed=int(nbytes), transcendentals=0
    )


def iota(shape, axis):
    return lax.broadcasted_iota(jnp.int32, shape, axis)


def hot_rows(wide, which):
    return (wide == which).astype(F32).astype(BF16)


def columns(row):
    return jnp.transpose(jnp.broadcast_to(row, (LANES, LANES)))


def rank_kernel(devices, me_ref, dest_ref, tile_ref, slot_ref, high_ref, low_ref, acc):
    blocks = dest_ref.shape[0]
    owner = iota((LANES, devices), 1)
    dst, src = iota((LANES + 8, LANES), 0), iota((LANES + 8, LANES), 1)
    tri = ((dst >= LANES) | (src < dst)).astype(F32).astype(BF16)
    ones = jnp.ones((8, devices), BF16)
    place = iota((LANES, LANES), 0)
    turn = (me_ref[0] * PAIR) & (LANES - 1)
    acc[...] = jnp.zeros_like(acc)
    group = 4

    def step(q, run):
        hots, spreads = [], []
        for j in range(group):
            b = q * group + j
            d = dest_ref[pl.ds(b, 1), :]
            wide = jnp.concatenate([columns(d)] * (devices // LANES), axis=1)
            hit = owner == wide
            hot = hit.astype(F32).astype(BF16)
            hots.append(hot)
            counts = jnp.dot(tri, hot, preferred_element_type=F32)
            before = counts[:LANES] + run[0:1]
            run = run + counts[LANES:]
            mine = jnp.where(hit, before, 0.0).astype(BF16)
            rank = lax.dot_general(
                ones, mine, (((1,), (1,)), ((), ())), preferred_element_type=F32
            )
            rank = rank[0:1].astype(jnp.int32)
            slot_ref[pl.ds(b, 1), :] = d * PAIR + rank
            label = tile_ref[pl.ds(b, 1), :] + 1
            at = place == ((rank + turn) & (LANES - 1))
            high = jnp.where(at, (label >> 2).astype(F32), 0.0)
            low = jnp.where(at, (label & 3).astype(F32), 0.0)
            spreads.append(jnp.concatenate([high, low], axis=0).astype(BF16))
        acc[...] += jnp.dot(
            jnp.concatenate(spreads, axis=1),
            jnp.concatenate(hots, axis=0),
            preferred_element_type=F32,
        )
        return run

    lax.fori_loop(0, blocks // group, step, jnp.zeros((8, devices), F32))
    high_ref[...] = jnp.transpose(acc[:LANES, :])
    low_ref[...] = jnp.transpose(acc[LANES:, :])


def ranks(me, dest, tile, devices):
    blocks = dest.shape[0]
    return pl.pallas_call(
        functools.partial(rank_kernel, devices),
        out_shape=(
            jax.ShapeDtypeStruct((blocks, LANES), jnp.int32),
            jax.ShapeDtypeStruct((devices, LANES), F32),
            jax.ShapeDtypeStruct((devices, LANES), F32),
        ),
        in_specs=[SMEM, VMEM, VMEM],
        out_specs=(VMEM,) * 3,
        scratch_shapes=[pltpu.VMEM((2 * LANES, devices), F32)],
        compiler_params=params(5),
        cost_estimate=cost(4, 1 << 18),
        name="rank",
    )(me, dest, tile)


ROWS = 64


def widen(src_ref, dst):
    def step(i, c):
        at = pl.ds(pl.multiple_of(i * 256, 256), 256)
        dst[at, :] = src_ref[at, :].astype(F32)
        return c

    lax.fori_loop(0, src_ref.shape[0] // 256, step, 0)


def pack_kernel(slot_ref, x_ref, high_ref, low_ref, out_ref, xf, of):
    rows = x_ref.shape[0]
    slots = of.shape[0]
    devices = high_ref.shape[0]
    widen(x_ref, xf)

    def clear(i, c):
        of[pl.ds(pl.multiple_of(i * 512, 512), 512), :] = jnp.zeros((512, LANES), F32)
        return c

    lax.fori_loop(0, slots // 512, clear, 0)

    def move(i, c):
        base = i * ROWS
        for j in range(ROWS):
            of[pl.ds(slot_ref[base + j], 1), :] = xf[pl.ds(base + j, 1), :]
        return c

    lax.fori_loop(0, rows // ROWS, move, 0)
    of[pl.ds(CAP, devices, stride=PAIR), :] = high_ref[...]
    of[pl.ds(CAP + 1, devices, stride=PAIR), :] = low_ref[...]

    def narrow(i, c):
        at = pl.ds(pl.multiple_of(i * 256, 256), 256)
        out_ref[at, :] = of[at, :].astype(BF16)
        return c

    lax.fori_loop(0, slots // 256, narrow, 0)


def pack(slot, x, high, low):
    rows = x.shape[0]
    slots = high.shape[0] * PAIR
    return pl.pallas_call(
        pack_kernel,
        out_shape=jax.ShapeDtypeStruct((slots, LANES), BF16),
        in_specs=[SMEM, VMEM, VMEM, VMEM],
        out_specs=VMEM,
        scratch_shapes=[pltpu.VMEM((rows, LANES), F32), pltpu.VMEM((slots, LANES), F32)],
        compiler_params=params(18),
        cost_estimate=cost(10, 5 << 20),
        name="pack",
    )(slot, x, high, low)


DEPTH = 1280
CHUNK = 1280


def slot_labels(high, low):
    devices = high.shape[0]
    groups = -(-devices * PAIR // LANES // 8) * 8
    source, lane = iota((devices, LANES), 0), iota((devices, LANES), 1)
    offset = (source * PAIR) & (LANES - 1)
    near = lane >= offset
    k, s = iota((groups, devices), 0), iota((groups, devices), 1)
    first = (s * PAIR) >> 7
    left = jnp.concatenate([first == k, first + 1 == k], axis=1)
    left = left.astype(F32).astype(BF16)

    def part(x):
        return jnp.concatenate(
            [jnp.where(near, x, 0.0), jnp.where(near, 0.0, x)], axis=0
        ).astype(BF16)

    right = jnp.concatenate([part(high), part(low)], axis=1)
    both = jnp.dot(left, right, preferred_element_type=F32)
    return (both[:, :LANES] * 4.0 + both[:, LANES:]).astype(jnp.int32) - 1


def owner_kernel(v_ref, field_ref, out_ref, charge_ref, vf, label, acc, pot):
    slots = v_ref.shape[0]
    tiles = field_ref.shape[0]
    devices = slots // PAIR
    widen(v_ref, vf)
    label[...] = slot_labels(
        vf[pl.ds(CAP, devices, stride=PAIR), :],
        vf[pl.ds(CAP + 1, devices, stride=PAIR), :],
    )
    acc[...] = jnp.zeros_like(acc)
    cell = iota((tiles, LANES), 0)

    def add(k, c):
        hot = []
        for j in range(DEPTH // LANES):
            hot.append(hot_rows(cell, label[pl.ds(k * (DEPTH // LANES) + j, 1), :]))
        v = vf[pl.ds(pl.multiple_of(k * DEPTH, DEPTH), DEPTH), :]
        square = v * v
        high = square.astype(BF16)
        low = (square - high.astype(F32)).astype(BF16)
        acc[...] += jnp.dot(
            jnp.concatenate(hot, axis=1),
            jnp.concatenate([high, low], axis=1),
            preferred_element_type=F32,
        )
        return c

    lax.fori_loop(0, slots // DEPTH, add, 0)
    charge = acc[:, :LANES] + acc[:, LANES:]
    charge_ref[...] = charge
    field = field_ref[...] - 1.5 * jnp.exp(jnp.log(1.0 + charge) * (1.0 / 3.0))
    high = field.astype(BF16)
    pot[:, :LANES] = high
    pot[:, LANES:] = (field - high.astype(F32)).astype(BF16)
    lane = iota((LANES, tiles), 1)

    def apply(k, c):
        hot = []
        for j in range(CHUNK // LANES):
            col = columns(label[pl.ds(k * (CHUNK // LANES) + j, 1), :])
            hot.append(hot_rows(lane, jnp.concatenate([col] * (tiles // LANES), axis=1)))
        got = jnp.dot(
            jnp.concatenate(hot, axis=0), pot[...], preferred_element_type=F32
        )
        at = pl.ds(pl.multiple_of(k * CHUNK, CHUNK), CHUNK)
        here = got[:, :LANES] + got[:, LANES:]
        out_ref[at, :] = (here * vf[at, :]).astype(BF16)
        return c

    lax.fori_loop(0, slots // CHUNK, apply, 0)


def owner_step(v, field):
    slots = v.shape[0]
    tiles = field.shape[0]
    return pl.pallas_call(
        owner_kernel,
        out_shape=(
            jax.ShapeDtypeStruct(v.shape, BF16),
            jax.ShapeDtypeStruct((tiles, LANES), F32),
        ),
        in_specs=[VMEM] * 2,
        out_specs=(VMEM,) * 2,
        scratch_shapes=[
            pltpu.VMEM((slots, LANES), F32),
            pltpu.VMEM((-(-slots // LANES // 8) * 8, LANES), jnp.int32),
            pltpu.VMEM((tiles, 2 * LANES), F32),
            pltpu.VMEM((tiles, 2 * LANES), BF16),
        ],
        compiler_params=params(28),
        cost_estimate=cost(16, 7 << 20),
        name="owner",
    )(v, field)


def unpack_kernel(n_row, slot_ref, ret_ref, x_ref, out_ref, shift_ref, rf, of, part):
    rows = x_ref.shape[0]
    widen(ret_ref, rf)

    def move(i, c):
        base = i * ROWS
        for j in range(ROWS):
            of[pl.ds(base + j, 1), :] = rf[pl.ds(slot_ref[base + j], 1), :]
        return c

    lax.fori_loop(0, rows // ROWS, move, 0)
    count = 8

    def narrow(i, c):
        at = pl.ds(pl.multiple_of(i * count * SEGF, count * SEGF), count * SEGF)
        got = of[at, :]
        out_ref[at, :] = got.astype(BF16)
        work = (got * x_ref[at, :].astype(F32)).reshape(count, SEGF, LANES)
        part[pl.ds(pl.multiple_of(i * count, count), count), :] = jnp.sum(work, axis=1)
        return c

    lax.fori_loop(0, rows // (count * SEGF), narrow, 0)
    functions = rows // SEGF
    total = lax.dot_general(
        jnp.ones((8, LANES), F32),
        part[...],
        (((1,), (1,)), ((), ())),
        precision=lax.Precision.HIGHEST,
        preferred_element_type=F32,
    )
    total = total * (1.0 / (SEGF * LANES))
    one = jnp.concatenate(
        [total[0:1, i * BLK : (i + 1) * BLK] for i in range(functions // BLK)]
        + [jnp.zeros((8 - functions // BLK, BLK), F32)],
        axis=0,
    )
    one = one.astype(BF16).astype(F32)
    for r in range(n_row):
        shift_ref[r] = one


def unpack(slot, ret, x, n_row):
    rows = x.shape[0]
    return pl.pallas_call(
        functools.partial(unpack_kernel, n_row),
        out_shape=(
            jax.ShapeDtypeStruct((rows, LANES), BF16),
            jax.ShapeDtypeStruct((n_row, 8, LANES), F32),
        ),
        in_specs=[SMEM, VMEM, VMEM],
        out_specs=(VMEM,) * 2,
        scratch_shapes=[
            pltpu.VMEM(ret.shape, F32),
            pltpu.VMEM((rows, LANES), F32),
            pltpu.VMEM((rows // SEGF, LANES), F32),
        ],
        compiler_params=params(20),
        cost_estimate=cost(10, 7 << 20),
        name="unpack",
    )(slot, ret, x)


def main_kernel(row_at, col_at, d_ref, *refs):
    bufs, (out_ref, sel, dcat) = refs[:-3], refs[-3:]
    rows, nnz = d_ref.shape[:2]
    width = nnz * BLK

    def one(i, carry):
        def clear(e, c):
            sel[pl.ds(pl.multiple_of(e * BLK, BLK), BLK), :] = jnp.zeros(
                (BLK, sel.shape[1]), BF16
            )
            return c

        lax.fori_loop(0, nnz, clear, 0)
        for e in range(nnz):
            dcat[:, e * BLK : (e + 1) * BLK] = d_ref[i, e]
        places = [(buf, j) for buf in bufs for j in range(buf.shape[0])]
        for q, (buf, j) in enumerate(places):
            e = row_at[i, q]

            @pl.when(e < nnz)
            def _():
                top = pl.multiple_of(e * BLK, BLK)

                def put(f, c):
                    g = col_at[i, q * nnz + f]
                    left = pl.multiple_of(g * BLK, BLK)
                    sel[pl.ds(top, BLK), pl.ds(left, BLK)] = buf[j, f]
                    return c

                lax.fori_loop(0, nnz, put, 0)

        def mult(n, c):
            at = pl.ds(pl.multiple_of(n * 256, 256), 256)
            out_ref[i, :, at] = jnp.dot(dcat[...], sel[:, at], preferred_element_type=F32)
            return c

        lax.fori_loop(0, width // 256, mult, 0)
        return carry

    lax.fori_loop(0, rows, one, 0)


def main_product(row_at, col_at, d, bufs):
    rows, nnz = d.shape[:2]
    return pl.pallas_call(
        main_kernel,
        out_shape=jax.ShapeDtypeStruct((rows, BLK, nnz * BLK), F32),
        in_specs=[SMEM, SMEM, VMEM] + [VMEM] * len(bufs),
        out_specs=VMEM,
        scratch_shapes=[
            pltpu.VMEM((nnz * BLK, (nnz + 1) * BLK), BF16),
            pltpu.VMEM((BLK, nnz * BLK), BF16),
        ],
        compiler_params=params(18),
        cost_estimate=cost(10, 10 << 20),
        name="hamiltonian",
    )(row_at, col_at, d, *bufs)


def final_kernel(at_ref, main_ref, d_ref, shift_ref, out_ref):
    rows, nnz = d_ref.shape[:2]
    for i in range(rows):
        for g in range(nnz):
            s = shift_ref[pl.ds(at_ref[i, g], 1), :]
            out_ref[i, g] = (
                main_ref[i, :, g * BLK : (g + 1) * BLK] + d_ref[i, g].astype(F32) * s
            ).astype(BF16)


def final(at, main, d, shift):
    return pl.pallas_call(
        final_kernel,
        out_shape=jax.ShapeDtypeStruct(d.shape, BF16),
        in_specs=[SMEM, VMEM, VMEM, VMEM],
        out_specs=VMEM,
        compiler_params=params(6),
        cost_estimate=cost(2, 4 << 20),
        name="final",
    )(at, main, d, shift)


ORDER = (0, 1, 3, 2)


def gather_hamiltonian(tiles, n_row):
    chips = n_row // 2
    assert chips == len(ORDER) and tiles.shape[0] == 2
    ahead = [(r, ((r // 2 + 1) % chips) * 2 + r % 2) for r in range(n_row)]
    behind = [(r, ((r // 2 - 1) % chips) * 2 + r % 2) for r in range(n_row)]
    one = lax.ppermute(tiles, "row", ahead)
    three = lax.ppermute(tiles, "row", behind)
    return one, three


def spread_hamiltonian(tiles, one, three, n_row):
    chips = n_row // 2
    ahead = [(r, ((r // 2 + 1) % chips) * 2 + r % 2) for r in range(n_row)]
    behind = [(r, ((r // 2 - 1) % chips) * 2 + r % 2) for r in range(n_row)]
    swap = [(r, r ^ 1) for r in range(n_row)]
    two_top = lax.ppermute(one[:1], "row", ahead)
    two_end = lax.ppermute(three[1:], "row", behind)
    same = [tiles, one, three, two_top, two_end]
    return same + [lax.ppermute(t, "row", swap) for t in same]


def positions(pattern, own_rows, n_row):
    me = lax.axis_index("row")
    chips = n_row // 2
    chip, core = me // 2, me % 2
    back = jnp.asarray(ORDER, jnp.int32)
    owner = (chip - back + chips) % chips * 2
    owner = jnp.concatenate([owner + core, owner + 1 - core])
    k = (owner[:, None] * own_rows + jnp.arange(own_rows, dtype=jnp.int32)).reshape(-1)
    own = lax.dynamic_slice_in_dim(pattern, me * own_rows, own_rows, 0)
    nnz = pattern.shape[1]
    local = own % (own_rows * n_row)
    index = jnp.arange(nnz, dtype=jnp.int32)
    row_at = jnp.min(
        jnp.where(local[:, None, :] == k[None, :, None], index, nnz), axis=2
    )
    rows = pattern[k]
    col_at = jnp.min(
        jnp.where(own[:, None, None, :] == rows[None, :, :, None], index, nnz), axis=3
    )
    shift_at = local // own_rows * 8 + local % own_rows
    return row_at, col_at.reshape(own_rows, -1), shift_at


def body(
    orbital_fragments,
    receiving_devices,
    fragment_grid_tile,
    outside_field_grid,
    density_matrix_tiles,
    energy_operator_tiles,
    tile_column_numbers,
):
    seg_dev = orbital_fragments.shape[0]
    n_orb = lax.axis_size("orb")
    n_row = lax.axis_size("row")
    devices = n_orb * n_row
    axes = ("orb", "row")

    def exchange(x):
        pairs = x.reshape(devices, -1, 2, LANES)
        got = lax.all_to_all(pairs, axes, split_axis=0, concat_axis=0, tiled=True)
        return got.reshape(-1, LANES)

    own_rows = density_matrix_tiles.shape[0]
    row_at, col_at, shift_at = positions(tile_column_numbers, own_rows, n_row)
    one, three = gather_hamiltonian(energy_operator_tiles, n_row)

    dest = receiving_devices.reshape(seg_dev // LANES, LANES)
    tile = fragment_grid_tile.reshape(seg_dev // LANES, LANES)
    me = (lax.axis_index("orb") * n_row + lax.axis_index("row")).reshape(1)
    slot, high, low = ranks(me, dest, tile, devices)
    slot = slot.reshape(seg_dev)
    outgoing = pack(slot, orbital_fragments, high, low)
    outgoing, one, three = lax.optimization_barrier((outgoing, one, three))
    arrived = exchange(outgoing)
    bufs = spread_hamiltonian(energy_operator_tiles, one, three, n_row)
    main = main_product(row_at, col_at, density_matrix_tiles, bufs)

    arrived, main = lax.optimization_barrier((arrived, main))
    results, charge = owner_step(arrived, outside_field_grid)
    applied, shift = unpack(slot, exchange(results), orbital_fragments, n_row)
    shift = lax.all_to_all(shift, "row", split_axis=0, concat_axis=0, tiled=True)
    product = final(shift_at, main, density_matrix_tiles, shift.reshape(n_row * 8, LANES))
    return (applied, charge, product)


def solution(mesh):
    return jax.shard_map(
        body,
        mesh=mesh,
        in_specs=(
            P(("orb", "row"), None),
            P(("orb", "row"), None),
            P(("orb", "row")),
            P(("orb", "row"), None),
            P(("orb", "row"), None, None, None),
            P(("orb", "row"), None, None, None),
            P("orb", None),
        ),
        out_specs=(
            P(("orb", "row"), None),
            P(("orb", "row"), None),
            P(("orb", "row"), None, None, None),
        ),
        check_vma=False,
    )
```

time: 290 us -> 243 us (0.84)
  Pallas kernels: 78.3 us -> 58.8 us
  starting transfers between devices: 38.9 us -> 24.9 us
  blocking collectives: 101 us -> 94.1 us
  waiting for transfers between devices: 59.1 us -> 52.8 us
    ppermute x7 -> x9, waiting for transfers between devices: 59.1 us -> 16.6 us  [the longest x1 16 us: spread_hamiltonian(): two_end = lax.ppermute(three[1:], 'row', behind)]
    all_to_all x2 -> x1, waiting for transfers between devices: 0.01 us -> 36.2 us  [exchange(): got = lax.all_to_all(pairs, axes, split_axis=0, concat_axis=0, tiled=True)]
    all_to_all x2 -> x1, starting transfers between devices: 29.4 us -> 15.3 us  [exchange(): got = lax.all_to_all(pairs, axes, split_axis=0, concat_axis=0, tiled=True)]
    pallas_call x1, Pallas kernels: 18.5 us -> 8.88 us  [unpack(): pl.pallas_call(functools.partial(unpack_kernel, n_row), out_shape=(jax.Sh...]
    pallas_call x1, Pallas kernels: 17 us -> 9.27 us  [pack(): pl.pallas_call(pack_kernel, out_shape=jax.ShapeDtypeStruct((slots, LANES)...]
    all_to_all x1, blocking collectives: 92 us -> 84.6 us  [exchange(): got = lax.all_to_all(pairs, axes, split_axis=0, concat_axis=0, tiled=True)]
    slice x0 -> x2, local copies, waits for them, and re-layouts: none -> 3.53 us  [the longest x1 1.77 us: spread_hamiltonian(): two_top = lax.ppermute(one[:1], 'row', ahead)]
    unnamed x24, local copies, waits for them, and re-layouts: 8.94 us -> 5.93 us
  transfers between devices with their start and end apart: 9 -> 10, of which waited for: 4 -> 4; matrix products, arithmetic and copies ran while one was open for 1% -> 2% of each run, Pallas kernels for 10% -> 14%
where the time goes in v2:
time: 243 us
  blocking collectives  94.1 us (39%)
  Pallas kernels  58.8 us (24%)
  waiting for transfers between devices  52.8 us (22%)
  starting transfers between devices  24.9 us (10%)
  local copies, waits for them, and re-layouts  10.6 us (4%)
    all_to_all x1, blocking collectives, exchange(): got = lax.all_to_all(pairs, axes, split_axis=0, concat_axis=0, tiled=True)  84.6 us
    all_to_all x1, waiting for transfers between devices, exchange(): got = lax.all_to_all(pairs, axes, split_axis=0, concat_axis=0, tiled=True)  36.2 us
    ppermute x1, waiting for transfers between devices, spread_hamiltonian(): two_end = lax.ppermute(three[1:], 'row', behind)  16 us
    all_to_all x1, starting transfers between devices, exchange(): got = lax.all_to_all(pairs, axes, split_axis=0, concat_axis=0, tiled=True)  15.3 us
    pallas_call x1, Pallas kernels, owner_step(): pl.pallas_call(owner_kernel, out_shape=(jax.ShapeDtypeStruct(v.shape, BF1...  15.3 us
    pallas_call x1, Pallas kernels, ranks(): pl.pallas_call(functools.partial(rank_kernel, devices), out_shape=(jax.Sh...  12.9 us
    pallas_call x1, Pallas kernels, main_product(): pl.pallas_call(main_kernel, out_shape=jax.ShapeDtypeStruct((rows, BLK, nn...  10.8 us
    all_to_all x1, blocking collectives, body(): lax.all_to_all(shift, 'row', split_axis=0, concat_axis=0, tiled=True)  9.51 us
  transfers between devices with their start and end apart: 10, of which 4 were waited for; matrix products, arithmetic and copies ran while one was open for 2% of the time, Pallas kernels for 14%

profile of v2, /device:TPU:1, one launch (start us, length us, event | category | flops | bytes accessed | tf_op | source)
XLA Modules:
  0.0 242.5 jit_solution(5186954990122194445)
XLA Ops:
  0.6 3.4 %collective-permute-start.1 = (bf16[2,12,128,128]{3,2,1,0:T(8,128)(2,1)}, bf16[2,12,128,128]{3,2,1,0:T(8,128)(2,1)}, u32[]{:S(2)}, u32[]{:S(2)}) collective-permute-start(bf16[2,12,128,128]{3,2,1,0:T(8,128)(2,1)} %refs_0_.1), channel_id=1, source_target_pairs={{0,6},{1,7},{2,0},{3,1},{4,2},{5,3},{6,4},{7,5},{8,14},{9,15},{10,... | collective-permute-start | bytes 2359304 | tf_op jit(solution)/shard_map/ppermute | solution.py:416
  4.0 0.0 collective-permute-start
  4.0 0.7 copy-done.6
  4.7 0.7 copy-done.7
  5.5 12.9 %rank.1 = (s32[48,128]{1,0:T(8,128)S(1)}, f32[256,128]{1,0:T(8,128)S(1)}, f32[256,128]{1,0:T(8,128)S(1)}) custom-call(s32[1]{0:T(128)} %bitcast.me_ref, s32[48,128]{1,0:T(8,128)S(1)} %bitcast.15, s32[48,128]{1,0:T(8,128)S(1)} %bitcast.16), custom_call_target="tpu_custom_call" | custom-call | flops 4000000000 | bytes 262144 | tf_op jit(solution)/shard_map/rank/pallas_call | solution.py:91
  18.4 9.3 %pack.1 = bf16[12800,128]{1,0:T(8,128)(2,1)} custom-call(s32[6144]{0:T(1024)S(1)} %bitcast.17, bf16[6144,128]{1,0:T(8,128)(2,1)S(1)} %copy-done, f32[256,128]{1,0:T(8,128)S(1)} %get-tuple-element.16.high_ref, f32[256,128]{1,0:T(8,128)S(1)} %get-tuple-element.17.low_ref), custom_call_target="tpu_custom_call" | custom-call | flops 10000000000 | bytes 5242880 | tf_op jit(solution)/shard_map/pack/pallas_call | solution.py:152
  27.7 0.0 collective-permute-done.1.refs_2_
  27.7 0.0 collective-permute-done.refs_1_
  27.7 0.0 copy-start.10
  27.7 15.3 %all-to-all-start = ((bf16[256,25,2,128]{3,2,1,0:T(2,128)(2,1)}), bf16[256,25,2,128]{3,2,1,0:T(2,128)(2,1)S(1)}, u32[]{:S(2)}, u32[]{:S(2)}) async-start(bf16[256,25,2,128]{3,2,1,0:T(2,128)(2,1)} %bitcast.4), calls=%async_computation | async-start | bytes 6553600 | tf_op jit(solution)/shard_map/all_to_all | solution.py:471
  43.0 2.2 collective-permute-start.4
  45.3 0.1 add_multiply_fusion
  45.4 1.8 slice.6
  47.1 0.0 collective-permute-start.5
  47.2 1.8 slice.7
  49.0 0.5 collective-permute-start.6
  49.4 0.8 collective-permute-start.3
  50.2 0.7 collective-permute-start.2
  50.9 0.1 iota_add_fusion
  51.0 0.1 add.97
  51.0 16.0 %collective-permute-done.3.refs_4_ = bf16[1,12,128,128]{3,2,1,0:T(8,128)(2,1)} collective-permute-done((bf16[1,12,128,128]{3,2,1,0:T(8,128)(2,1)}, bf16[1,12,128,128]{3,2,1,0:T(8,128)(2,1)}, u32[]{:S(2)}, u32[]{:S(2)}) %collective-permute-start.3) | collective-permute-done | bytes 393248 | tf_op jit(solution)/shard_map/ppermute | solution.py:426
  67.1 0.9 collective-permute-start.8
  68.0 0.3 collective-permute-done.2.refs_3_
  68.3 1.1 collective-permute-start.7
  69.4 0.1 add.96
  69.4 0.6 gather_fusion
  70.0 0.1 copy.13
  70.1 0.1 copy.11
  70.2 0.1 copy.12
  70.3 0.2 fusion
  70.5 0.1 copy.14
  70.6 0.1 reshape.105.col_at
  70.7 0.1 fusion.1.row_at
  70.8 0.0 collective-permute-done.4.refs_5_
  70.8 0.0 collective-permute-done.8.refs_9_
  70.8 0.2 collective-permute-done.7.refs_8_
  71.0 0.0 collective-permute-done.5.refs_6_
  71.1 1.1 copy-done.2
  72.2 1.1 copy-done.3
  73.3 10.8 %hamiltonian.1.main_ref = f32[2,128,1536]{2,1,0:T(8,128)S(1)} custom-call(s32[2,16]{1,0:T(2,128)S(1)} %fusion.1.row_at, s32[2,192]{1,0:T(2,128)S(1)} %reshape.105.col_at, bf16[2,12,128,128]{3,2,1,0:T(8,128)(2,1)S(1)} %copy-done.3, bf16[2,12,128,128]{3,2,1,0:T(8,128)(2,1)S(1)} %copy-done.2, bf16[2,12,128,128]{3,2,1,0:T(8,128)(2,1)} %collective-permute-done.refs_1_, ...), custom_call_target="tpu_custom_call" | custom-call | flops 10000000000 | bytes 10485760 | tf_op jit(solution)/shard_map/hamiltonian/pallas_call | solution.py:370
  84.2 1.2 copy-done.8
  85.3 36.2 %all-to-all-done = bf16[256,25,2,128]{3,2,1,0:T(2,128)(2,1)S(1)} async-done(((bf16[256,25,2,128]{3,2,1,0:T(2,128)(2,1)}), bf16[256,25,2,128]{3,2,1,0:T(2,128)(2,1)S(1)}, u32[]{:S(2)}, u32[]{:S(2)}) %all-to-all-start) | async-done | bytes 3276832 | tf_op jit(solution)/shard_map/all_to_all | solution.py:471
  121.6 1.0 copy-done.5
  122.6 15.3 %owner.1 = (bf16[12800,128]{1,0:T(8,128)(2,1)S(1)}, f32[768,128]{1,0:T(8,128)}) custom-call(bf16[12800,128]{1,0:T(8,128)(2,1)S(1)} %bitcast.11, f32[768,128]{1,0:T(8,128)S(1)} %copy-done.5), custom_call_target="tpu_custom_call" | custom-call | flops 16000000000 | bytes 7340032 | tf_op jit(solution)/shard_map/owner/pallas_call | solution.py:244
  137.8 84.6 %all_to_all.15 = bf16[256,25,2,128]{3,2,1,0:T(2,128)(2,1)S(1)} all-to-all(bf16[256,25,2,128]{3,2,1,0:T(2,128)(2,1)S(1)} %bitcast.13), channel_id=1, replica_groups=mesh['orb'=32,'row'=8] {'orb','row'}, dimensions={0} | all-to-all | bytes 6553600 | tf_op jit(solution)/shard_map/all_to_all | solution.py:471
  222.5 8.9 %unpack.1 = (bf16[6144,128]{1,0:T(8,128)(2,1)}, f32[8,8,128]{2,1,0:T(8,128)S(1)}) custom-call(s32[6144]{0:T(1024)S(1)} %bitcast.18, bf16[12800,128]{1,0:T(8,128)(2,1)S(1)} %bitcast.12, bf16[6144,128]{1,0:T(8,128)(2,1)S(1)} %copy-done.1), custom_call_target="tpu_custom_call" | custom-call | flops 10000000000 | bytes 7340032 | tf_op jit(solution)/shard_map/unpack/pallas_call | solution.py:307
  231.4 9.5 %all_to_all.16 = f32[8,8,128]{2,1,0:T(8,128)S(1)} all-to-all(f32[8,8,128]{2,1,0:T(8,128)S(1)} %get-tuple-element.26), channel_id=1, replica_groups=mesh['orb'=32,'row'=8] {'row'}, dimensions={0} | all-to-all | bytes 65536 | tf_op jit(solution)/shard_map/all_to_all | solution.py:492
  240.9 1.6 final.1
  (23 shorter events, 0.1 us)
Async XLA Ops:
  0.6 27.1 %collective-permute-start.1 = (bf16[2,12,128,128]{3,2,1,0:T(8,128)(2,1)}, bf16[2,12,128,128]{3,2,1,0:T(8,128)(2,1)}, u32[]{:S(2)}, u32[]{:S(2)}) collective-permute-start(bf16[2,12,128,128]{3,2,1,0:T(8,128)(2,1)} %refs_0_.1), channel_id=1, source_target_pairs={{0,6},{1,7},{2,0},{3,1},{4,2},{5,3},{6,4},{7,5},{8,14},{9,15},{10,... | collective-permute-start | bytes 2359304 | tf_op jit(solution)/shard_map/ppermute | solution.py:416
  4.0 23.7 %collective-permute-start = (bf16[2,12,128,128]{3,2,1,0:T(8,128)(2,1)}, bf16[2,12,128,128]{3,2,1,0:T(8,128)(2,1)}, u32[]{:S(2)}, u32[]{:S(2)}) collective-permute-start(bf16[2,12,128,128]{3,2,1,0:T(8,128)(2,1)} %refs_0_.1), channel_id=1, source_target_pairs={{0,2},{1,3},{2,4},{3,5},{4,6},{5,7},{6,0},{7,1},{8,10},{9,11},{10,... | collective-permute-start | bytes 2359304 | tf_op jit(solution)/shard_map/ppermute | solution.py:415
  4.0 0.7 copy-start.6
  4.7 0.7 copy-start.7
  5.5 12.9 %copy-start = (bf16[6144,128]{1,0:T(8,128)(2,1)S(1)}, bf16[6144,128]{1,0:T(8,128)(2,1)}, u32[]{:S(2)}) copy-start(bf16[6144,128]{1,0:T(8,128)(2,1)} %x_ref.3) | copy-start | bytes 4718596
  27.7 17.6 %copy-start.11 = (s32[4]{0:T(128)S(1)}, s32[4]{0:T(128)}, u32[]{:S(2)}) copy-start(s32[4]{0:T(128)} %constant.95) | copy-start | bytes 52
  27.7 41.8 %copy-start.10 = (s32[16,12]{1,0:T(8,128)S(1)}, s32[16,12]{1,0:T(8,128)}, u32[]{:S(2)}) copy-start(s32[16,12]{1,0:T(8,128)} %param.14) | copy-start | bytes 2308
  27.7 93.9 %all-to-all-start = ((bf16[256,25,2,128]{3,2,1,0:T(2,128)(2,1)}), bf16[256,25,2,128]{3,2,1,0:T(2,128)(2,1)S(1)}, u32[]{:S(2)}, u32[]{:S(2)}) async-start(bf16[256,25,2,128]{3,2,1,0:T(2,128)(2,1)} %bitcast.4), calls=%async_computation | async-start | bytes 6553600 | tf_op jit(solution)/shard_map/all_to_all | solution.py:471
  43.0 27.7 %collective-permute-start.4 = (bf16[2,12,128,128]{3,2,1,0:T(8,128)(2,1)}, bf16[2,12,128,128]{3,2,1,0:T(8,128)(2,1)}, u32[]{:S(2)}, u32[]{:S(2)}) collective-permute-start(bf16[2,12,128,128]{3,2,1,0:T(8,128)(2,1)} %refs_0_.1), channel_id=1, source_target_pairs={{0,1},{1,0},{2,3},{3,2},{4,5},{5,4},{6,7},{7,6},{8,9},{9,8},{10,11... | collective-permute-start | bytes 2359304 | tf_op jit(solution)/shard_map/ppermute | solution.py:428
  47.1 23.9 %collective-permute-start.5 = (bf16[2,12,128,128]{3,2,1,0:T(8,128)(2,1)}, bf16[2,12,128,128]{3,2,1,0:T(8,128)(2,1)}, u32[]{:S(2)}, u32[]{:S(2)}) collective-permute-start(bf16[2,12,128,128]{3,2,1,0:T(8,128)(2,1)} %collective-permute-done.refs_1_), channel_id=1, source_target_pairs={{0,1},{1,0},{2,3},{3,2},{4,5},{5,4},{6,7},{7,6},{8,9},{9,8},{10,11... | collective-permute-start | bytes 2359304 | tf_op jit(solution)/shard_map/ppermute | solution.py:428
  49.0 22.1 %collective-permute-start.6 = (bf16[2,12,128,128]{3,2,1,0:T(8,128)(2,1)}, bf16[2,12,128,128]{3,2,1,0:T(8,128)(2,1)}, u32[]{:S(2)}, u32[]{:S(2)}) collective-permute-start(bf16[2,12,128,128]{3,2,1,0:T(8,128)(2,1)} %collective-permute-done.1.refs_2_), channel_id=1, source_target_pairs={{0,1},{1,0},{2,3},{3,2},{4,5},{5,4},{6,7},{7,6},{8,9},{9,8},{10,11... | collective-permute-start | bytes 2359304 | tf_op jit(solution)/shard_map/ppermute | solution.py:428
  49.4 17.7 %collective-permute-start.3 = (bf16[1,12,128,128]{3,2,1,0:T(8,128)(2,1)}, bf16[1,12,128,128]{3,2,1,0:T(8,128)(2,1)}, u32[]{:S(2)}, u32[]{:S(2)}) collective-permute-start(bf16[1,12,128,128]{3,2,1,0:T(8,128)(2,1)} %slice.7), channel_id=1, source_target_pairs={{0,6},{1,7},{2,0},{3,1},{4,2},{5,3},{6,4},{7,5},{8,14},{9,15},{10,... | collective-permute-start | bytes 1179656 | tf_op jit(solution)/shard_map/ppermute | solution.py:426
  50.2 18.0 %collective-permute-start.2 = (bf16[1,12,128,128]{3,2,1,0:T(8,128)(2,1)}, bf16[1,12,128,128]{3,2,1,0:T(8,128)(2,1)}, u32[]{:S(2)}, u32[]{:S(2)}) collective-permute-start(bf16[1,12,128,128]{3,2,1,0:T(8,128)(2,1)} %slice.6), channel_id=1, source_target_pairs={{0,2},{1,3},{2,4},{3,5},{4,6},{5,7},{6,0},{7,1},{8,10},{9,11},{10,... | collective-permute-start | bytes 1179656 | tf_op jit(solution)/shard_map/ppermute | solution.py:425
  67.1 3.7 %collective-permute-start.8 = (bf16[1,12,128,128]{3,2,1,0:T(8,128)(2,1)}, bf16[1,12,128,128]{3,2,1,0:T(8,128)(2,1)}, u32[]{:S(2)}, u32[]{:S(2)}) collective-permute-start(bf16[1,12,128,128]{3,2,1,0:T(8,128)(2,1)} %collective-permute-done.3.refs_4_), channel_id=1, source_target_pairs={{0,1},{1,0},{2,3},{3,2},{4,5},{5,4},{6,7},{7,6},{8,9},{9,8},{10,11... | collective-permute-start | bytes 1179656 | tf_op jit(solution)/shard_map/ppermute | solution.py:428
  68.3 2.8 %collective-permute-start.7 = (bf16[1,12,128,128]{3,2,1,0:T(8,128)(2,1)}, bf16[1,12,128,128]{3,2,1,0:T(8,128)(2,1)}, u32[]{:S(2)}, u32[]{:S(2)}) collective-permute-start(bf16[1,12,128,128]{3,2,1,0:T(8,128)(2,1)} %collective-permute-done.2.refs_3_), channel_id=1, source_target_pairs={{0,1},{1,0},{2,3},{3,2},{4,5},{5,4},{6,7},{7,6},{8,9},{9,8},{10,11... | collective-permute-start | bytes 1179656 | tf_op jit(solution)/shard_map/ppermute | solution.py:428
  71.1 1.1 copy-start.2
  72.2 1.1 copy-start.3
  84.2 1.2 copy-start.8
  121.6 1.0 copy-start.5
  137.8 84.6 %copy-start.1 = (bf16[6144,128]{1,0:T(8,128)(2,1)S(1)}, bf16[6144,128]{1,0:T(8,128)(2,1)}, u32[]{:S(2)}) copy-start(bf16[6144,128]{1,0:T(8,128)(2,1)} %x_ref.3) | copy-start | bytes 4718596
  222.5 18.4 %copy-start.4 = (bf16[2,12,128,128]{3,2,1,0:T(8,128)(2,1)S(1)}, bf16[2,12,128,128]{3,2,1,0:T(8,128)(2,1)}, u32[]{:S(2)}) copy-start(bf16[2,12,128,128]{3,2,1,0:T(8,128)(2,1)} %d_ref.3) | copy-start | bytes 2359300
  222.5 18.4 %copy-start.9 = (f32[2,128,1536]{2,1,0:T(8,128)S(1)}, f32[2,128,1536]{2,1,0:T(8,128)}, u32[]{:S(2)}) copy-start(f32[2,128,1536]{2,1,0:T(8,128)} %copy-done.8) | copy-start | bytes 4718596

commit v3 on v2

--- a/solution.py
+++ b/solution.py
@@ -40,50 +40,78 @@
     return jnp.transpose(jnp.broadcast_to(row, (LANES, LANES)))
 
 
-def rank_kernel(devices, me_ref, dest_ref, tile_ref, slot_ref, high_ref, low_ref, acc):
+def rank_kernel(devices, me_ref, dest_ref, tile_ref, slot_ref, back_ref, high_ref, low_ref, run, rank, acc):
     blocks = dest_ref.shape[0]
-    owner = iota((LANES, devices), 1)
-    dst, src = iota((LANES + 8, LANES), 0), iota((LANES + 8, LANES), 1)
-    tri = ((dst >= LANES) | (src < dst)).astype(F32).astype(BF16)
-    ones = jnp.ones((8, devices), BF16)
-    place = iota((LANES, LANES), 0)
-    turn = (me_ref[0] * PAIR) & (LANES - 1)
+    group = 12
+    owner = iota((devices, LANES), 0)
+    lane = iota((16, LANES), 1)
+    src, dst = iota((LANES, LANES), 0), iota((LANES, LANES), 1)
+    ahead = src < dst
+    run[...] = jnp.zeros_like(run)
+
+    def count(q, c):
+        hots, later = [], []
+        for j in range(group):
+            b = q * group + j
+            d = dest_ref[pl.ds(b, 1), :]
+            hots.append(hot_rows(owner, d))
+            after = (lane > b).astype(F32).astype(BF16)
+            later += [after] * (LANES // 16)
+            same = (columns(d) == d) & ahead
+            rank[pl.ds(b, 1), :] = jnp.sum(
+                jnp.where(same, 1.0, 0.0), axis=0, keepdims=True
+            )
+        run[...] += jnp.dot(
+            jnp.concatenate(hots, axis=1),
+            jnp.concatenate(later, axis=0),
+            preferred_element_type=F32,
+        )
+        return c
+
+    lax.fori_loop(0, blocks // group, count, 0)
+    totals = jnp.concatenate(
+        [jnp.transpose(run[i : i + LANES, :]) for i in range(0, devices, LANES)], axis=1
+    )
+    acc[:LANES, :] = totals
+
+    def order(q, c):
+        for j in range(group):
+            b = q * group + j
+            d = dest_ref[pl.ds(b, 1), :]
+            table = jnp.broadcast_to(acc[pl.ds(b, 1), :], (16, devices)).astype(BF16)
+            before = jnp.dot(table, hot_rows(owner, d), preferred_element_type=F32)
+            mine = (before[0:1] + rank[pl.ds(b, 1), :]).astype(jnp.int32)
+            rank[pl.ds(b, 1), :] = mine.astype(F32)
+            slot_ref[pl.ds(b, 1), :] = d * PAIR + mine
+            back_ref[pl.ds(b, 1), :] = d * CAP + mine
+        return c
+
+    lax.fori_loop(0, blocks // group, order, 0)
+    turn = me_ref[0] * PAIR
     acc[...] = jnp.zeros_like(acc)
-    group = 4
-
-    def step(q, run):
+
+    def mark(q, c):
         hots, spreads = [], []
         for j in range(group):
             b = q * group + j
-            d = dest_ref[pl.ds(b, 1), :]
-            wide = jnp.concatenate([columns(d)] * (devices // LANES), axis=1)
-            hit = owner == wide
-            hot = hit.astype(F32).astype(BF16)
-            hots.append(hot)
-            counts = jnp.dot(tri, hot, preferred_element_type=F32)
-            before = counts[:LANES] + run[0:1]
-            run = run + counts[LANES:]
-            mine = jnp.where(hit, before, 0.0).astype(BF16)
-            rank = lax.dot_general(
-                ones, mine, (((1,), (1,)), ((), ())), preferred_element_type=F32
-            )
-            rank = rank[0:1].astype(jnp.int32)
-            slot_ref[pl.ds(b, 1), :] = d * PAIR + rank
+            hots.append(hot_rows(owner, dest_ref[pl.ds(b, 1), :]))
+            place = rank[pl.ds(b, 1), :].astype(jnp.int32) + turn
+            at = src == (place & (LANES - 1))
             label = tile_ref[pl.ds(b, 1), :] + 1
-            at = place == ((rank + turn) & (LANES - 1))
             high = jnp.where(at, (label >> 2).astype(F32), 0.0)
             low = jnp.where(at, (label & 3).astype(F32), 0.0)
             spreads.append(jnp.concatenate([high, low], axis=0).astype(BF16))
-        acc[...] += jnp.dot(
+        acc[...] += lax.dot_general(
+            jnp.concatenate(hots, axis=1),
             jnp.concatenate(spreads, axis=1),
-            jnp.concatenate(hots, axis=0),
+            (((1,), (1,)), ((), ())),
             preferred_element_type=F32,
         )
-        return run
-
-    lax.fori_loop(0, blocks // group, step, jnp.zeros((8, devices), F32))
-    high_ref[...] = jnp.transpose(acc[:LANES, :])
-    low_ref[...] = jnp.transpose(acc[LANES:, :])
+        return c
+
+    lax.fori_loop(0, blocks // group, mark, 0)
+    high_ref[...] = acc[:, :LANES]
+    low_ref[...] = acc[:, LANES:]
 
 
 def ranks(me, dest, tile, devices):
@@ -92,12 +120,17 @@
         functools.partial(rank_kernel, devices),
         out_shape=(
             jax.ShapeDtypeStruct((blocks, LANES), jnp.int32),
+            jax.ShapeDtypeStruct((blocks, LANES), jnp.int32),
             jax.ShapeDtypeStruct((devices, LANES), F32),
             jax.ShapeDtypeStruct((devices, LANES), F32),
         ),
         in_specs=[SMEM, VMEM, VMEM],
-        out_specs=(VMEM,) * 3,
-        scratch_shapes=[pltpu.VMEM((2 * LANES, devices), F32)],
+        out_specs=(VMEM,) * 4,
+        scratch_shapes=[
+            pltpu.VMEM((devices, LANES), F32),
+            pltpu.VMEM((blocks, LANES), F32),
+            pltpu.VMEM((devices, 2 * LANES), F32),
+        ],
         compiler_params=params(5),
         cost_estimate=cost(4, 1 << 18),
         name="rank",
@@ -129,9 +162,11 @@
     lax.fori_loop(0, slots // 512, clear, 0)
 
     def move(i, c):
-        base = i * ROWS
+        base = pl.multiple_of(i * ROWS, ROWS)
+        here = slot_ref.at[pl.ds(base, ROWS)]
+        rows_in = xf.at[pl.ds(base, ROWS)]
         for j in range(ROWS):
-            of[pl.ds(slot_ref[base + j], 1), :] = xf[pl.ds(base + j, 1), :]
+            of[pl.ds(here[j], 1), :] = rows_in[j : j + 1, :]
         return c
 
     lax.fori_loop(0, rows // ROWS, move, 0)
@@ -186,10 +221,12 @@
     return (both[:, :LANES] * 4.0 + both[:, LANES:]).astype(jnp.int32) - 1
 
 
-def owner_kernel(v_ref, field_ref, out_ref, charge_ref, vf, label, acc, pot):
+def owner_kernel(v_ref, field_hbm, out_ref, charge_ref, vf, label, acc, pot, field_ref, sem):
     slots = v_ref.shape[0]
-    tiles = field_ref.shape[0]
+    tiles = charge_ref.shape[0]
     devices = slots // PAIR
+    fetch = pltpu.make_async_copy(field_hbm, field_ref, sem)
+    fetch.start()
     widen(v_ref, vf)
     label[...] = slot_labels(
         vf[pl.ds(CAP, devices, stride=PAIR), :],
@@ -216,6 +253,7 @@
     lax.fori_loop(0, slots // DEPTH, add, 0)
     charge = acc[:, :LANES] + acc[:, LANES:]
     charge_ref[...] = charge
+    fetch.wait()
     field = field_ref[...] - 1.5 * jnp.exp(jnp.log(1.0 + charge) * (1.0 / 3.0))
     high = field.astype(BF16)
     pot[:, :LANES] = high
@@ -232,10 +270,21 @@
         )
         at = pl.ds(pl.multiple_of(k * CHUNK, CHUNK), CHUNK)
         here = got[:, :LANES] + got[:, LANES:]
-        out_ref[at, :] = (here * vf[at, :]).astype(BF16)
+        vf[at, :] = here * vf[at, :]
         return c
 
     lax.fori_loop(0, slots // CHUNK, apply, 0)
+    pairs = 8
+
+    def narrow(i, c):
+        source = vf.at[pl.ds(pl.multiple_of(i * pairs * PAIR, 8), pairs * PAIR)]
+        at = pl.ds(pl.multiple_of(i * pairs * CAP, pairs * CAP), pairs * CAP)
+        out_ref[at, :] = jnp.concatenate(
+            [source[j * PAIR : j * PAIR + CAP, :] for j in range(pairs)], axis=0
+        ).astype(BF16)
+        return c
+
+    lax.fori_loop(0, devices // pairs, narrow, 0)
 
 
 def owner_step(v, field):
@@ -244,16 +293,18 @@
     return pl.pallas_call(
         owner_kernel,
         out_shape=(
-            jax.ShapeDtypeStruct(v.shape, BF16),
+            jax.ShapeDtypeStruct((slots // PAIR * CAP, LANES), BF16),
             jax.ShapeDtypeStruct((tiles, LANES), F32),
         ),
-        in_specs=[VMEM] * 2,
+        in_specs=[VMEM, pl.BlockSpec(memory_space=pl.ANY)],
         out_specs=(VMEM,) * 2,
         scratch_shapes=[
             pltpu.VMEM((slots, LANES), F32),
             pltpu.VMEM((-(-slots // LANES // 8) * 8, LANES), jnp.int32),
             pltpu.VMEM((tiles, 2 * LANES), F32),
             pltpu.VMEM((tiles, 2 * LANES), BF16),
+            pltpu.VMEM((tiles, LANES), F32),
+            pltpu.SemaphoreType.DMA,
         ],
         compiler_params=params(28),
         cost_estimate=cost(16, 7 << 20),
@@ -266,9 +317,11 @@
     widen(ret_ref, rf)
 
     def move(i, c):
-        base = i * ROWS
+        base = pl.multiple_of(i * ROWS, ROWS)
+        here = slot_ref.at[pl.ds(base, ROWS)]
+        rows_out = of.at[pl.ds(base, ROWS)]
         for j in range(ROWS):
-            of[pl.ds(base + j, 1), :] = rf[pl.ds(slot_ref[base + j], 1), :]
+            rows_out[j : j + 1, :] = rf[pl.ds(here[j], 1), :]
         return c
 
     lax.fori_loop(0, rows // ROWS, move, 0)
@@ -466,8 +519,8 @@
     devices = n_orb * n_row
     axes = ("orb", "row")
 
-    def exchange(x):
-        pairs = x.reshape(devices, -1, 2, LANES)
+    def exchange(x, *block):
+        pairs = x.reshape(devices, *block, LANES)
         got = lax.all_to_all(pairs, axes, split_axis=0, concat_axis=0, tiled=True)
         return got.reshape(-1, LANES)
 
@@ -478,17 +531,17 @@
     dest = receiving_devices.reshape(seg_dev // LANES, LANES)
     tile = fragment_grid_tile.reshape(seg_dev // LANES, LANES)
     me = (lax.axis_index("orb") * n_row + lax.axis_index("row")).reshape(1)
-    slot, high, low = ranks(me, dest, tile, devices)
-    slot = slot.reshape(seg_dev)
+    slot, back, high, low = ranks(me, dest, tile, devices)
+    slot, back = slot.reshape(seg_dev), back.reshape(seg_dev)
     outgoing = pack(slot, orbital_fragments, high, low)
     outgoing, one, three = lax.optimization_barrier((outgoing, one, three))
-    arrived = exchange(outgoing)
+    arrived = exchange(outgoing, PAIR // 2, 2)
     bufs = spread_hamiltonian(energy_operator_tiles, one, three, n_row)
     main = main_product(row_at, col_at, density_matrix_tiles, bufs)
 
     arrived, main = lax.optimization_barrier((arrived, main))
     results, charge = owner_step(arrived, outside_field_grid)
-    applied, shift = unpack(slot, exchange(results), orbital_fragments, n_row)
+    applied, shift = unpack(back, exchange(results, CAP), orbital_fragments, n_row)
     shift = lax.all_to_all(shift, "row", split_axis=0, concat_axis=0, tiled=True)
     product = final(shift_at, main, density_matrix_tiles, shift.reshape(n_row * 8, LANES))
     return (applied, charge, product)

time: 243 us -> 236 us (0.971)
  Pallas kernels: 58.8 us -> 51.6 us
  waiting for transfers between devices: 52.8 us -> 57.4 us
  blocking collectives: 94.1 us -> 91.3 us
    pallas_call x1, Pallas kernels: 12.9 us -> 4.26 us  [ranks(): pl.pallas_call(functools.partial(rank_kernel, devices), out_shape=(jax.Sh...]
    ppermute x1, waiting for transfers between devices: 0.01 us -> 3.13 us  [gather_hamiltonian(): one = lax.ppermute(tiles, 'row', ahead)]
    all_to_all x1, blocking collectives: 84.6 us -> 81.8 us  [exchange(): got = lax.all_to_all(pairs, axes, split_axis=0, concat_axis=0, tiled=True)]
  transfers between devices with their start and end apart: 10 -> 10, of which waited for: 4 -> 6; matrix products, arithmetic and copies ran while one was open for 2% -> 2% of each run, Pallas kernels for 14% -> 10%
where the time goes in v3:
time: 236 us; the launch traced here: 235 us
  blocking collectives  91.3 us (39%)
  waiting for transfers between devices  57.4 us (24%)
  Pallas kernels  51.6 us (22%)
  starting transfers between devices  23.1 us (10%)
  local copies, waits for them, and re-layouts  10.6 us (4%)
    all_to_all x1, blocking collectives, exchange(): got = lax.all_to_all(pairs, axes, split_axis=0, concat_axis=0, tiled=True)  81.8 us
    all_to_all x1, waiting for transfers between devices, exchange(): got = lax.all_to_all(pairs, axes, split_axis=0, concat_axis=0, tiled=True)  36.2 us
    pallas_call x1, Pallas kernels, owner_step(): pl.pallas_call(owner_kernel, out_shape=(jax.ShapeDtypeStruct((slots // PA...  16.7 us
    ppermute x1, waiting for transfers between devices, spread_hamiltonian(): two_end = lax.ppermute(three[1:], 'row', behind)  16 us
    all_to_all x1, starting transfers between devices, exchange(): got = lax.all_to_all(pairs, axes, split_axis=0, concat_axis=0, tiled=True)  13.5 us
    pallas_call x1, Pallas kernels, main_product(): pl.pallas_call(main_kernel, out_shape=jax.ShapeDtypeStruct((rows, BLK, nn...  10.8 us
    all_to_all x1, blocking collectives, body(): lax.all_to_all(shift, 'row', split_axis=0, concat_axis=0, tiled=True)  9.5 us
    pallas_call x1, Pallas kernels, pack(): pl.pallas_call(pack_kernel, out_shape=jax.ShapeDtypeStruct((slots, LANES)...  9.32 us
  transfers between devices with their start and end apart: 10, of which 6 were waited for; matrix products, arithmetic and copies ran while one was open for 2% of the time, Pallas kernels for 10%

profile of v3, /device:TPU:1, one launch (start us, length us, event | category | flops | bytes accessed | tf_op | source)
XLA Modules:
  0.0 235.3 jit_solution(1367153091729001211)
XLA Ops:
  0.6 3.4 %collective-permute-start.1 = (bf16[2,12,128,128]{3,2,1,0:T(8,128)(2,1)}, bf16[2,12,128,128]{3,2,1,0:T(8,128)(2,1)}, u32[]{:S(2)}, u32[]{:S(2)}) collective-permute-start(bf16[2,12,128,128]{3,2,1,0:T(8,128)(2,1)} %refs_0_.1), channel_id=1, source_target_pairs={{0,6},{1,7},{2,0},{3,1},{4,2},{5,3},{6,4},{7,5},{8,14},{9,15},{10,... | collective-permute-start | bytes 2359304 | tf_op jit(solution)/shard_map/ppermute | solution.py:469
  4.0 0.0 collective-permute-start
  4.0 0.7 copy-done.6
  4.7 0.7 copy-done.7
  5.5 4.3 %rank.1 = (s32[48,128]{1,0:T(8,128)S(1)}, s32[48,128]{1,0:T(8,128)S(1)}, f32[256,128]{1,0:T(8,128)S(1)}, f32[256,128]{1,0:T(8,128)S(1)}) custom-call(s32[1]{0:T(128)} %bitcast.me_ref, s32[48,128]{1,0:T(8,128)S(1)} %bitcast.16, s32[48,128]{1,0:T(8,128)S(1)} %bitcast.17), custom_call_target="tpu_custom_call" | custom-call | flops 4000000000 | bytes 262144 | tf_op jit(solution)/shard_map/rank/pallas_call | solution.py:119
  9.8 9.3 %pack.1 = bf16[12800,128]{1,0:T(8,128)(2,1)} custom-call(s32[6144]{0:T(1024)S(1)} %bitcast.19, bf16[6144,128]{1,0:T(8,128)(2,1)S(1)} %copy-done, f32[256,128]{1,0:T(8,128)S(1)} %get-tuple-element.18.high_ref, f32[256,128]{1,0:T(8,128)S(1)} %get-tuple-element.19.low_ref), custom_call_target="tpu_custom_call" | custom-call | flops 10000000000 | bytes 5242880 | tf_op jit(solution)/shard_map/pack/pallas_call | solution.py:187
  19.1 1.5 collective-permute-done.1.refs_2_
  20.5 3.1 %collective-permute-done.refs_1_ = bf16[2,12,128,128]{3,2,1,0:T(8,128)(2,1)} collective-permute-done((bf16[2,12,128,128]{3,2,1,0:T(8,128)(2,1)}, bf16[2,12,128,128]{3,2,1,0:T(8,128)(2,1)}, u32[]{:S(2)}, u32[]{:S(2)}) %collective-permute-start) | collective-permute-done | bytes 786464 | tf_op jit(solution)/shard_map/ppermute | solution.py:468
  23.7 13.5 %all-to-all-start = ((bf16[256,25,2,128]{3,2,1,0:T(2,128)(2,1)}), bf16[256,25,2,128]{3,2,1,0:T(2,128)(2,1)S(1)}, u32[]{:S(2)}, u32[]{:S(2)}) async-start(bf16[256,25,2,128]{3,2,1,0:T(2,128)(2,1)} %bitcast.5), calls=%async_computation | async-start | bytes 6553600 | tf_op jit(solution)/shard_map/all_to_all | solution.py:524
  37.2 2.2 collective-permute-start.4
  39.5 0.1 add_multiply_fusion
  39.5 1.8 slice.6
  41.3 0.0 collective-permute-start.5
  41.3 1.8 slice.7
  43.1 0.5 collective-permute-start.6
  43.6 0.8 collective-permute-start.3
  44.4 0.7 collective-permute-start.2
  45.0 0.1 iota_add_fusion
  45.1 0.1 add.97
  45.2 16.0 %collective-permute-done.3.refs_4_ = bf16[1,12,128,128]{3,2,1,0:T(8,128)(2,1)} collective-permute-done((bf16[1,12,128,128]{3,2,1,0:T(8,128)(2,1)}, bf16[1,12,128,128]{3,2,1,0:T(8,128)(2,1)}, u32[]{:S(2)}, u32[]{:S(2)}) %collective-permute-start.3) | collective-permute-done | bytes 393248 | tf_op jit(solution)/shard_map/ppermute | solution.py:479
  61.2 0.9 collective-permute-start.8
  62.2 0.3 collective-permute-done.2.refs_3_
  62.4 1.1 collective-permute-start.7
  63.5 0.1 add.96
  63.6 0.6 gather_fusion
  64.2 0.1 copy.13
  64.3 0.1 copy.11
  64.4 0.1 copy.12
  64.5 0.2 fusion
  64.7 0.1 copy.14
  64.7 0.1 reshape.109.col_at
  64.8 0.1 fusion.1.row_at
  64.9 0.0 collective-permute-done.4.refs_5_
  64.9 0.0 collective-permute-done.8.refs_9_
  65.0 0.2 collective-permute-done.7.refs_8_
  65.2 0.0 collective-permute-done.5.refs_6_
  65.2 1.1 copy-done.2
  66.4 1.1 copy-done.3
  67.5 10.8 %hamiltonian.1.main_ref = f32[2,128,1536]{2,1,0:T(8,128)S(1)} custom-call(s32[2,16]{1,0:T(2,128)S(1)} %fusion.1.row_at, s32[2,192]{1,0:T(2,128)S(1)} %reshape.109.col_at, bf16[2,12,128,128]{3,2,1,0:T(8,128)(2,1)S(1)} %copy-done.3, bf16[2,12,128,128]{3,2,1,0:T(8,128)(2,1)S(1)} %copy-done.2, bf16[2,12,128,128]{3,2,1,0:T(8,128)(2,1)} %collective-permute-done.refs_1_, ...), custom_call_target="tpu_custom_call" | custom-call | flops 10000000000 | bytes 10485760 | tf_op jit(solution)/shard_map/hamiltonian/pallas_call | solution.py:423
  78.3 1.2 copy-done.8
  79.5 36.2 %all-to-all-done = bf16[256,25,2,128]{3,2,1,0:T(2,128)(2,1)S(1)} async-done(((bf16[256,25,2,128]{3,2,1,0:T(2,128)(2,1)}), bf16[256,25,2,128]{3,2,1,0:T(2,128)(2,1)S(1)}, u32[]{:S(2)}, u32[]{:S(2)}) %all-to-all-start) | async-done | bytes 3276832 | tf_op jit(solution)/shard_map/all_to_all | solution.py:524
  115.7 1.0 copy-done.5
  116.7 16.7 %owner.1 = (bf16[12288,128]{1,0:T(8,128)(2,1)S(1)}, f32[768,128]{1,0:T(8,128)}) custom-call(bf16[12800,128]{1,0:T(8,128)(2,1)S(1)} %bitcast.12, f32[768,128]{1,0:T(8,128)S(1)} %copy-done.5), custom_call_target="tpu_custom_call" | custom-call | flops 16000000000 | bytes 7340032 | tf_op jit(solution)/shard_map/owner/pallas_call | solution.py:293
  133.4 0.0 copy-start.1
  133.4 81.8 %all_to_all.15 = bf16[256,48,128]{2,1,0:T(8,128)(2,1)S(1)} all-to-all(bf16[256,48,128]{2,1,0:T(8,128)(2,1)S(1)} %bitcast.14), channel_id=1, replica_groups=mesh['orb'=32,'row'=8] {'orb','row'}, dimensions={0} | all-to-all | bytes 6291456 | tf_op jit(solution)/shard_map/all_to_all | solution.py:524
  215.3 8.9 %unpack.1 = (bf16[6144,128]{1,0:T(8,128)(2,1)}, f32[8,8,128]{2,1,0:T(8,128)S(1)}) custom-call(s32[6144]{0:T(1024)S(1)} %bitcast.18, bf16[12288,128]{1,0:T(8,128)(2,1)S(1)} %bitcast.13, bf16[6144,128]{1,0:T(8,128)(2,1)S(1)} %copy-done.1), custom_call_target="tpu_custom_call" | custom-call | flops 10000000000 | bytes 7340032 | tf_op jit(solution)/shard_map/unpack/pallas_call | solution.py:360
  224.1 9.5 %all_to_all.16 = f32[8,8,128]{2,1,0:T(8,128)S(1)} all-to-all(f32[8,8,128]{2,1,0:T(8,128)S(1)} %get-tuple-element.28), channel_id=1, replica_groups=mesh['orb'=32,'row'=8] {'row'}, dimensions={0} | all-to-all | bytes 65536 | tf_op jit(solution)/shard_map/all_to_all | solution.py:545
  233.7 1.6 final.1
  (23 shorter events, 0.1 us)
Async XLA Ops:
  0.6 19.9 %collective-permute-start.1 = (bf16[2,12,128,128]{3,2,1,0:T(8,128)(2,1)}, bf16[2,12,128,128]{3,2,1,0:T(8,128)(2,1)}, u32[]{:S(2)}, u32[]{:S(2)}) collective-permute-start(bf16[2,12,128,128]{3,2,1,0:T(8,128)(2,1)} %refs_0_.1), channel_id=1, source_target_pairs={{0,6},{1,7},{2,0},{3,1},{4,2},{5,3},{6,4},{7,5},{8,14},{9,15},{10,... | collective-permute-start | bytes 2359304 | tf_op jit(solution)/shard_map/ppermute | solution.py:469
  4.0 19.7 %collective-permute-start = (bf16[2,12,128,128]{3,2,1,0:T(8,128)(2,1)}, bf16[2,12,128,128]{3,2,1,0:T(8,128)(2,1)}, u32[]{:S(2)}, u32[]{:S(2)}) collective-permute-start(bf16[2,12,128,128]{3,2,1,0:T(8,128)(2,1)} %refs_0_.1), channel_id=1, source_target_pairs={{0,2},{1,3},{2,4},{3,5},{4,6},{5,7},{6,0},{7,1},{8,10},{9,11},{10,... | collective-permute-start | bytes 2359304 | tf_op jit(solution)/shard_map/ppermute | solution.py:468
  4.0 0.7 copy-start.6
  4.7 0.7 copy-start.7
  5.5 4.3 %copy-start = (bf16[6144,128]{1,0:T(8,128)(2,1)S(1)}, bf16[6144,128]{1,0:T(8,128)(2,1)}, u32[]{:S(2)}) copy-start(bf16[6144,128]{1,0:T(8,128)(2,1)} %x_ref.3) | copy-start | bytes 4718596
  23.7 15.8 %copy-start.11 = (s32[4]{0:T(128)S(1)}, s32[4]{0:T(128)}, u32[]{:S(2)}) copy-start(s32[4]{0:T(128)} %constant.95) | copy-start | bytes 52
  23.7 39.9 %copy-start.10 = (s32[16,12]{1,0:T(8,128)S(1)}, s32[16,12]{1,0:T(8,128)}, u32[]{:S(2)}) copy-start(s32[16,12]{1,0:T(8,128)} %param.14) | copy-start | bytes 2308
  23.7 92.1 %all-to-all-start = ((bf16[256,25,2,128]{3,2,1,0:T(2,128)(2,1)}), bf16[256,25,2,128]{3,2,1,0:T(2,128)(2,1)S(1)}, u32[]{:S(2)}, u32[]{:S(2)}) async-start(bf16[256,25,2,128]{3,2,1,0:T(2,128)(2,1)} %bitcast.5), calls=%async_computation | async-start | bytes 6553600 | tf_op jit(solution)/shard_map/all_to_all | solution.py:524
  37.2 27.7 %collective-permute-start.4 = (bf16[2,12,128,128]{3,2,1,0:T(8,128)(2,1)}, bf16[2,12,128,128]{3,2,1,0:T(8,128)(2,1)}, u32[]{:S(2)}, u32[]{:S(2)}) collective-permute-start(bf16[2,12,128,128]{3,2,1,0:T(8,128)(2,1)} %refs_0_.1), channel_id=1, source_target_pairs={{0,1},{1,0},{2,3},{3,2},{4,5},{5,4},{6,7},{7,6},{8,9},{9,8},{10,11... | collective-permute-start | bytes 2359304 | tf_op jit(solution)/shard_map/ppermute | solution.py:481
  41.3 23.9 %collective-permute-start.5 = (bf16[2,12,128,128]{3,2,1,0:T(8,128)(2,1)}, bf16[2,12,128,128]{3,2,1,0:T(8,128)(2,1)}, u32[]{:S(2)}, u32[]{:S(2)}) collective-permute-start(bf16[2,12,128,128]{3,2,1,0:T(8,128)(2,1)} %collective-permute-done.refs_1_), channel_id=1, source_target_pairs={{0,1},{1,0},{2,3},{3,2},{4,5},{5,4},{6,7},{7,6},{8,9},{9,8},{10,11... | collective-permute-start | bytes 2359304 | tf_op jit(solution)/shard_map/ppermute | solution.py:481
  43.1 22.1 %collective-permute-start.6 = (bf16[2,12,128,128]{3,2,1,0:T(8,128)(2,1)}, bf16[2,12,128,128]{3,2,1,0:T(8,128)(2,1)}, u32[]{:S(2)}, u32[]{:S(2)}) collective-permute-start(bf16[2,12,128,128]{3,2,1,0:T(8,128)(2,1)} %collective-permute-done.1.refs_2_), channel_id=1, source_target_pairs={{0,1},{1,0},{2,3},{3,2},{4,5},{5,4},{6,7},{7,6},{8,9},{9,8},{10,11... | collective-permute-start | bytes 2359304 | tf_op jit(solution)/shard_map/ppermute | solution.py:481
  43.6 17.7 %collective-permute-start.3 = (bf16[1,12,128,128]{3,2,1,0:T(8,128)(2,1)}, bf16[1,12,128,128]{3,2,1,0:T(8,128)(2,1)}, u32[]{:S(2)}, u32[]{:S(2)}) collective-permute-start(bf16[1,12,128,128]{3,2,1,0:T(8,128)(2,1)} %slice.7), channel_id=1, source_target_pairs={{0,6},{1,7},{2,0},{3,1},{4,2},{5,3},{6,4},{7,5},{8,14},{9,15},{10,... | collective-permute-start | bytes 1179656 | tf_op jit(solution)/shard_map/ppermute | solution.py:479
  44.4 18.0 %collective-permute-start.2 = (bf16[1,12,128,128]{3,2,1,0:T(8,128)(2,1)}, bf16[1,12,128,128]{3,2,1,0:T(8,128)(2,1)}, u32[]{:S(2)}, u32[]{:S(2)}) collective-permute-start(bf16[1,12,128,128]{3,2,1,0:T(8,128)(2,1)} %slice.6), channel_id=1, source_target_pairs={{0,2},{1,3},{2,4},{3,5},{4,6},{5,7},{6,0},{7,1},{8,10},{9,11},{10,... | collective-permute-start | bytes 1179656 | tf_op jit(solution)/shard_map/ppermute | solution.py:478
  61.2 3.7 %collective-permute-start.8 = (bf16[1,12,128,128]{3,2,1,0:T(8,128)(2,1)}, bf16[1,12,128,128]{3,2,1,0:T(8,128)(2,1)}, u32[]{:S(2)}, u32[]{:S(2)}) collective-permute-start(bf16[1,12,128,128]{3,2,1,0:T(8,128)(2,1)} %collective-permute-done.3.refs_4_), channel_id=1, source_target_pairs={{0,1},{1,0},{2,3},{3,2},{4,5},{5,4},{6,7},{7,6},{8,9},{9,8},{10,11... | collective-permute-start | bytes 1179656 | tf_op jit(solution)/shard_map/ppermute | solution.py:481
  62.4 2.8 %collective-permute-start.7 = (bf16[1,12,128,128]{3,2,1,0:T(8,128)(2,1)}, bf16[1,12,128,128]{3,2,1,0:T(8,128)(2,1)}, u32[]{:S(2)}, u32[]{:S(2)}) collective-permute-start(bf16[1,12,128,128]{3,2,1,0:T(8,128)(2,1)} %collective-permute-done.2.refs_3_), channel_id=1, source_target_pairs={{0,1},{1,0},{2,3},{3,2},{4,5},{5,4},{6,7},{7,6},{8,9},{9,8},{10,11... | collective-permute-start | bytes 1179656 | tf_op jit(solution)/shard_map/ppermute | solution.py:481
  65.2 1.1 copy-start.2
  66.3 1.1 copy-start.3
  78.3 1.2 copy-start.8
  115.7 1.0 copy-start.5
  133.4 81.9 %copy-start.1 = (bf16[6144,128]{1,0:T(8,128)(2,1)S(1)}, bf16[6144,128]{1,0:T(8,128)(2,1)}, u32[]{:S(2)}) copy-start(bf16[6144,128]{1,0:T(8,128)(2,1)} %x_ref.3) | copy-start | bytes 4718596
  215.3 18.4 %copy-start.4 = (bf16[2,12,128,128]{3,2,1,0:T(8,128)(2,1)S(1)}, bf16[2,12,128,128]{3,2,1,0:T(8,128)(2,1)}, u32[]{:S(2)}) copy-start(bf16[2,12,128,128]{3,2,1,0:T(8,128)(2,1)} %d_ref.3) | copy-start | bytes 2359300
  215.3 18.4 %copy-start.9 = (f32[2,128,1536]{2,1,0:T(8,128)S(1)}, f32[2,128,1536]{2,1,0:T(8,128)}, u32[]{:S(2)}) copy-start(f32[2,128,1536]{2,1,0:T(8,128)} %copy-done.8) | copy-start | bytes 4718596

commit v4 on v3

--- a/solution.py
+++ b/solution.py
@@ -19,7 +19,7 @@
 
 
 def params(mib):
-    return pltpu.CompilerParams(vmem_limit_bytes=mib << 20)
+    return pltpu.CompilerParams(vmem_limit_bytes=int(mib * 1024) << 10)
 
 
 def cost(us, nbytes):
@@ -40,16 +40,104 @@
     return jnp.transpose(jnp.broadcast_to(row, (LANES, LANES)))
 
 
-def rank_kernel(devices, me_ref, dest_ref, tile_ref, slot_ref, back_ref, high_ref, low_ref, run, rank, acc):
+ROWS = 64
+ANY = pl.BlockSpec(memory_space=pltpu.HBM)
+
+
+def widen(src_ref, dst):
+    def step(i, c):
+        at = pl.ds(pl.multiple_of(i * 256, 256), 256)
+        dst[at, :] = src_ref[at, :].astype(F32)
+        return c
+
+    lax.fori_loop(0, src_ref.shape[0] // 256, step, 0)
+
+
+STRIP = 8
+
+
+def index_copies(slot_ref, regions, sems, strip):
+    return [
+        pltpu.make_async_copy(
+            slot_ref.at[pl.ds(pl.multiple_of((strip + r) * STRIP, STRIP), STRIP)],
+            region,
+            sems.at[r],
+        )
+        for r, region in enumerate(regions)
+    ]
+
+
+def load_index(slot_ref, regions, sems, strip):
+    for copy in index_copies(slot_ref, regions, sems, strip):
+        copy.start()
+
+
+def by_strips(slot_ref, regions, sems, work):
+    strips = slot_ref.shape[0] // STRIP
+    count = len(regions)
+
+    def step(q, c):
+        copies = index_copies(slot_ref, regions, sems, q * count)
+        later = index_copies(slot_ref, regions, sems, (q + 1) * count)
+        for r, region in enumerate(regions):
+            copies[r].wait()
+            first = pl.multiple_of((q * count + r) * STRIP * LANES, STRIP * LANES)
+            work(first, lambda i: region[i // LANES, i % LANES])
+
+            @pl.when((q + 1) * count < strips)
+            def _():
+                later[r].start()
+
+        return c
+
+    lax.fori_loop(0, strips // count, step, 0)
+
+
+def send_kernel(
+    devices,
+    me_ref,
+    dest_hbm,
+    tile_hbm,
+    x_hbm,
+    out_hbm,
+    back_ref,
+    dest_ref,
+    tile_ref,
+    x_ref,
+    run,
+    rank,
+    acc,
+    slot_ref,
+    smem0,
+    smem1,
+    xf,
+    of,
+    out_ref,
+    sems,
+    out_sems,
+):
+    loads = [
+        pltpu.make_async_copy(src, dst, sems.at[i])
+        for i, (src, dst) in enumerate(
+            [(dest_hbm, dest_ref), (tile_hbm, tile_ref), (x_hbm, x_ref)]
+        )
+    ]
+    for load in loads:
+        load.start()
     blocks = dest_ref.shape[0]
+    slots = of.shape[0]
     group = 12
+    steps = blocks // group
     owner = iota((devices, LANES), 0)
     lane = iota((16, LANES), 1)
     src, dst = iota((LANES, LANES), 0), iota((LANES, LANES), 1)
     ahead = src < dst
     run[...] = jnp.zeros_like(run)
+    loads[0].wait()
 
     def count(q, c):
+        part = slots // steps
+        of[pl.ds(pl.multiple_of(q * part, 128), part), :] = jnp.zeros((part, LANES), F32)
         hots, later = [], []
         for j in range(group):
             b = q * group + j
@@ -68,13 +156,17 @@
         )
         return c
 
-    lax.fori_loop(0, blocks // group, count, 0)
-    totals = jnp.concatenate(
+    lax.fori_loop(0, steps, count, 0)
+    acc[:LANES, :] = jnp.concatenate(
         [jnp.transpose(run[i : i + LANES, :]) for i in range(0, devices, LANES)], axis=1
     )
-    acc[:LANES, :] = totals
+    loads[1].wait()
+    loads[2].wait()
 
     def order(q, c):
+        part = group * LANES
+        rows = pl.ds(pl.multiple_of(q * part, part), part)
+        xf[rows, :] = x_ref[rows, :].astype(F32)
         for j in range(group):
             b = q * group + j
             d = dest_ref[pl.ds(b, 1), :]
@@ -86,14 +178,18 @@
             back_ref[pl.ds(b, 1), :] = d * CAP + mine
         return c
 
-    lax.fori_loop(0, blocks // group, order, 0)
+    lax.fori_loop(0, steps, order, 0)
+    regions = (smem0, smem1)
+    index_sems = sems.at[pl.ds(3, 2)]
+    load_index(slot_ref, regions, index_sems, 0)
     turn = me_ref[0] * PAIR
     acc[...] = jnp.zeros_like(acc)
-
-    def mark(q, c):
+    few = 4
+
+    def mark(first):
         hots, spreads = [], []
-        for j in range(group):
-            b = q * group + j
+        for j in range(few):
+            b = first + j
             hots.append(hot_rows(owner, dest_ref[pl.ds(b, 1), :]))
             place = rank[pl.ds(b, 1), :].astype(jnp.int32) + turn
             at = src == (place & (LANES - 1))
@@ -107,95 +203,76 @@
             (((1,), (1,)), ((), ())),
             preferred_element_type=F32,
         )
-        return c
-
-    lax.fori_loop(0, blocks // group, mark, 0)
-    high_ref[...] = acc[:, :LANES]
-    low_ref[...] = acc[:, LANES:]
-
-
-def ranks(me, dest, tile, devices):
+
+    def move(first, place):
+        here = xf.at[pl.ds(first, STRIP * LANES)]
+        block = first // LANES
+        for q in range(STRIP // few):
+            mark(block + q * few)
+            for i in range(q * few * LANES, (q + 1) * few * LANES):
+                of[pl.ds(place(i), 1), :] = here[i : i + 1, :]
+
+    by_strips(slot_ref, regions, index_sems, move)
+    of[pl.ds(CAP, devices, stride=PAIR), :] = acc[:, :LANES]
+    of[pl.ds(CAP + 1, devices, stride=PAIR), :] = acc[:, LANES:]
+    for copy in put_out(lambda at: of[at, :], out_ref, out_hbm, out_sems, 320):
+        copy.wait()
+
+
+def put_out(get, out_ref, out_hbm, sems, size):
+    pieces = sems.shape[0]
+    part = out_ref.shape[0] // pieces
+    copies = []
+    for p in range(pieces):
+
+        def narrow(i, c):
+            at = pl.ds(pl.multiple_of(p * part + i * size, size), size)
+            out_ref[at, :] = get(at).astype(BF16)
+            return c
+
+        lax.fori_loop(0, part // size, narrow, 0)
+        at = pl.ds(p * part, part)
+        copies.append(
+            pltpu.make_async_copy(out_ref.at[at], out_hbm.at[at], sems.at[p])
+        )
+        copies[-1].start()
+    return copies
+
+
+def send_side(me, dest, tile, x, devices):
     blocks = dest.shape[0]
+    slots = devices * PAIR
     return pl.pallas_call(
-        functools.partial(rank_kernel, devices),
+        functools.partial(send_kernel, devices),
         out_shape=(
+            jax.ShapeDtypeStruct((slots, LANES), BF16),
             jax.ShapeDtypeStruct((blocks, LANES), jnp.int32),
-            jax.ShapeDtypeStruct((blocks, LANES), jnp.int32),
-            jax.ShapeDtypeStruct((devices, LANES), F32),
-            jax.ShapeDtypeStruct((devices, LANES), F32),
         ),
-        in_specs=[SMEM, VMEM, VMEM],
-        out_specs=(VMEM,) * 4,
+        in_specs=[SMEM, ANY, ANY, ANY],
+        out_specs=(ANY, VMEM),
         scratch_shapes=[
+            pltpu.VMEM((blocks, LANES), jnp.int32),
+            pltpu.VMEM((blocks, LANES), jnp.int32),
+            pltpu.VMEM(x.shape, BF16),
             pltpu.VMEM((devices, LANES), F32),
             pltpu.VMEM((blocks, LANES), F32),
             pltpu.VMEM((devices, 2 * LANES), F32),
+            pltpu.VMEM((blocks, LANES), jnp.int32),
+            pltpu.SMEM((STRIP, LANES), jnp.int32),
+            pltpu.SMEM((STRIP, LANES), jnp.int32),
+            pltpu.VMEM(x.shape, F32),
+            pltpu.VMEM((slots, LANES), F32),
+            pltpu.VMEM((slots, LANES), BF16),
+            pltpu.SemaphoreType.DMA((5,)),
+            pltpu.SemaphoreType.DMA((5,)),
         ],
-        compiler_params=params(5),
-        cost_estimate=cost(4, 1 << 18),
-        name="rank",
-    )(me, dest, tile)
-
-
-ROWS = 64
-
-
-def widen(src_ref, dst):
-    def step(i, c):
-        at = pl.ds(pl.multiple_of(i * 256, 256), 256)
-        dst[at, :] = src_ref[at, :].astype(F32)
-        return c
-
-    lax.fori_loop(0, src_ref.shape[0] // 256, step, 0)
-
-
-def pack_kernel(slot_ref, x_ref, high_ref, low_ref, out_ref, xf, of):
-    rows = x_ref.shape[0]
-    slots = of.shape[0]
-    devices = high_ref.shape[0]
-    widen(x_ref, xf)
-
-    def clear(i, c):
-        of[pl.ds(pl.multiple_of(i * 512, 512), 512), :] = jnp.zeros((512, LANES), F32)
-        return c
-
-    lax.fori_loop(0, slots // 512, clear, 0)
-
-    def move(i, c):
-        base = pl.multiple_of(i * ROWS, ROWS)
-        here = slot_ref.at[pl.ds(base, ROWS)]
-        rows_in = xf.at[pl.ds(base, ROWS)]
-        for j in range(ROWS):
-            of[pl.ds(here[j], 1), :] = rows_in[j : j + 1, :]
-        return c
-
-    lax.fori_loop(0, rows // ROWS, move, 0)
-    of[pl.ds(CAP, devices, stride=PAIR), :] = high_ref[...]
-    of[pl.ds(CAP + 1, devices, stride=PAIR), :] = low_ref[...]
-
-    def narrow(i, c):
-        at = pl.ds(pl.multiple_of(i * 256, 256), 256)
-        out_ref[at, :] = of[at, :].astype(BF16)
-        return c
-
-    lax.fori_loop(0, slots // 256, narrow, 0)
-
-
-def pack(slot, x, high, low):
-    rows = x.shape[0]
-    slots = high.shape[0] * PAIR
-    return pl.pallas_call(
-        pack_kernel,
-        out_shape=jax.ShapeDtypeStruct((slots, LANES), BF16),
-        in_specs=[SMEM, VMEM, VMEM, VMEM],
-        out_specs=VMEM,
-        scratch_shapes=[pltpu.VMEM((rows, LANES), F32), pltpu.VMEM((slots, LANES), F32)],
-        compiler_params=params(18),
-        cost_estimate=cost(10, 5 << 20),
-        name="pack",
-    )(slot, x, high, low)
-
-
+        compiler_params=params(61),
+        cost_estimate=cost(12, 5 << 20),
+        name="send",
+    )(me, dest, tile, x)
+
+
+OWNER = 28
 DEPTH = 1280
 CHUNK = 1280
 
@@ -221,18 +298,31 @@
     return (both[:, :LANES] * 4.0 + both[:, LANES:]).astype(jnp.int32) - 1
 
 
-def owner_kernel(v_ref, field_hbm, out_ref, charge_ref, vf, label, acc, pot, field_ref, sem):
+def owner_kernel(
+    v_ref,
+    field_hbm,
+    out_hbm,
+    charge_ref,
+    vf,
+    label,
+    acc,
+    pot,
+    field_ref,
+    out_ref,
+    sem,
+    out_sems,
+):
     slots = v_ref.shape[0]
     tiles = charge_ref.shape[0]
     devices = slots // PAIR
     fetch = pltpu.make_async_copy(field_hbm, field_ref, sem)
     fetch.start()
+    acc[...] = jnp.zeros_like(acc)
     widen(v_ref, vf)
     label[...] = slot_labels(
         vf[pl.ds(CAP, devices, stride=PAIR), :],
         vf[pl.ds(CAP + 1, devices, stride=PAIR), :],
     )
-    acc[...] = jnp.zeros_like(acc)
     cell = iota((tiles, LANES), 0)
 
     def add(k, c):
@@ -276,15 +366,15 @@
     lax.fori_loop(0, slots // CHUNK, apply, 0)
     pairs = 8
 
-    def narrow(i, c):
-        source = vf.at[pl.ds(pl.multiple_of(i * pairs * PAIR, 8), pairs * PAIR)]
-        at = pl.ds(pl.multiple_of(i * pairs * CAP, pairs * CAP), pairs * CAP)
-        out_ref[at, :] = jnp.concatenate(
+    def without_labels(at):
+        first = pl.multiple_of(at.start // CAP * PAIR, 8)
+        source = vf.at[pl.ds(first, pairs * PAIR)]
+        return jnp.concatenate(
             [source[j * PAIR : j * PAIR + CAP, :] for j in range(pairs)], axis=0
-        ).astype(BF16)
-        return c
-
-    lax.fori_loop(0, devices // pairs, narrow, 0)
+        )
+
+    for copy in put_out(without_labels, out_ref, out_hbm, out_sems, pairs * CAP):
+        copy.wait()
 
 
 def owner_step(v, field):
@@ -296,46 +386,61 @@
             jax.ShapeDtypeStruct((slots // PAIR * CAP, LANES), BF16),
             jax.ShapeDtypeStruct((tiles, LANES), F32),
         ),
-        in_specs=[VMEM, pl.BlockSpec(memory_space=pl.ANY)],
-        out_specs=(VMEM,) * 2,
+        in_specs=[VMEM, ANY],
+        out_specs=(ANY, VMEM),
         scratch_shapes=[
             pltpu.VMEM((slots, LANES), F32),
             pltpu.VMEM((-(-slots // LANES // 8) * 8, LANES), jnp.int32),
             pltpu.VMEM((tiles, 2 * LANES), F32),
             pltpu.VMEM((tiles, 2 * LANES), BF16),
             pltpu.VMEM((tiles, LANES), F32),
+            pltpu.VMEM((slots // PAIR * CAP, LANES), BF16),
             pltpu.SemaphoreType.DMA,
+            pltpu.SemaphoreType.DMA((4,)),
         ],
-        compiler_params=params(28),
+        compiler_params=params(OWNER),
         cost_estimate=cost(16, 7 << 20),
         name="owner",
     )(v, field)
 
 
-def unpack_kernel(n_row, slot_ref, ret_ref, x_ref, out_ref, shift_ref, rf, of, part):
+def unpack_kernel(
+    n_row,
+    slot_ref,
+    ret_ref,
+    x_ref,
+    out_hbm,
+    shift_ref,
+    rf,
+    of,
+    part,
+    out_ref,
+    smem0,
+    smem1,
+    sems,
+    out_sems,
+):
     rows = x_ref.shape[0]
+    regions = (smem0, smem1)
+    load_index(slot_ref, regions, sems, 0)
     widen(ret_ref, rf)
 
-    def move(i, c):
-        base = pl.multiple_of(i * ROWS, ROWS)
-        here = slot_ref.at[pl.ds(base, ROWS)]
-        rows_out = of.at[pl.ds(base, ROWS)]
-        for j in range(ROWS):
-            rows_out[j : j + 1, :] = rf[pl.ds(here[j], 1), :]
-        return c
-
-    lax.fori_loop(0, rows // ROWS, move, 0)
+    def take(first, place):
+        rows_out = of.at[pl.ds(first, STRIP * LANES)]
+        for i in range(STRIP * LANES):
+            rows_out[i : i + 1, :] = rf[pl.ds(place(i), 1), :]
+
+    by_strips(slot_ref, regions, sems, take)
     count = 8
 
-    def narrow(i, c):
-        at = pl.ds(pl.multiple_of(i * count * SEGF, count * SEGF), count * SEGF)
+    def with_shift(at):
         got = of[at, :]
-        out_ref[at, :] = got.astype(BF16)
         work = (got * x_ref[at, :].astype(F32)).reshape(count, SEGF, LANES)
-        part[pl.ds(pl.multiple_of(i * count, count), count), :] = jnp.sum(work, axis=1)
-        return c
-
-    lax.fori_loop(0, rows // (count * SEGF), narrow, 0)
+        first = pl.multiple_of(at.start // SEGF, count)
+        part[pl.ds(first, count), :] = jnp.sum(work, axis=1)
+        return got
+
+    copies = put_out(with_shift, out_ref, out_hbm, out_sems, count * SEGF)
     functions = rows // SEGF
     total = lax.dot_general(
         jnp.ones((8, LANES), F32),
@@ -353,6 +458,8 @@
     one = one.astype(BF16).astype(F32)
     for r in range(n_row):
         shift_ref[r] = one
+    for copy in copies:
+        copy.wait()
 
 
 def unpack(slot, ret, x, n_row):
@@ -363,12 +470,17 @@
             jax.ShapeDtypeStruct((rows, LANES), BF16),
             jax.ShapeDtypeStruct((n_row, 8, LANES), F32),
         ),
-        in_specs=[SMEM, VMEM, VMEM],
-        out_specs=(VMEM,) * 2,
+        in_specs=[VMEM, VMEM, VMEM],
+        out_specs=(ANY, VMEM),
         scratch_shapes=[
             pltpu.VMEM(ret.shape, F32),
             pltpu.VMEM((rows, LANES), F32),
             pltpu.VMEM((rows // SEGF, LANES), F32),
+            pltpu.VMEM((rows, LANES), BF16),
+            pltpu.SMEM((STRIP, LANES), jnp.int32),
+            pltpu.SMEM((STRIP, LANES), jnp.int32),
+            pltpu.SemaphoreType.DMA((2,)),
+            pltpu.SemaphoreType.DMA((4,)),
         ],
         compiler_params=params(20),
         cost_estimate=cost(10, 7 << 20),
@@ -526,16 +638,16 @@
 
     own_rows = density_matrix_tiles.shape[0]
     row_at, col_at, shift_at = positions(tile_column_numbers, own_rows, n_row)
-    one, three = gather_hamiltonian(energy_operator_tiles, n_row)
 
     dest = receiving_devices.reshape(seg_dev // LANES, LANES)
     tile = fragment_grid_tile.reshape(seg_dev // LANES, LANES)
     me = (lax.axis_index("orb") * n_row + lax.axis_index("row")).reshape(1)
-    slot, back, high, low = ranks(me, dest, tile, devices)
-    slot, back = slot.reshape(seg_dev), back.reshape(seg_dev)
-    outgoing = pack(slot, orbital_fragments, high, low)
-    outgoing, one, three = lax.optimization_barrier((outgoing, one, three))
+    outgoing, back = send_side(me, dest, tile, orbital_fragments, devices)
+    outgoing, energy_operator_tiles = lax.optimization_barrier(
+        (outgoing, energy_operator_tiles)
+    )
     arrived = exchange(outgoing, PAIR // 2, 2)
+    one, three = gather_hamiltonian(energy_operator_tiles, n_row)
     bufs = spread_hamiltonian(energy_operator_tiles, one, three, n_row)
     main = main_product(row_at, col_at, density_matrix_tiles, bufs)
 

time: 236 us -> 229 us (0.970)
  waiting for transfers between devices: 57.4 us -> 48.6 us
  blocking collectives: 91.3 us -> 96.9 us
  Pallas kernels: 51.6 us -> 46.2 us
  starting transfers between devices: 23.1 us -> 26.1 us
    all_to_all x1, waiting for transfers between devices: 36.2 us -> 0.47 us  [exchange(): got = lax.all_to_all(pairs, axes, split_axis=0, concat_axis=0, tiled=True)]
    ppermute x1, waiting for transfers between devices: 1.46 us -> 32 us  [gather_hamiltonian(): three = lax.ppermute(tiles, 'row', behind)]
    all_to_all x1, blocking collectives: 81.8 us -> 87.4 us  [exchange(): got = lax.all_to_all(pairs, axes, split_axis=0, concat_axis=0, tiled=True)]
    ppermute x1, waiting for transfers between devices: 16 us -> 11.9 us  [spread_hamiltonian(): two_end = lax.ppermute(three[1:], 'row', behind)]
    ppermute x1, waiting for transfers between devices: 0.26 us -> 3.97 us  [spread_hamiltonian(): two_top = lax.ppermute(one[:1], 'row', ahead)]
    pallas_call x1, Pallas kernels: 8.89 us -> 5.58 us  [unpack(): pl.pallas_call(functools.partial(unpack_kernel, n_row), out_shape=(jax.Sh...]
    ppermute x1, waiting for transfers between devices: 3.13 us -> 0.01 us  [gather_hamiltonian(): one = lax.ppermute(tiles, 'row', ahead)]
    pallas_call x2 -> x1, Pallas kernels: 13.6 us -> 10.9 us  [send_side(): pl.pallas_call(functools.partial(send_kernel, devices), out_shape=(jax.Sh...]
  transfers between devices with their start and end apart: 10 -> 10, of which waited for: 6 -> 5; matrix products, arithmetic and copies ran while one was open for 2% -> 2% of each run, Pallas kernels for 10% -> 5%
where the time goes in v4:
time: 229 us; the launch traced here: 228 us
  blocking collectives  96.9 us (42%)
  waiting for transfers between devices  48.6 us (21%)
  Pallas kernels  46.2 us (20%)
  starting transfers between devices  26.1 us (11%)
  local copies, waits for them, and re-layouts  9.17 us (4%)
    all_to_all x1, blocking collectives, exchange(): got = lax.all_to_all(pairs, axes, split_axis=0, concat_axis=0, tiled=True)  87.4 us
    ppermute x1, waiting for transfers between devices, gather_hamiltonian(): three = lax.ppermute(tiles, 'row', behind)  32 us
    pallas_call x1, Pallas kernels, owner_step(): pl.pallas_call(owner_kernel, out_shape=(jax.ShapeDtypeStruct((slots // PA...  17.3 us
    all_to_all x1, starting transfers between devices, exchange(): got = lax.all_to_all(pairs, axes, split_axis=0, concat_axis=0, tiled=True)  15.7 us
    ppermute x1, waiting for transfers between devices, spread_hamiltonian(): two_end = lax.ppermute(three[1:], 'row', behind)  11.9 us
    pallas_call x1, Pallas kernels, send_side(): pl.pallas_call(functools.partial(send_kernel, devices), out_shape=(jax.Sh...  10.9 us
    pallas_call x1, Pallas kernels, main_product(): pl.pallas_call(main_kernel, out_shape=jax.ShapeDtypeStruct((rows, BLK, nn...  10.8 us
    all_to_all x1, blocking collectives, body(): lax.all_to_all(shift, 'row', split_axis=0, concat_axis=0, tiled=True)  9.51 us
  transfers between devices with their start and end apart: 10, of which 5 were waited for; matrix products, arithmetic and copies ran while one was open for 2% of the time, Pallas kernels for 5%

profile of v4, /device:TPU:1, one launch (start us, length us, event | category | flops | bytes accessed | tf_op | source)
XLA Modules:
  0.0 228.2 jit_solution(10527709293447925087)
XLA Ops:
  0.6 10.9 %send.1 = (bf16[12800,128]{1,0:T(8,128)(2,1)}, s32[48,128]{1,0:T(8,128)}) custom-call(s32[1]{0:T(128)} %bitcast.me_ref, s32[48,128]{1,0:T(8,128)} %bitcast.15, s32[48,128]{1,0:T(8,128)} %bitcast.16, bf16[6144,128]{1,0:T(8,128)(2,1)} %x_ref.1), custom_call_target="tpu_custom_call" | custom-call | flops 12000000000 | bytes 5242880 | tf_op jit(solution)/shard_map/send/pallas_call | solution.py:245
  11.5 0.0 copy-start.9
  11.5 0.0 copy-start.8
  11.5 15.7 %all-to-all-start = ((bf16[256,25,2,128]{3,2,1,0:T(2,128)(2,1)}), bf16[256,25,2,128]{3,2,1,0:T(2,128)(2,1)S(1)}, u32[]{:S(2)}, u32[]{:S(2)}) async-start(bf16[256,25,2,128]{3,2,1,0:T(2,128)(2,1)} %bitcast.14), calls=%async_computation | async-start | bytes 6553600 | tf_op jit(solution)/shard_map/all_to_all | solution.py:636
  27.2 2.6 %collective-permute-start.1 = (bf16[2,12,128,128]{3,2,1,0:T(8,128)(2,1)}, bf16[2,12,128,128]{3,2,1,0:T(8,128)(2,1)}, u32[]{:S(2)}, u32[]{:S(2)}) collective-permute-start(bf16[2,12,128,128]{3,2,1,0:T(8,128)(2,1)} %refs_0_), channel_id=1, source_target_pairs={{0,6},{1,7},{2,0},{3,1},{4,2},{5,3},{6,4},{7,5},{8,14},{9,15},{10,... | collective-permute-start | bytes 2359304 | tf_op jit(solution)/shard_map/ppermute | solution.py:581
  29.9 0.0 collective-permute-start
  29.9 1.6 collective-permute-start.4
  31.5 0.1 add_multiply_fusion
  31.6 32.0 %collective-permute-done.1.refs_2_ = bf16[2,12,128,128]{3,2,1,0:T(8,128)(2,1)} collective-permute-done((bf16[2,12,128,128]{3,2,1,0:T(8,128)(2,1)}, bf16[2,12,128,128]{3,2,1,0:T(8,128)(2,1)}, u32[]{:S(2)}, u32[]{:S(2)}) %collective-permute-start.1) | collective-permute-done | bytes 786464 | tf_op jit(solution)/shard_map/ppermute | solution.py:581
  63.5 1.8 slice.11
  65.3 2.5 %collective-permute-start.3 = (bf16[1,12,128,128]{3,2,1,0:T(8,128)(2,1)}, bf16[1,12,128,128]{3,2,1,0:T(8,128)(2,1)}, u32[]{:S(2)}, u32[]{:S(2)}) collective-permute-start(bf16[1,12,128,128]{3,2,1,0:T(8,128)(2,1)} %slice.11), channel_id=1, source_target_pairs={{0,6},{1,7},{2,0},{3,1},{4,2},{5,3},{6,4},{7,5},{8,14},{9,15},{10,... | collective-permute-start | bytes 1179656 | tf_op jit(solution)/shard_map/ppermute | solution.py:591
  67.7 0.0 collective-permute-done.refs_1_
  67.7 1.8 slice.10
  69.5 0.0 collective-permute-start.2
  69.5 0.9 collective-permute-start.6
  70.4 0.0 collective-permute-start.5
  70.4 0.1 iota_add_fusion
  70.5 0.1 add.97
  70.6 11.9 %collective-permute-done.3.refs_4_ = bf16[1,12,128,128]{3,2,1,0:T(8,128)(2,1)} collective-permute-done((bf16[1,12,128,128]{3,2,1,0:T(8,128)(2,1)}, bf16[1,12,128,128]{3,2,1,0:T(8,128)(2,1)}, u32[]{:S(2)}, u32[]{:S(2)}) %collective-permute-start.3) | collective-permute-done | bytes 393248 | tf_op jit(solution)/shard_map/ppermute | solution.py:591
  82.5 1.4 collective-permute-start.8
  83.9 4.0 %collective-permute-done.2.refs_3_ = bf16[1,12,128,128]{3,2,1,0:T(8,128)(2,1)} collective-permute-done((bf16[1,12,128,128]{3,2,1,0:T(8,128)(2,1)}, bf16[1,12,128,128]{3,2,1,0:T(8,128)(2,1)}, u32[]{:S(2)}, u32[]{:S(2)}) %collective-permute-start.2) | collective-permute-done | bytes 393248 | tf_op jit(solution)/shard_map/ppermute | solution.py:590
  87.9 1.4 collective-permute-start.7
  89.3 0.1 add.96
  89.4 0.6 gather_fusion
  90.0 0.1 copy.13
  90.1 0.1 copy.11
  90.2 0.1 copy.12
  90.2 0.2 fusion
  90.4 0.1 copy.14
  90.5 0.1 reshape.101.col_at
  90.6 0.1 fusion.1.row_at
  90.7 0.0 collective-permute-done.4.refs_5_
  90.7 0.0 collective-permute-done.8.refs_9_
  90.7 0.0 collective-permute-done.6.refs_7_
  90.8 0.2 collective-permute-done.7.refs_8_
  91.0 1.1 copy-done.1
  92.1 1.1 copy-done.2
  93.3 10.8 %hamiltonian.1.main_ref = f32[2,128,1536]{2,1,0:T(8,128)S(1)} custom-call(s32[2,16]{1,0:T(2,128)S(1)} %fusion.1.row_at, s32[2,192]{1,0:T(2,128)S(1)} %reshape.101.col_at, bf16[2,12,128,128]{3,2,1,0:T(8,128)(2,1)S(1)} %copy-done.2, bf16[2,12,128,128]{3,2,1,0:T(8,128)(2,1)S(1)} %copy-done.1, bf16[2,12,128,128]{3,2,1,0:T(8,128)(2,1)} %collective-permute-done.refs_1_, ...), custom_call_target="tpu_custom_call" | custom-call | flops 10000000000 | bytes 10485760 | tf_op jit(solution)/shard_map/hamiltonian/pallas_call | solution.py:535
  104.1 1.2 copy-done.5
  105.3 0.5 all-to-all-done
  105.8 1.0 copy-done.4
  106.7 17.3 %owner.1 = (bf16[12288,128]{1,0:T(8,128)(2,1)S(1)}, f32[768,128]{1,0:T(8,128)}) custom-call(bf16[12800,128]{1,0:T(8,128)(2,1)S(1)} %bitcast.10, f32[768,128]{1,0:T(8,128)S(1)} %copy-done.4), custom_call_target="tpu_custom_call" | custom-call | flops 16000000000 | bytes 7340032 | tf_op jit(solution)/shard_map/owner/pallas_call | solution.py:383
  124.1 0.0 copy-start
  124.1 0.0 copy-start.7
  124.1 87.4 %all_to_all.15 = bf16[256,48,128]{2,1,0:T(8,128)(2,1)S(1)} all-to-all(bf16[256,48,128]{2,1,0:T(8,128)(2,1)S(1)} %bitcast.12), channel_id=1, replica_groups=mesh['orb'=32,'row'=8] {'orb','row'}, dimensions={0} | all-to-all | bytes 6291456 | tf_op jit(solution)/shard_map/all_to_all | solution.py:636
  211.5 5.6 %unpack.1 = (bf16[6144,128]{1,0:T(8,128)(2,1)}, f32[8,8,128]{2,1,0:T(8,128)S(1)}) custom-call(s32[48,128]{1,0:T(8,128)S(1)} %copy-done.7, bf16[12288,128]{1,0:T(8,128)(2,1)S(1)} %bitcast.11, bf16[6144,128]{1,0:T(8,128)(2,1)S(1)} %copy-done), custom_call_target="tpu_custom_call" | custom-call | flops 10000000000 | bytes 7340032 | tf_op jit(solution)/shard_map/unpack/pallas_call | solution.py:467
  217.1 9.5 %all_to_all.16 = f32[8,8,128]{2,1,0:T(8,128)S(1)} all-to-all(f32[8,8,128]{2,1,0:T(8,128)S(1)} %get-tuple-element.22), channel_id=1, replica_groups=mesh['orb'=32,'row'=8] {'row'}, dimensions={0} | all-to-all | bytes 65536 | tf_op jit(solution)/shard_map/all_to_all | solution.py:657
  226.6 1.6 final.1
  (18 shorter events, 0.1 us)
Async XLA Ops:
  11.5 19.9 %copy-start.9 = (s32[4]{0:T(128)S(1)}, s32[4]{0:T(128)}, u32[]{:S(2)}) copy-start(s32[4]{0:T(128)} %constant.95) | copy-start | bytes 52
  11.5 77.9 %copy-start.8 = (s32[16,12]{1,0:T(8,128)S(1)}, s32[16,12]{1,0:T(8,128)}, u32[]{:S(2)}) copy-start(s32[16,12]{1,0:T(8,128)} %param.14) | copy-start | bytes 2308
  11.5 94.2 %all-to-all-start = ((bf16[256,25,2,128]{3,2,1,0:T(2,128)(2,1)}), bf16[256,25,2,128]{3,2,1,0:T(2,128)(2,1)S(1)}, u32[]{:S(2)}, u32[]{:S(2)}) async-start(bf16[256,25,2,128]{3,2,1,0:T(2,128)(2,1)} %bitcast.14), calls=%async_computation | async-start | bytes 6553600 | tf_op jit(solution)/shard_map/all_to_all | solution.py:636
  27.2 36.3 %collective-permute-start.1 = (bf16[2,12,128,128]{3,2,1,0:T(8,128)(2,1)}, bf16[2,12,128,128]{3,2,1,0:T(8,128)(2,1)}, u32[]{:S(2)}, u32[]{:S(2)}) collective-permute-start(bf16[2,12,128,128]{3,2,1,0:T(8,128)(2,1)} %refs_0_), channel_id=1, source_target_pairs={{0,6},{1,7},{2,0},{3,1},{4,2},{5,3},{6,4},{7,5},{8,14},{9,15},{10,... | collective-permute-start | bytes 2359304 | tf_op jit(solution)/shard_map/ppermute | solution.py:581
  29.9 37.9 %collective-permute-start = (bf16[2,12,128,128]{3,2,1,0:T(8,128)(2,1)}, bf16[2,12,128,128]{3,2,1,0:T(8,128)(2,1)}, u32[]{:S(2)}, u32[]{:S(2)}) collective-permute-start(bf16[2,12,128,128]{3,2,1,0:T(8,128)(2,1)} %refs_0_), channel_id=1, source_target_pairs={{0,2},{1,3},{2,4},{3,5},{4,6},{5,7},{6,0},{7,1},{8,10},{9,11},{10,... | collective-permute-start | bytes 2359304 | tf_op jit(solution)/shard_map/ppermute | solution.py:580
  29.9 60.9 %collective-permute-start.4 = (bf16[2,12,128,128]{3,2,1,0:T(8,128)(2,1)}, bf16[2,12,128,128]{3,2,1,0:T(8,128)(2,1)}, u32[]{:S(2)}, u32[]{:S(2)}) collective-permute-start(bf16[2,12,128,128]{3,2,1,0:T(8,128)(2,1)} %refs_0_), channel_id=1, source_target_pairs={{0,1},{1,0},{2,3},{3,2},{4,5},{5,4},{6,7},{7,6},{8,9},{9,8},{10,11... | collective-permute-start | bytes 2359304 | tf_op jit(solution)/shard_map/ppermute | solution.py:593
  65.3 17.2 %collective-permute-start.3 = (bf16[1,12,128,128]{3,2,1,0:T(8,128)(2,1)}, bf16[1,12,128,128]{3,2,1,0:T(8,128)(2,1)}, u32[]{:S(2)}, u32[]{:S(2)}) collective-permute-start(bf16[1,12,128,128]{3,2,1,0:T(8,128)(2,1)} %slice.11), channel_id=1, source_target_pairs={{0,6},{1,7},{2,0},{3,1},{4,2},{5,3},{6,4},{7,5},{8,14},{9,15},{10,... | collective-permute-start | bytes 1179656 | tf_op jit(solution)/shard_map/ppermute | solution.py:591
  69.5 18.4 %collective-permute-start.2 = (bf16[1,12,128,128]{3,2,1,0:T(8,128)(2,1)}, bf16[1,12,128,128]{3,2,1,0:T(8,128)(2,1)}, u32[]{:S(2)}, u32[]{:S(2)}) collective-permute-start(bf16[1,12,128,128]{3,2,1,0:T(8,128)(2,1)} %slice.10), channel_id=1, source_target_pairs={{0,2},{1,3},{2,4},{3,5},{4,6},{5,7},{6,0},{7,1},{8,10},{9,11},{10,... | collective-permute-start | bytes 1179656 | tf_op jit(solution)/shard_map/ppermute | solution.py:590
  69.5 21.2 %collective-permute-start.6 = (bf16[2,12,128,128]{3,2,1,0:T(8,128)(2,1)}, bf16[2,12,128,128]{3,2,1,0:T(8,128)(2,1)}, u32[]{:S(2)}, u32[]{:S(2)}) collective-permute-start(bf16[2,12,128,128]{3,2,1,0:T(8,128)(2,1)} %collective-permute-done.1.refs_2_), channel_id=1, source_target_pairs={{0,1},{1,0},{2,3},{3,2},{4,5},{5,4},{6,7},{7,6},{8,9},{9,8},{10,11... | collective-permute-start | bytes 2359304 | tf_op jit(solution)/shard_map/ppermute | solution.py:593
  70.4 20.6 %collective-permute-start.5 = (bf16[2,12,128,128]{3,2,1,0:T(8,128)(2,1)}, bf16[2,12,128,128]{3,2,1,0:T(8,128)(2,1)}, u32[]{:S(2)}, u32[]{:S(2)}) collective-permute-start(bf16[2,12,128,128]{3,2,1,0:T(8,128)(2,1)} %collective-permute-done.refs_1_), channel_id=1, source_target_pairs={{0,1},{1,0},{2,3},{3,2},{4,5},{5,4},{6,7},{7,6},{8,9},{9,8},{10,11... | collective-permute-start | bytes 2359304 | tf_op jit(solution)/shard_map/ppermute | solution.py:593
  82.5 8.2 %collective-permute-start.8 = (bf16[1,12,128,128]{3,2,1,0:T(8,128)(2,1)}, bf16[1,12,128,128]{3,2,1,0:T(8,128)(2,1)}, u32[]{:S(2)}, u32[]{:S(2)}) collective-permute-start(bf16[1,12,128,128]{3,2,1,0:T(8,128)(2,1)} %collective-permute-done.3.refs_4_), channel_id=1, source_target_pairs={{0,1},{1,0},{2,3},{3,2},{4,5},{5,4},{6,7},{7,6},{8,9},{9,8},{10,11... | collective-permute-start | bytes 1179656 | tf_op jit(solution)/shard_map/ppermute | solution.py:593
  87.9 3.1 %collective-permute-start.7 = (bf16[1,12,128,128]{3,2,1,0:T(8,128)(2,1)}, bf16[1,12,128,128]{3,2,1,0:T(8,128)(2,1)}, u32[]{:S(2)}, u32[]{:S(2)}) collective-permute-start(bf16[1,12,128,128]{3,2,1,0:T(8,128)(2,1)} %collective-permute-done.2.refs_3_), channel_id=1, source_target_pairs={{0,1},{1,0},{2,3},{3,2},{4,5},{5,4},{6,7},{7,6},{8,9},{9,8},{10,11... | collective-permute-start | bytes 1179656 | tf_op jit(solution)/shard_map/ppermute | solution.py:593
  91.0 1.1 copy-start.1
  92.1 1.1 copy-start.2
  104.1 1.2 copy-start.5
  105.8 1.0 copy-start.4
  124.1 87.4 %copy-start = (bf16[6144,128]{1,0:T(8,128)(2,1)S(1)}, bf16[6144,128]{1,0:T(8,128)(2,1)}, u32[]{:S(2)}) copy-start(bf16[6144,128]{1,0:T(8,128)(2,1)} %x_ref.1) | copy-start | bytes 4718596
  124.1 87.4 %copy-start.7 = (s32[48,128]{1,0:T(8,128)S(1)}, s32[48,128]{1,0:T(8,128)}, u32[]{:S(2)}) copy-start(s32[48,128]{1,0:T(8,128)} %get-tuple-element.13.slot_ref) | copy-start | bytes 73732
  211.5 15.1 %copy-start.3 = (bf16[2,12,128,128]{3,2,1,0:T(8,128)(2,1)S(1)}, bf16[2,12,128,128]{3,2,1,0:T(8,128)(2,1)}, u32[]{:S(2)}) copy-start(bf16[2,12,128,128]{3,2,1,0:T(8,128)(2,1)} %d_ref.3) | copy-start | bytes 2359300
  211.5 15.1 %copy-start.6 = (f32[2,128,1536]{2,1,0:T(8,128)S(1)}, f32[2,128,1536]{2,1,0:T(8,128)}, u32[]{:S(2)}) copy-start(f32[2,128,1536]{2,1,0:T(8,128)} %copy-done.5) | copy-start | bytes 4718596

commit v5 on v4

--- a/solution.py
+++ b/solution.py
@@ -6,6 +6,7 @@
 from jax.experimental import pallas as pl
 from jax.experimental.pallas import tpu as pltpu
 from jax.sharding import PartitionSpec as P
+
 
 BLK = 128
 SEGF = 24
@@ -40,7 +41,6 @@
     return jnp.transpose(jnp.broadcast_to(row, (LANES, LANES)))
 
 
-ROWS = 64
 ANY = pl.BlockSpec(memory_space=pltpu.HBM)
 
 
@@ -301,16 +301,14 @@
 def owner_kernel(
     v_ref,
     field_hbm,
-    out_hbm,
+    out_ref,
     charge_ref,
     vf,
     label,
     acc,
     pot,
     field_ref,
-    out_ref,
     sem,
-    out_sems,
 ):
     slots = v_ref.shape[0]
     tiles = charge_ref.shape[0]
@@ -366,15 +364,15 @@
     lax.fori_loop(0, slots // CHUNK, apply, 0)
     pairs = 8
 
-    def without_labels(at):
-        first = pl.multiple_of(at.start // CAP * PAIR, 8)
-        source = vf.at[pl.ds(first, pairs * PAIR)]
-        return jnp.concatenate(
+    def narrow(i, c):
+        source = vf.at[pl.ds(pl.multiple_of(i * pairs * PAIR, 8), pairs * PAIR)]
+        at = pl.ds(pl.multiple_of(i * pairs * CAP, pairs * CAP), pairs * CAP)
+        out_ref[at, :] = jnp.concatenate(
             [source[j * PAIR : j * PAIR + CAP, :] for j in range(pairs)], axis=0
-        )
-
-    for copy in put_out(without_labels, out_ref, out_hbm, out_sems, pairs * CAP):
-        copy.wait()
+        ).astype(BF16)
+        return c
+
+    lax.fori_loop(0, devices // pairs, narrow, 0)
 
 
 def owner_step(v, field):
@@ -387,16 +385,14 @@
             jax.ShapeDtypeStruct((tiles, LANES), F32),
         ),
         in_specs=[VMEM, ANY],
-        out_specs=(ANY, VMEM),
+        out_specs=(VMEM, VMEM),
         scratch_shapes=[
             pltpu.VMEM((slots, LANES), F32),
             pltpu.VMEM((-(-slots // LANES // 8) * 8, LANES), jnp.int32),
             pltpu.VMEM((tiles, 2 * LANES), F32),
             pltpu.VMEM((tiles, 2 * LANES), BF16),
             pltpu.VMEM((tiles, LANES), F32),
-            pltpu.VMEM((slots // PAIR * CAP, LANES), BF16),
             pltpu.SemaphoreType.DMA,
-            pltpu.SemaphoreType.DMA((4,)),
         ],
         compiler_params=params(OWNER),
         cost_estimate=cost(16, 7 << 20),
@@ -638,16 +634,13 @@
 
     own_rows = density_matrix_tiles.shape[0]
     row_at, col_at, shift_at = positions(tile_column_numbers, own_rows, n_row)
+    one, three = gather_hamiltonian(energy_operator_tiles, n_row)
 
     dest = receiving_devices.reshape(seg_dev // LANES, LANES)
     tile = fragment_grid_tile.reshape(seg_dev // LANES, LANES)
     me = (lax.axis_index("orb") * n_row + lax.axis_index("row")).reshape(1)
     outgoing, back = send_side(me, dest, tile, orbital_fragments, devices)
-    outgoing, energy_operator_tiles = lax.optimization_barrier(
-        (outgoing, energy_operator_tiles)
-    )
     arrived = exchange(outgoing, PAIR // 2, 2)
-    one, three = gather_hamiltonian(energy_operator_tiles, n_row)
     bufs = spread_hamiltonian(energy_operator_tiles, one, three, n_row)
     main = main_product(row_at, col_at, density_matrix_tiles, bufs)
 

time: 229 us -> 228 us (level)
  no operation moved by 1% of the time
where the time goes in v5:
time: 228 us
  blocking collectives  96.9 us (42%)
  waiting for transfers between devices  48.6 us (21%)
  Pallas kernels  45.6 us (20%)
  starting transfers between devices  26.1 us (11%)
  local copies, waits for them, and re-layouts  9.17 us (4%)
    all_to_all x1, blocking collectives, exchange(): got = lax.all_to_all(pairs, axes, split_axis=0, concat_axis=0, tiled=True)  87.4 us
    ppermute x1, waiting for transfers between devices, gather_hamiltonian(): three = lax.ppermute(tiles, 'row', behind)  32 us
    pallas_call x1, Pallas kernels, owner_step(): pl.pallas_call(owner_kernel, out_shape=(jax.ShapeDtypeStruct((slots // PA...  16.7 us
    all_to_all x1, starting transfers between devices, exchange(): got = lax.all_to_all(pairs, axes, split_axis=0, concat_axis=0, tiled=True)  15.7 us
    ppermute x1, waiting for transfers between devices, spread_hamiltonian(): two_end = lax.ppermute(three[1:], 'row', behind)  11.9 us
    pallas_call x1, Pallas kernels, send_side(): pl.pallas_call(functools.partial(send_kernel, devices), out_shape=(jax.Sh...  10.9 us
    pallas_call x1, Pallas kernels, main_product(): pl.pallas_call(main_kernel, out_shape=jax.ShapeDtypeStruct((rows, BLK, nn...  10.8 us
    all_to_all x1, blocking collectives, body(): lax.all_to_all(shift, 'row', split_axis=0, concat_axis=0, tiled=True)  9.51 us
  transfers between devices with their start and end apart: 10, of which 5 were waited for; matrix products, arithmetic and copies ran while one was open for 2% of the time, Pallas kernels for 5%

profile of v5, /device:TPU:1, one launch (start us, length us, event | category | flops | bytes accessed | tf_op | source)
XLA Modules:
  0.0 227.6 jit_solution(4796442053551940577)
XLA Ops:
  0.6 10.9 %send.1 = (bf16[12800,128]{1,0:T(8,128)(2,1)}, s32[48,128]{1,0:T(8,128)}) custom-call(s32[1]{0:T(128)} %bitcast.me_ref, s32[48,128]{1,0:T(8,128)} %bitcast.15, s32[48,128]{1,0:T(8,128)} %bitcast.16, bf16[6144,128]{1,0:T(8,128)(2,1)} %x_ref.1), custom_call_target="tpu_custom_call" | custom-call | flops 12000000000 | bytes 5242880 | tf_op jit(solution)/shard_map/send/pallas_call | solution.py:245
  11.5 0.0 copy-start.9
  11.5 0.0 copy-start.8
  11.5 15.7 %all-to-all-start = ((bf16[256,25,2,128]{3,2,1,0:T(2,128)(2,1)}), bf16[256,25,2,128]{3,2,1,0:T(2,128)(2,1)S(1)}, u32[]{:S(2)}, u32[]{:S(2)}) async-start(bf16[256,25,2,128]{3,2,1,0:T(2,128)(2,1)} %bitcast.14), calls=%async_computation | async-start | bytes 6553600 | tf_op jit(solution)/shard_map/all_to_all | solution.py:632
  27.2 2.6 %collective-permute-start.1 = (bf16[2,12,128,128]{3,2,1,0:T(8,128)(2,1)}, bf16[2,12,128,128]{3,2,1,0:T(8,128)(2,1)}, u32[]{:S(2)}, u32[]{:S(2)}) collective-permute-start(bf16[2,12,128,128]{3,2,1,0:T(8,128)(2,1)} %refs_0_.1), channel_id=1, source_target_pairs={{0,6},{1,7},{2,0},{3,1},{4,2},{5,3},{6,4},{7,5},{8,14},{9,15},{10,... | collective-permute-start | bytes 2359304 | tf_op jit(solution)/shard_map/ppermute | solution.py:577
  29.9 0.0 collective-permute-start
  29.9 1.6 collective-permute-start.4
  31.5 0.1 add_multiply_fusion
  31.6 32.0 %collective-permute-done.1.refs_2_ = bf16[2,12,128,128]{3,2,1,0:T(8,128)(2,1)} collective-permute-done((bf16[2,12,128,128]{3,2,1,0:T(8,128)(2,1)}, bf16[2,12,128,128]{3,2,1,0:T(8,128)(2,1)}, u32[]{:S(2)}, u32[]{:S(2)}) %collective-permute-start.1) | collective-permute-done | bytes 786464 | tf_op jit(solution)/shard_map/ppermute | solution.py:577
  63.5 1.8 slice.11
  65.3 2.5 %collective-permute-start.3 = (bf16[1,12,128,128]{3,2,1,0:T(8,128)(2,1)}, bf16[1,12,128,128]{3,2,1,0:T(8,128)(2,1)}, u32[]{:S(2)}, u32[]{:S(2)}) collective-permute-start(bf16[1,12,128,128]{3,2,1,0:T(8,128)(2,1)} %slice.11), channel_id=1, source_target_pairs={{0,6},{1,7},{2,0},{3,1},{4,2},{5,3},{6,4},{7,5},{8,14},{9,15},{10,... | collective-permute-start | bytes 1179656 | tf_op jit(solution)/shard_map/ppermute | solution.py:587
  67.7 0.0 collective-permute-done.refs_1_
  67.7 1.8 slice.10
  69.5 0.0 collective-permute-start.2
  69.5 0.9 collective-permute-start.6
  70.4 0.0 collective-permute-start.5
  70.4 0.1 iota_add_fusion
  70.5 0.1 add.97
  70.6 11.9 %collective-permute-done.3.refs_4_ = bf16[1,12,128,128]{3,2,1,0:T(8,128)(2,1)} collective-permute-done((bf16[1,12,128,128]{3,2,1,0:T(8,128)(2,1)}, bf16[1,12,128,128]{3,2,1,0:T(8,128)(2,1)}, u32[]{:S(2)}, u32[]{:S(2)}) %collective-permute-start.3) | collective-permute-done | bytes 393248 | tf_op jit(solution)/shard_map/ppermute | solution.py:587
  82.5 1.4 collective-permute-start.8
  83.9 4.0 %collective-permute-done.2.refs_3_ = bf16[1,12,128,128]{3,2,1,0:T(8,128)(2,1)} collective-permute-done((bf16[1,12,128,128]{3,2,1,0:T(8,128)(2,1)}, bf16[1,12,128,128]{3,2,1,0:T(8,128)(2,1)}, u32[]{:S(2)}, u32[]{:S(2)}) %collective-permute-start.2) | collective-permute-done | bytes 393248 | tf_op jit(solution)/shard_map/ppermute | solution.py:586
  87.9 1.4 collective-permute-start.7
  89.3 0.1 add.96
  89.4 0.6 gather_fusion
  90.0 0.1 copy.13
  90.1 0.1 copy.11
  90.2 0.1 copy.12
  90.2 0.2 fusion
  90.4 0.1 copy.14
  90.5 0.1 reshape.101.col_at
  90.6 0.1 fusion.1.row_at
  90.7 0.0 collective-permute-done.8.refs_9_
  90.7 0.0 collective-permute-done.6.refs_7_
  90.8 0.2 collective-permute-done.7.refs_8_
  91.0 0.0 collective-permute-done.5.refs_6_
  91.0 1.1 copy-done.1
  92.1 1.1 copy-done.2
  93.3 10.8 %hamiltonian.1.main_ref = f32[2,128,1536]{2,1,0:T(8,128)S(1)} custom-call(s32[2,16]{1,0:T(2,128)S(1)} %fusion.1.row_at, s32[2,192]{1,0:T(2,128)S(1)} %reshape.101.col_at, bf16[2,12,128,128]{3,2,1,0:T(8,128)(2,1)S(1)} %copy-done.2, bf16[2,12,128,128]{3,2,1,0:T(8,128)(2,1)S(1)} %copy-done.1, bf16[2,12,128,128]{3,2,1,0:T(8,128)(2,1)} %collective-permute-done.refs_1_, ...), custom_call_target="tpu_custom_call" | custom-call | flops 10000000000 | bytes 10485760 | tf_op jit(solution)/shard_map/hamiltonian/pallas_call | solution.py:531
  104.1 1.2 copy-done.5
  105.3 0.5 all-to-all-done
  105.8 1.0 copy-done.4
  106.7 16.7 %owner.1 = (bf16[12288,128]{1,0:T(8,128)(2,1)S(1)}, f32[768,128]{1,0:T(8,128)}) custom-call(bf16[12800,128]{1,0:T(8,128)(2,1)S(1)} %bitcast.10, f32[768,128]{1,0:T(8,128)S(1)} %copy-done.4), custom_call_target="tpu_custom_call" | custom-call | flops 16000000000 | bytes 7340032 | tf_op jit(solution)/shard_map/owner/pallas_call | solution.py:381
  123.5 0.0 copy-start
  123.5 0.0 copy-start.7
  123.5 87.4 %all_to_all.15 = bf16[256,48,128]{2,1,0:T(8,128)(2,1)S(1)} all-to-all(bf16[256,48,128]{2,1,0:T(8,128)(2,1)S(1)} %bitcast.12), channel_id=1, replica_groups=mesh['orb'=32,'row'=8] {'orb','row'}, dimensions={0} | all-to-all | bytes 6291456 | tf_op jit(solution)/shard_map/all_to_all | solution.py:632
  210.9 5.6 %unpack.1 = (bf16[6144,128]{1,0:T(8,128)(2,1)}, f32[8,8,128]{2,1,0:T(8,128)S(1)}) custom-call(s32[48,128]{1,0:T(8,128)S(1)} %copy-done.7, bf16[12288,128]{1,0:T(8,128)(2,1)S(1)} %bitcast.11, bf16[6144,128]{1,0:T(8,128)(2,1)S(1)} %copy-done), custom_call_target="tpu_custom_call" | custom-call | flops 10000000000 | bytes 7340032 | tf_op jit(solution)/shard_map/unpack/pallas_call | solution.py:463
  216.5 9.5 %all_to_all.16 = f32[8,8,128]{2,1,0:T(8,128)S(1)} all-to-all(f32[8,8,128]{2,1,0:T(8,128)S(1)} %get-tuple-element.18), channel_id=1, replica_groups=mesh['orb'=32,'row'=8] {'row'}, dimensions={0} | all-to-all | bytes 65536 | tf_op jit(solution)/shard_map/all_to_all | solution.py:650
  226.0 1.6 final.1
  (18 shorter events, 0.1 us)
Async XLA Ops:
  11.5 19.9 %copy-start.9 = (s32[4]{0:T(128)S(1)}, s32[4]{0:T(128)}, u32[]{:S(2)}) copy-start(s32[4]{0:T(128)} %constant.95) | copy-start | bytes 52
  11.5 77.9 %copy-start.8 = (s32[16,12]{1,0:T(8,128)S(1)}, s32[16,12]{1,0:T(8,128)}, u32[]{:S(2)}) copy-start(s32[16,12]{1,0:T(8,128)} %param.14) | copy-start | bytes 2308
  11.5 94.2 %all-to-all-start = ((bf16[256,25,2,128]{3,2,1,0:T(2,128)(2,1)}), bf16[256,25,2,128]{3,2,1,0:T(2,128)(2,1)S(1)}, u32[]{:S(2)}, u32[]{:S(2)}) async-start(bf16[256,25,2,128]{3,2,1,0:T(2,128)(2,1)} %bitcast.14), calls=%async_computation | async-start | bytes 6553600 | tf_op jit(solution)/shard_map/all_to_all | solution.py:632
  27.2 36.3 %collective-permute-start.1 = (bf16[2,12,128,128]{3,2,1,0:T(8,128)(2,1)}, bf16[2,12,128,128]{3,2,1,0:T(8,128)(2,1)}, u32[]{:S(2)}, u32[]{:S(2)}) collective-permute-start(bf16[2,12,128,128]{3,2,1,0:T(8,128)(2,1)} %refs_0_.1), channel_id=1, source_target_pairs={{0,6},{1,7},{2,0},{3,1},{4,2},{5,3},{6,4},{7,5},{8,14},{9,15},{10,... | collective-permute-start | bytes 2359304 | tf_op jit(solution)/shard_map/ppermute | solution.py:577
  29.9 37.9 %collective-permute-start = (bf16[2,12,128,128]{3,2,1,0:T(8,128)(2,1)}, bf16[2,12,128,128]{3,2,1,0:T(8,128)(2,1)}, u32[]{:S(2)}, u32[]{:S(2)}) collective-permute-start(bf16[2,12,128,128]{3,2,1,0:T(8,128)(2,1)} %refs_0_.1), channel_id=1, source_target_pairs={{0,2},{1,3},{2,4},{3,5},{4,6},{5,7},{6,0},{7,1},{8,10},{9,11},{10,... | collective-permute-start | bytes 2359304 | tf_op jit(solution)/shard_map/ppermute | solution.py:576
  29.9 60.9 %collective-permute-start.4 = (bf16[2,12,128,128]{3,2,1,0:T(8,128)(2,1)}, bf16[2,12,128,128]{3,2,1,0:T(8,128)(2,1)}, u32[]{:S(2)}, u32[]{:S(2)}) collective-permute-start(bf16[2,12,128,128]{3,2,1,0:T(8,128)(2,1)} %refs_0_.1), channel_id=1, source_target_pairs={{0,1},{1,0},{2,3},{3,2},{4,5},{5,4},{6,7},{7,6},{8,9},{9,8},{10,11... | collective-permute-start | bytes 2359304 | tf_op jit(solution)/shard_map/ppermute | solution.py:589
  65.3 17.2 %collective-permute-start.3 = (bf16[1,12,128,128]{3,2,1,0:T(8,128)(2,1)}, bf16[1,12,128,128]{3,2,1,0:T(8,128)(2,1)}, u32[]{:S(2)}, u32[]{:S(2)}) collective-permute-start(bf16[1,12,128,128]{3,2,1,0:T(8,128)(2,1)} %slice.11), channel_id=1, source_target_pairs={{0,6},{1,7},{2,0},{3,1},{4,2},{5,3},{6,4},{7,5},{8,14},{9,15},{10,... | collective-permute-start | bytes 1179656 | tf_op jit(solution)/shard_map/ppermute | solution.py:587
  69.5 18.4 %collective-permute-start.2 = (bf16[1,12,128,128]{3,2,1,0:T(8,128)(2,1)}, bf16[1,12,128,128]{3,2,1,0:T(8,128)(2,1)}, u32[]{:S(2)}, u32[]{:S(2)}) collective-permute-start(bf16[1,12,128,128]{3,2,1,0:T(8,128)(2,1)} %slice.10), channel_id=1, source_target_pairs={{0,2},{1,3},{2,4},{3,5},{4,6},{5,7},{6,0},{7,1},{8,10},{9,11},{10,... | collective-permute-start | bytes 1179656 | tf_op jit(solution)/shard_map/ppermute | solution.py:586
  69.5 21.2 %collective-permute-start.6 = (bf16[2,12,128,128]{3,2,1,0:T(8,128)(2,1)}, bf16[2,12,128,128]{3,2,1,0:T(8,128)(2,1)}, u32[]{:S(2)}, u32[]{:S(2)}) collective-permute-start(bf16[2,12,128,128]{3,2,1,0:T(8,128)(2,1)} %collective-permute-done.1.refs_2_), channel_id=1, source_target_pairs={{0,1},{1,0},{2,3},{3,2},{4,5},{5,4},{6,7},{7,6},{8,9},{9,8},{10,11... | collective-permute-start | bytes 2359304 | tf_op jit(solution)/shard_map/ppermute | solution.py:589
  70.4 20.6 %collective-permute-start.5 = (bf16[2,12,128,128]{3,2,1,0:T(8,128)(2,1)}, bf16[2,12,128,128]{3,2,1,0:T(8,128)(2,1)}, u32[]{:S(2)}, u32[]{:S(2)}) collective-permute-start(bf16[2,12,128,128]{3,2,1,0:T(8,128)(2,1)} %collective-permute-done.refs_1_), channel_id=1, source_target_pairs={{0,1},{1,0},{2,3},{3,2},{4,5},{5,4},{6,7},{7,6},{8,9},{9,8},{10,11... | collective-permute-start | bytes 2359304 | tf_op jit(solution)/shard_map/ppermute | solution.py:589
  82.5 8.2 %collective-permute-start.8 = (bf16[1,12,128,128]{3,2,1,0:T(8,128)(2,1)}, bf16[1,12,128,128]{3,2,1,0:T(8,128)(2,1)}, u32[]{:S(2)}, u32[]{:S(2)}) collective-permute-start(bf16[1,12,128,128]{3,2,1,0:T(8,128)(2,1)} %collective-permute-done.3.refs_4_), channel_id=1, source_target_pairs={{0,1},{1,0},{2,3},{3,2},{4,5},{5,4},{6,7},{7,6},{8,9},{9,8},{10,11... | collective-permute-start | bytes 1179656 | tf_op jit(solution)/shard_map/ppermute | solution.py:589
  87.9 3.1 %collective-permute-start.7 = (bf16[1,12,128,128]{3,2,1,0:T(8,128)(2,1)}, bf16[1,12,128,128]{3,2,1,0:T(8,128)(2,1)}, u32[]{:S(2)}, u32[]{:S(2)}) collective-permute-start(bf16[1,12,128,128]{3,2,1,0:T(8,128)(2,1)} %collective-permute-done.2.refs_3_), channel_id=1, source_target_pairs={{0,1},{1,0},{2,3},{3,2},{4,5},{5,4},{6,7},{7,6},{8,9},{9,8},{10,11... | collective-permute-start | bytes 1179656 | tf_op jit(solution)/shard_map/ppermute | solution.py:589
  91.0 1.1 copy-start.1
  92.1 1.1 copy-start.2
  104.1 1.2 copy-start.5
  105.8 1.0 copy-start.4
  123.5 87.4 %copy-start = (bf16[6144,128]{1,0:T(8,128)(2,1)S(1)}, bf16[6144,128]{1,0:T(8,128)(2,1)}, u32[]{:S(2)}) copy-start(bf16[6144,128]{1,0:T(8,128)(2,1)} %x_ref.1) | copy-start | bytes 4718596
  123.5 87.4 %copy-start.7 = (s32[48,128]{1,0:T(8,128)S(1)}, s32[48,128]{1,0:T(8,128)}, u32[]{:S(2)}) copy-start(s32[48,128]{1,0:T(8,128)} %get-tuple-element.11.slot_ref) | copy-start | bytes 73732
  210.9 15.1 %copy-start.3 = (bf16[2,12,128,128]{3,2,1,0:T(8,128)(2,1)S(1)}, bf16[2,12,128,128]{3,2,1,0:T(8,128)(2,1)}, u32[]{:S(2)}) copy-start(bf16[2,12,128,128]{3,2,1,0:T(8,128)(2,1)} %d_ref.3) | copy-start | bytes 2359300
  210.9 15.1 %copy-start.6 = (f32[2,128,1536]{2,1,0:T(8,128)S(1)}, f32[2,128,1536]{2,1,0:T(8,128)}, u32[]{:S(2)}) copy-start(f32[2,128,1536]{2,1,0:T(8,128)} %copy-done.5) | copy-start | bytes 4718596

commit v6 on v5

--- a/solution.py
+++ b/solution.py
@@ -54,6 +54,7 @@
 
 
 STRIP = 8
+GROUP = 16
 
 
 def index_copies(slot_ref, regions, sems, strip):
@@ -110,6 +111,7 @@
     slot_ref,
     smem0,
     smem1,
+    smem2,
     xf,
     of,
     out_ref,
@@ -126,7 +128,7 @@
         load.start()
     blocks = dest_ref.shape[0]
     slots = of.shape[0]
-    group = 12
+    group = GROUP
     steps = blocks // group
     owner = iota((devices, LANES), 0)
     lane = iota((16, LANES), 1)
@@ -179,8 +181,8 @@
         return c
 
     lax.fori_loop(0, steps, order, 0)
-    regions = (smem0, smem1)
-    index_sems = sems.at[pl.ds(3, 2)]
+    regions = (smem0, smem1, smem2)
+    index_sems = sems.at[pl.ds(3, 3)]
     load_index(slot_ref, regions, index_sems, 0)
     turn = me_ref[0] * PAIR
     acc[...] = jnp.zeros_like(acc)
@@ -260,10 +262,11 @@
             pltpu.VMEM((blocks, LANES), jnp.int32),
             pltpu.SMEM((STRIP, LANES), jnp.int32),
             pltpu.SMEM((STRIP, LANES), jnp.int32),
+            pltpu.SMEM((STRIP, LANES), jnp.int32),
             pltpu.VMEM(x.shape, F32),
             pltpu.VMEM((slots, LANES), F32),
             pltpu.VMEM((slots, LANES), BF16),
-            pltpu.SemaphoreType.DMA((5,)),
+            pltpu.SemaphoreType.DMA((6,)),
             pltpu.SemaphoreType.DMA((5,)),
         ],
         compiler_params=params(61),
@@ -413,11 +416,12 @@
     out_ref,
     smem0,
     smem1,
+    smem2,
     sems,
     out_sems,
 ):
     rows = x_ref.shape[0]
-    regions = (smem0, smem1)
+    regions = (smem0, smem1, smem2)
     load_index(slot_ref, regions, sems, 0)
     widen(ret_ref, rf)
 
@@ -475,7 +479,8 @@
             pltpu.VMEM((rows, LANES), BF16),
             pltpu.SMEM((STRIP, LANES), jnp.int32),
             pltpu.SMEM((STRIP, LANES), jnp.int32),
-            pltpu.SemaphoreType.DMA((2,)),
+            pltpu.SMEM((STRIP, LANES), jnp.int32),
+            pltpu.SemaphoreType.DMA((3,)),
             pltpu.SemaphoreType.DMA((4,)),
         ],
         compiler_params=params(20),

time: 228 us -> 227 us (level)
  no operation moved by 1% of the time
where the time goes in v6:
time: 227 us
  blocking collectives  96.9 us (43%)
  waiting for transfers between devices  48.6 us (21%)
  Pallas kernels  44.9 us (20%)
  starting transfers between devices  26.1 us (11%)
  local copies, waits for them, and re-layouts  9.17 us (4%)
    all_to_all x1, blocking collectives, exchange(): got = lax.all_to_all(pairs, axes, split_axis=0, concat_axis=0, tiled=True)  87.4 us
    ppermute x1, waiting for transfers between devices, gather_hamiltonian(): three = lax.ppermute(tiles, 'row', behind)  32 us
    pallas_call x1, Pallas kernels, owner_step(): pl.pallas_call(owner_kernel, out_shape=(jax.ShapeDtypeStruct((slots // PA...  16.7 us
    all_to_all x1, starting transfers between devices, exchange(): got = lax.all_to_all(pairs, axes, split_axis=0, concat_axis=0, tiled=True)  15.7 us
    ppermute x1, waiting for transfers between devices, spread_hamiltonian(): two_end = lax.ppermute(three[1:], 'row', behind)  11.9 us
    pallas_call x1, Pallas kernels, main_product(): pl.pallas_call(main_kernel, out_shape=jax.ShapeDtypeStruct((rows, BLK, nn...  10.8 us
    pallas_call x1, Pallas kernels, send_side(): pl.pallas_call(functools.partial(send_kernel, devices), out_shape=(jax.Sh...  10.3 us
    all_to_all x1, blocking collectives, body(): lax.all_to_all(shift, 'row', split_axis=0, concat_axis=0, tiled=True)  9.51 us
  transfers between devices with their start and end apart: 10, of which 5 were waited for; matrix products, arithmetic and copies ran while one was open for 2% of the time, Pallas kernels for 5%

profile of v6, /device:TPU:1, one launch (start us, length us, event | category | flops | bytes accessed | tf_op | source)
XLA Modules:
  0.0 227.0 jit_solution(4744722392036838937)
XLA Ops:
  0.6 10.3 %send.1 = (bf16[12800,128]{1,0:T(8,128)(2,1)}, s32[48,128]{1,0:T(8,128)}) custom-call(s32[1]{0:T(128)} %bitcast.me_ref, s32[48,128]{1,0:T(8,128)} %bitcast.15, s32[48,128]{1,0:T(8,128)} %bitcast.16, bf16[6144,128]{1,0:T(8,128)(2,1)} %x_ref.1), custom_call_target="tpu_custom_call" | custom-call | flops 12000000000 | bytes 5242880 | tf_op jit(solution)/shard_map/send/pallas_call | solution.py:247
  10.9 0.0 copy-start.9
  10.9 0.0 copy-start.8
  10.9 15.7 %all-to-all-start = ((bf16[256,25,2,128]{3,2,1,0:T(2,128)(2,1)}), bf16[256,25,2,128]{3,2,1,0:T(2,128)(2,1)S(1)}, u32[]{:S(2)}, u32[]{:S(2)}) async-start(bf16[256,25,2,128]{3,2,1,0:T(2,128)(2,1)} %bitcast.14), calls=%async_computation | async-start | bytes 6553600 | tf_op jit(solution)/shard_map/all_to_all | solution.py:637
  26.6 2.6 %collective-permute-start.1 = (bf16[2,12,128,128]{3,2,1,0:T(8,128)(2,1)}, bf16[2,12,128,128]{3,2,1,0:T(8,128)(2,1)}, u32[]{:S(2)}, u32[]{:S(2)}) collective-permute-start(bf16[2,12,128,128]{3,2,1,0:T(8,128)(2,1)} %refs_0_.1), channel_id=1, source_target_pairs={{0,6},{1,7},{2,0},{3,1},{4,2},{5,3},{6,4},{7,5},{8,14},{9,15},{10,... | collective-permute-start | bytes 2359304 | tf_op jit(solution)/shard_map/ppermute | solution.py:582
  29.2 0.0 collective-permute-start
  29.2 1.6 collective-permute-start.4
  30.9 0.1 add_multiply_fusion
  30.9 32.0 %collective-permute-done.1.refs_2_ = bf16[2,12,128,128]{3,2,1,0:T(8,128)(2,1)} collective-permute-done((bf16[2,12,128,128]{3,2,1,0:T(8,128)(2,1)}, bf16[2,12,128,128]{3,2,1,0:T(8,128)(2,1)}, u32[]{:S(2)}, u32[]{:S(2)}) %collective-permute-start.1) | collective-permute-done | bytes 786464 | tf_op jit(solution)/shard_map/ppermute | solution.py:582
  62.9 1.8 slice.11
  64.7 2.5 %collective-permute-start.3 = (bf16[1,12,128,128]{3,2,1,0:T(8,128)(2,1)}, bf16[1,12,128,128]{3,2,1,0:T(8,128)(2,1)}, u32[]{:S(2)}, u32[]{:S(2)}) collective-permute-start(bf16[1,12,128,128]{3,2,1,0:T(8,128)(2,1)} %slice.11), channel_id=1, source_target_pairs={{0,6},{1,7},{2,0},{3,1},{4,2},{5,3},{6,4},{7,5},{8,14},{9,15},{10,... | collective-permute-start | bytes 1179656 | tf_op jit(solution)/shard_map/ppermute | solution.py:592
  67.1 0.0 collective-permute-done.refs_1_
  67.1 1.8 slice.10
  68.9 0.0 collective-permute-start.2
  68.9 0.9 collective-permute-start.6
  69.8 0.0 collective-permute-start.5
  69.8 0.1 iota_add_fusion
  69.9 0.1 add.97
  70.0 11.9 %collective-permute-done.3.refs_4_ = bf16[1,12,128,128]{3,2,1,0:T(8,128)(2,1)} collective-permute-done((bf16[1,12,128,128]{3,2,1,0:T(8,128)(2,1)}, bf16[1,12,128,128]{3,2,1,0:T(8,128)(2,1)}, u32[]{:S(2)}, u32[]{:S(2)}) %collective-permute-start.3) | collective-permute-done | bytes 393248 | tf_op jit(solution)/shard_map/ppermute | solution.py:592
  81.9 1.4 collective-permute-start.8
  83.3 4.0 %collective-permute-done.2.refs_3_ = bf16[1,12,128,128]{3,2,1,0:T(8,128)(2,1)} collective-permute-done((bf16[1,12,128,128]{3,2,1,0:T(8,128)(2,1)}, bf16[1,12,128,128]{3,2,1,0:T(8,128)(2,1)}, u32[]{:S(2)}, u32[]{:S(2)}) %collective-permute-start.2) | collective-permute-done | bytes 393248 | tf_op jit(solution)/shard_map/ppermute | solution.py:591
  87.3 1.4 collective-permute-start.7
  88.7 0.1 add.96
  88.8 0.6 gather_fusion
  89.3 0.1 copy.13
  89.4 0.1 copy.11
  89.5 0.1 copy.12
  89.6 0.2 fusion
  89.8 0.1 copy.14
  89.9 0.1 reshape.101.col_at
  90.0 0.1 fusion.1.row_at
  90.1 0.0 collective-permute-done.8.refs_9_
  90.1 0.0 collective-permute-done.6.refs_7_
  90.1 0.2 collective-permute-done.7.refs_8_
  90.4 0.0 collective-permute-done.5.refs_6_
  90.4 1.1 copy-done.1
  91.5 1.1 copy-done.2
  92.6 10.8 %hamiltonian.1.main_ref = f32[2,128,1536]{2,1,0:T(8,128)S(1)} custom-call(s32[2,16]{1,0:T(2,128)S(1)} %fusion.1.row_at, s32[2,192]{1,0:T(2,128)S(1)} %reshape.101.col_at, bf16[2,12,128,128]{3,2,1,0:T(8,128)(2,1)S(1)} %copy-done.2, bf16[2,12,128,128]{3,2,1,0:T(8,128)(2,1)S(1)} %copy-done.1, bf16[2,12,128,128]{3,2,1,0:T(8,128)(2,1)} %collective-permute-done.refs_1_, ...), custom_call_target="tpu_custom_call" | custom-call | flops 10000000000 | bytes 10485760 | tf_op jit(solution)/shard_map/hamiltonian/pallas_call | solution.py:536
  103.5 1.2 copy-done.5
  104.7 0.5 all-to-all-done
  105.1 1.0 copy-done.4
  106.1 16.7 %owner.1 = (bf16[12288,128]{1,0:T(8,128)(2,1)S(1)}, f32[768,128]{1,0:T(8,128)}) custom-call(bf16[12800,128]{1,0:T(8,128)(2,1)S(1)} %bitcast.10, f32[768,128]{1,0:T(8,128)S(1)} %copy-done.4), custom_call_target="tpu_custom_call" | custom-call | flops 16000000000 | bytes 7340032 | tf_op jit(solution)/shard_map/owner/pallas_call | solution.py:384
  122.8 0.0 copy-start
  122.9 0.0 copy-start.7
  122.9 87.4 %all_to_all.15 = bf16[256,48,128]{2,1,0:T(8,128)(2,1)S(1)} all-to-all(bf16[256,48,128]{2,1,0:T(8,128)(2,1)S(1)} %bitcast.12), channel_id=1, replica_groups=mesh['orb'=32,'row'=8] {'orb','row'}, dimensions={0} | all-to-all | bytes 6291456 | tf_op jit(solution)/shard_map/all_to_all | solution.py:637
  210.3 5.5 %unpack.1 = (bf16[6144,128]{1,0:T(8,128)(2,1)}, f32[8,8,128]{2,1,0:T(8,128)S(1)}) custom-call(s32[48,128]{1,0:T(8,128)S(1)} %copy-done.7, bf16[12288,128]{1,0:T(8,128)(2,1)S(1)} %bitcast.11, bf16[6144,128]{1,0:T(8,128)(2,1)S(1)} %copy-done), custom_call_target="tpu_custom_call" | custom-call | flops 10000000000 | bytes 7340032 | tf_op jit(solution)/shard_map/unpack/pallas_call | solution.py:467
  215.8 9.5 %all_to_all.16 = f32[8,8,128]{2,1,0:T(8,128)S(1)} all-to-all(f32[8,8,128]{2,1,0:T(8,128)S(1)} %get-tuple-element.18), channel_id=1, replica_groups=mesh['orb'=32,'row'=8] {'row'}, dimensions={0} | all-to-all | bytes 65536 | tf_op jit(solution)/shard_map/all_to_all | solution.py:655
  225.4 1.6 final.1
  (18 shorter events, 0.1 us)
Async XLA Ops:
  10.9 19.9 %copy-start.9 = (s32[4]{0:T(128)S(1)}, s32[4]{0:T(128)}, u32[]{:S(2)}) copy-start(s32[4]{0:T(128)} %constant.95) | copy-start | bytes 52
  10.9 77.9 %copy-start.8 = (s32[16,12]{1,0:T(8,128)S(1)}, s32[16,12]{1,0:T(8,128)}, u32[]{:S(2)}) copy-start(s32[16,12]{1,0:T(8,128)} %param.14) | copy-start | bytes 2308
  10.9 94.2 %all-to-all-start = ((bf16[256,25,2,128]{3,2,1,0:T(2,128)(2,1)}), bf16[256,25,2,128]{3,2,1,0:T(2,128)(2,1)S(1)}, u32[]{:S(2)}, u32[]{:S(2)}) async-start(bf16[256,25,2,128]{3,2,1,0:T(2,128)(2,1)} %bitcast.14), calls=%async_computation | async-start | bytes 6553600 | tf_op jit(solution)/shard_map/all_to_all | solution.py:637
  26.6 36.3 %collective-permute-start.1 = (bf16[2,12,128,128]{3,2,1,0:T(8,128)(2,1)}, bf16[2,12,128,128]{3,2,1,0:T(8,128)(2,1)}, u32[]{:S(2)}, u32[]{:S(2)}) collective-permute-start(bf16[2,12,128,128]{3,2,1,0:T(8,128)(2,1)} %refs_0_.1), channel_id=1, source_target_pairs={{0,6},{1,7},{2,0},{3,1},{4,2},{5,3},{6,4},{7,5},{8,14},{9,15},{10,... | collective-permute-start | bytes 2359304 | tf_op jit(solution)/shard_map/ppermute | solution.py:582
  29.2 37.9 %collective-permute-start = (bf16[2,12,128,128]{3,2,1,0:T(8,128)(2,1)}, bf16[2,12,128,128]{3,2,1,0:T(8,128)(2,1)}, u32[]{:S(2)}, u32[]{:S(2)}) collective-permute-start(bf16[2,12,128,128]{3,2,1,0:T(8,128)(2,1)} %refs_0_.1), channel_id=1, source_target_pairs={{0,2},{1,3},{2,4},{3,5},{4,6},{5,7},{6,0},{7,1},{8,10},{9,11},{10,... | collective-permute-start | bytes 2359304 | tf_op jit(solution)/shard_map/ppermute | solution.py:581
  29.2 60.9 %collective-permute-start.4 = (bf16[2,12,128,128]{3,2,1,0:T(8,128)(2,1)}, bf16[2,12,128,128]{3,2,1,0:T(8,128)(2,1)}, u32[]{:S(2)}, u32[]{:S(2)}) collective-permute-start(bf16[2,12,128,128]{3,2,1,0:T(8,128)(2,1)} %refs_0_.1), channel_id=1, source_target_pairs={{0,1},{1,0},{2,3},{3,2},{4,5},{5,4},{6,7},{7,6},{8,9},{9,8},{10,11... | collective-permute-start | bytes 2359304 | tf_op jit(solution)/shard_map/ppermute | solution.py:594
  64.7 17.2 %collective-permute-start.3 = (bf16[1,12,128,128]{3,2,1,0:T(8,128)(2,1)}, bf16[1,12,128,128]{3,2,1,0:T(8,128)(2,1)}, u32[]{:S(2)}, u32[]{:S(2)}) collective-permute-start(bf16[1,12,128,128]{3,2,1,0:T(8,128)(2,1)} %slice.11), channel_id=1, source_target_pairs={{0,6},{1,7},{2,0},{3,1},{4,2},{5,3},{6,4},{7,5},{8,14},{9,15},{10,... | collective-permute-start | bytes 1179656 | tf_op jit(solution)/shard_map/ppermute | solution.py:592
  68.9 18.4 %collective-permute-start.2 = (bf16[1,12,128,128]{3,2,1,0:T(8,128)(2,1)}, bf16[1,12,128,128]{3,2,1,0:T(8,128)(2,1)}, u32[]{:S(2)}, u32[]{:S(2)}) collective-permute-start(bf16[1,12,128,128]{3,2,1,0:T(8,128)(2,1)} %slice.10), channel_id=1, source_target_pairs={{0,2},{1,3},{2,4},{3,5},{4,6},{5,7},{6,0},{7,1},{8,10},{9,11},{10,... | collective-permute-start | bytes 1179656 | tf_op jit(solution)/shard_map/ppermute | solution.py:591
  68.9 21.2 %collective-permute-start.6 = (bf16[2,12,128,128]{3,2,1,0:T(8,128)(2,1)}, bf16[2,12,128,128]{3,2,1,0:T(8,128)(2,1)}, u32[]{:S(2)}, u32[]{:S(2)}) collective-permute-start(bf16[2,12,128,128]{3,2,1,0:T(8,128)(2,1)} %collective-permute-done.1.refs_2_), channel_id=1, source_target_pairs={{0,1},{1,0},{2,3},{3,2},{4,5},{5,4},{6,7},{7,6},{8,9},{9,8},{10,11... | collective-permute-start | bytes 2359304 | tf_op jit(solution)/shard_map/ppermute | solution.py:594
  69.8 20.6 %collective-permute-start.5 = (bf16[2,12,128,128]{3,2,1,0:T(8,128)(2,1)}, bf16[2,12,128,128]{3,2,1,0:T(8,128)(2,1)}, u32[]{:S(2)}, u32[]{:S(2)}) collective-permute-start(bf16[2,12,128,128]{3,2,1,0:T(8,128)(2,1)} %collective-permute-done.refs_1_), channel_id=1, source_target_pairs={{0,1},{1,0},{2,3},{3,2},{4,5},{5,4},{6,7},{7,6},{8,9},{9,8},{10,11... | collective-permute-start | bytes 2359304 | tf_op jit(solution)/shard_map/ppermute | solution.py:594
  81.9 8.2 %collective-permute-start.8 = (bf16[1,12,128,128]{3,2,1,0:T(8,128)(2,1)}, bf16[1,12,128,128]{3,2,1,0:T(8,128)(2,1)}, u32[]{:S(2)}, u32[]{:S(2)}) collective-permute-start(bf16[1,12,128,128]{3,2,1,0:T(8,128)(2,1)} %collective-permute-done.3.refs_4_), channel_id=1, source_target_pairs={{0,1},{1,0},{2,3},{3,2},{4,5},{5,4},{6,7},{7,6},{8,9},{9,8},{10,11... | collective-permute-start | bytes 1179656 | tf_op jit(solution)/shard_map/ppermute | solution.py:594
  87.3 3.1 %collective-permute-start.7 = (bf16[1,12,128,128]{3,2,1,0:T(8,128)(2,1)}, bf16[1,12,128,128]{3,2,1,0:T(8,128)(2,1)}, u32[]{:S(2)}, u32[]{:S(2)}) collective-permute-start(bf16[1,12,128,128]{3,2,1,0:T(8,128)(2,1)} %collective-permute-done.2.refs_3_), channel_id=1, source_target_pairs={{0,1},{1,0},{2,3},{3,2},{4,5},{5,4},{6,7},{7,6},{8,9},{9,8},{10,11... | collective-permute-start | bytes 1179656 | tf_op jit(solution)/shard_map/ppermute | solution.py:594
  90.4 1.1 copy-start.1
  91.5 1.1 copy-start.2
  103.5 1.2 copy-start.5
  105.1 1.0 copy-start.4
  122.8 87.4 %copy-start = (bf16[6144,128]{1,0:T(8,128)(2,1)S(1)}, bf16[6144,128]{1,0:T(8,128)(2,1)}, u32[]{:S(2)}) copy-start(bf16[6144,128]{1,0:T(8,128)(2,1)} %x_ref.1) | copy-start | bytes 4718596
  122.9 87.4 %copy-start.7 = (s32[48,128]{1,0:T(8,128)S(1)}, s32[48,128]{1,0:T(8,128)}, u32[]{:S(2)}) copy-start(s32[48,128]{1,0:T(8,128)} %get-tuple-element.11.slot_ref) | copy-start | bytes 73732
  210.3 15.1 %copy-start.3 = (bf16[2,12,128,128]{3,2,1,0:T(8,128)(2,1)S(1)}, bf16[2,12,128,128]{3,2,1,0:T(8,128)(2,1)}, u32[]{:S(2)}) copy-start(bf16[2,12,128,128]{3,2,1,0:T(8,128)(2,1)} %d_ref.3) | copy-start | bytes 2359300
  210.3 15.1 %copy-start.6 = (f32[2,128,1536]{2,1,0:T(8,128)S(1)}, f32[2,128,1536]{2,1,0:T(8,128)}, u32[]{:S(2)}) copy-start(f32[2,128,1536]{2,1,0:T(8,128)} %copy-done.5) | copy-start | bytes 4718596
